TPU v7x, 256 devices: a whole 4x4x8 slice. The times are simulated.
256 devices in a mesh: frame: 32 (over x, y, core), head: 8 (over z).
Axes of the slice: x: 4, y: 4, z: 8, core: 2. Of those that a mesh axis runs over, the one named last changes fastest.
Arguments:
- query_rows: bfloat16 [16384, 2048], P(('frame', 'head')), may hold values from -10 to 10
- key_rows: bfloat16 [16384, 2048], P(('frame', 'head')), may hold values from -10 to 10
- value_rows: bfloat16 [16384, 2048], P(('frame', 'head')), may hold values from -48 to 48
- out_grad: bfloat16 [16384, 2048], P(('frame', 'head')), may hold values from -48 to 48
- block_order: int32 [32, 4], replicated, may hold values from 0 to 3, each once within a row
Outputs:
- attended: bfloat16 [16384, 2048], P(('frame', 'head'))
- query_grad: bfloat16 [16384, 2048], P(('frame', 'head'))
- key_grad: bfloat16 [16384, 2048], P(('frame', 'head'))
- value_grad: bfloat16 [16384, 2048], P(('frame', 'head'))
Inputs may be any that keep to these rules, and one draw needn't show every extreme that they name: `block_order`: each row holds every block index of a frame once.
All inputs are finite; a program needn't handle non-finite values.
Results may differ from a plain program's by a relative error of at most 0.028.
Values may be sent and summed in bfloat16 or wider, within the bound.
No kernel may reach another device: no remote copies, remote signals or barrier semaphores. Data moves between devices by JAX's collectives and lax.ppermute only.
A program may use at most 64 MiB of HBM per device.

v0:
```python
import math

import jax
import jax.numpy as jnp
from jax import lax
from jax.sharding import PartitionSpec as P

HD = 128
BLK = 128
BANDS = 2


def passed_along(array, axis, by):
    length = lax.axis_size(axis)
    pairs = [(i, i + by) for i in range(length) if 0 <= i + by < length]
    return lax.ppermute(array, axis, pairs)


def pick_blocks(panel, chosen, block_size):
    stacked = panel.reshape(
        panel.shape[0], panel.shape[1] // block_size, block_size, panel.shape[2]
    )
    taken = jnp.take(stacked, chosen, axis=1)
    return taken.reshape(panel.shape[0], chosen.shape[0] * block_size, panel.shape[2])


def attend_tile(query_tile, grad_tile, key_head, value_head, key_valid, score_scale):
    scores = (
        jnp.einsum("qd,kd->qk", query_tile, key_head, preferred_element_type=jnp.float32)
        * score_scale
    )
    scores = jnp.where(key_valid[None, :], scores, -jnp.inf)
    row_peak = jnp.max(scores, axis=1, keepdims=True)
    row_total = jnp.sum(jnp.exp(scores - row_peak), axis=1, keepdims=True)
    weights = jnp.exp(scores - (row_peak + jnp.log(row_total)))
    weights_low = weights.astype(jnp.bfloat16)
    out_tile = jnp.dot(weights_low, value_head, preferred_element_type=jnp.float32).astype(
        jnp.bfloat16
    )
    row_delta = jnp.sum(
        grad_tile.astype(jnp.float32) * out_tile.astype(jnp.float32), axis=1, keepdims=True
    )
    weight_grad = jnp.einsum("qd,kd->qk", grad_tile, value_head, preferred_element_type=jnp.float32)
    score_grad = (weights * (weight_grad - row_delta)).astype(jnp.bfloat16)
    query_part = jnp.dot(score_grad, key_head, preferred_element_type=jnp.float32) * score_scale
    key_part = (
        jnp.einsum("qk,qd->kd", score_grad, query_tile, preferred_element_type=jnp.float32)
        * score_scale
    )
    value_part = jnp.einsum("qk,qd->kd", weights_low, grad_tile, preferred_element_type=jnp.float32)
    return (out_tile, query_part.astype(jnp.bfloat16), key_part, value_part)


def local(query_rows, key_rows, value_rows, out_grad, block_order):
    query_local, key_local, value_local, grad_local = (
        lax.all_to_all(query_rows, "head", split_axis=1, concat_axis=0, tiled=True),
        lax.all_to_all(key_rows, "head", split_axis=1, concat_axis=0, tiled=True),
        lax.all_to_all(value_rows, "head", split_axis=1, concat_axis=0, tiled=True),
        lax.all_to_all(out_grad, "head", split_axis=1, concat_axis=0, tiled=True),
    )
    frame_count = lax.axis_size("frame")
    frame_pos = lax.axis_index("frame")
    token_count = query_local.shape[0]
    feature_width = query_local.shape[1]
    block_count = token_count // BLK
    pair_local = jnp.stack([key_local, value_local])
    own_order = lax.dynamic_index_in_dim(block_order, frame_pos, 0, keepdims=False)
    pair_parts = [pair_local]
    valid_parts = [jnp.ones((token_count,), dtype=jnp.bool_)]
    for band_index in range(1, BANDS + 1):
        distance = 2 ** (band_index - 1)
        chosen_count = block_count >> band_index
        lower_frame = frame_pos - distance
        upper_frame = frame_pos + distance
        panel_lower = passed_along(pair_local, "frame", distance)
        panel_upper = passed_along(pair_local, "frame", -distance)
        lower_order = lax.dynamic_index_in_dim(
            block_order, jnp.clip(lower_frame, 0, frame_count - 1), 0, keepdims=False
        )
        upper_order = lax.dynamic_index_in_dim(
            block_order, jnp.clip(upper_frame, 0, frame_count - 1), 0, keepdims=False
        )
        from_lower = pick_blocks(panel_lower, lower_order[:chosen_count], BLK)
        from_upper = pick_blocks(panel_upper, upper_order[:chosen_count], BLK)
        pair_parts.append(from_lower)
        pair_parts.append(from_upper)
        valid_parts.append(jnp.broadcast_to(lower_frame >= 0, (chosen_count * BLK,)))
        valid_parts.append(jnp.broadcast_to(upper_frame < frame_count, (chosen_count * BLK,)))
    key_pairs = jnp.concatenate(pair_parts, axis=1)
    key_valid = jnp.concatenate(valid_parts)
    score_scale = 1.0 / math.sqrt(HD)
    tile_rows = min(512, token_count)
    out_columns, query_columns, key_columns, value_columns = ([], [], [], [])
    for head_index in range(feature_width // HD):
        column_start = head_index * HD
        key_head = key_pairs[0, :, column_start : column_start + HD]
        value_head = key_pairs[1, :, column_start : column_start + HD]
        out_tiles, query_tiles = ([], [])
        query_tile = query_local[0:tile_rows, column_start : column_start + HD]
        grad_tile = grad_local[0:tile_rows, column_start : column_start + HD]
        out_tile, query_part, key_part, value_part = attend_tile(
            query_tile, grad_tile, key_head, value_head, key_valid, score_scale
        )
        out_tiles.append(out_tile)
        query_tiles.append(query_part)
        out_columns.append(out_tiles[0])
        query_columns.append(query_tiles[0])
        key_columns.append(key_part)
        value_columns.append(value_part)
    out_all = jnp.concatenate(out_columns, axis=1)
    query_all = jnp.concatenate(query_columns, axis=1)
    grad_pairs = jnp.stack(
        [jnp.concatenate(key_columns, axis=1), jnp.concatenate(value_columns, axis=1)]
    )
    local_grads = grad_pairs[:, :token_count].reshape(2, block_count, BLK, feature_width)
    offset = token_count
    for band_index in range(1, BANDS + 1):
        distance = 2 ** (band_index - 1)
        chosen_count = block_count >> band_index
        segment_rows = chosen_count * BLK
        lower_part = grad_pairs[:, offset : offset + segment_rows].astype(jnp.bfloat16)
        upper_part = grad_pairs[:, offset + segment_rows : offset + 2 * segment_rows].astype(
            jnp.bfloat16
        )
        offset = offset + 2 * segment_rows
        back_above = passed_along(lower_part, "frame", -distance)
        back_below = passed_along(upper_part, "frame", distance)
        returned = (back_above.astype(jnp.float32) + back_below.astype(jnp.float32)).reshape(
            2, chosen_count, BLK, feature_width
        )
        local_grads = local_grads.at[:, own_order[:chosen_count]].add(returned)
    key_grad_local = local_grads[0].reshape(token_count, feature_width).astype(jnp.bfloat16)
    value_grad_local = local_grads[1].reshape(token_count, feature_width).astype(jnp.bfloat16)
    attended, query_grad, key_grad, value_grad = (
        lax.all_to_all(out_all, "head", split_axis=0, concat_axis=1, tiled=True),
        lax.all_to_all(query_all, "head", split_axis=0, concat_axis=1, tiled=True),
        lax.all_to_all(key_grad_local, "head", split_axis=0, concat_axis=1, tiled=True),
        lax.all_to_all(value_grad_local, "head", split_axis=0, concat_axis=1, tiled=True),
    )
    return (attended, query_grad, key_grad, value_grad)


def solution(mesh):
    placed = (
        P(("frame", "head"), None),
        P(("frame", "head"), None),
        P(("frame", "head"), None),
        P(("frame", "head"), None),
        P(),
    )
    return jax.shard_map(
        local,
        mesh=mesh,
        in_specs=placed,
        out_specs=(
            P(("frame", "head"), None),
            P(("frame", "head"), None),
            P(("frame", "head"), None),
            P(("frame", "head"), None),
        ),
        check_vma=False,
    )
```

profile of v0, /device:TPU:4, one launch (start us, length us, event | category | flops | bytes accessed | tf_op | source)
XLA Modules:
  0.0 158.4 jit_solution(7856534883758554899)
XLA Ops:
  0.7 1.7 %copy.85 = bf16[8,8,8,256]{3,2,0,1:T(8,128)(2,1)} copy(bf16[8,8,8,256]{3,2,1,0:T(8,128)(2,1)} %bitcast.143) | data formatting | bytes 524288 | tf_op jit(solution)/shard_map/all_to_all | solution.py:57
  2.4 8.5 %all-to-all-start = ((bf16[64,8,256]{2,0,1:T(8,128)(2,1)}), bf16[64,8,256]{2,0,1:T(8,128)(2,1)S(1)}, u32[]{:S(2)}, u32[]{:S(2)}) async-start(bf16[64,8,256]{2,0,1:T(8,128)(2,1)} %bitcast.123), calls=%async_computation | async-start | bytes 524288 | tf_op jit(solution)/shard_map/all_to_all | solution.py:57
  10.9 0.9 constant_dynamic-slice_fusion.1
  13.9 0.7 copy.84
  15.3 0.8 and_reduce_fusion
  16.0 6.7 %all-to-all-done = bf16[64,8,256]{2,0,1:T(8,128)(2,1)S(1)} async-done(((bf16[64,8,256]{2,0,1:T(8,128)(2,1)}), bf16[64,8,256]{2,0,1:T(8,128)(2,1)S(1)}, u32[]{:S(2)}, u32[]{:S(2)}) %all-to-all-start) | async-done | bytes 262176 | tf_op jit(solution)/shard_map/all_to_all | solution.py:57
  22.7 3.4 %all-to-all-start.1 = ((bf16[64,8,256]{2,0,1:T(8,128)(2,1)}), bf16[64,8,256]{2,0,1:T(8,128)(2,1)S(1)}, u32[]{:S(2)}, u32[]{:S(2)}) async-start(bf16[64,8,256]{2,0,1:T(8,128)(2,1)} %bitcast.122), calls=%async_computation.1 | async-start | bytes 524288 | tf_op jit(solution)/shard_map/all_to_all | solution.py:58
  26.3 0.7 copy.82
  27.0 9.5 %all-to-all-done.1 = bf16[64,8,256]{2,0,1:T(8,128)(2,1)S(1)} async-done(((bf16[64,8,256]{2,0,1:T(8,128)(2,1)}), bf16[64,8,256]{2,0,1:T(8,128)(2,1)S(1)}, u32[]{:S(2)}, u32[]{:S(2)}) %all-to-all-start.1) | async-done | bytes 262176 | tf_op jit(solution)/shard_map/all_to_all | solution.py:58
  36.5 3.4 %all-to-all-start.4 = ((bf16[64,8,256]{2,0,1:T(8,128)(2,1)}), bf16[64,8,256]{2,0,1:T(8,128)(2,1)S(1)}, u32[]{:S(2)}, u32[]{:S(2)}) async-start(bf16[64,8,256]{2,0,1:T(8,128)(2,1)} %bitcast.120), calls=%async_computation.4 | async-start | bytes 524288 | tf_op jit(solution)/shard_map/all_to_all | solution.py:59
  40.0 1.9 %collective-permute-start.1 = (bf16[2,512,256]{2,1,0:T(8,128)(2,1)S(1)}, bf16[2,512,256]{2,1,0:T(8,128)(2,1)}, u32[]{:S(2)}, u32[]{:S(2)}) collective-permute-start(bf16[2,512,256]{2,1,0:T(8,128)(2,1)S(1)} %get-tuple-element.35), channel_id=1, source_target_pairs={{8,0},{16,8},{24,16},{32,24},{40,32},{48,40},{56,48},{64,56},{72,6... | collective-permute-start | bytes 1572872 | tf_op jit(solution)/shard_map/ppermute | solution.py:16
  42.0 2.4 %collective-permute-start = (bf16[2,512,256]{2,1,0:T(8,128)(2,1)S(1)}, bf16[2,512,256]{2,1,0:T(8,128)(2,1)}, u32[]{:S(2)}, u32[]{:S(2)}) collective-permute-start(bf16[2,512,256]{2,1,0:T(8,128)(2,1)S(1)} %get-tuple-element.35), channel_id=1, source_target_pairs={{0,8},{8,16},{16,24},{24,32},{32,40},{40,48},{48,56},{56,64},{64,7... | collective-permute-start | bytes 1572872 | tf_op jit(solution)/shard_map/ppermute | solution.py:16
  49.4 0.7 copy.83
  51.2 3.5 %collective-permute-start.2 = (bf16[2,512,256]{2,1,0:T(8,128)(2,1)S(1)}, bf16[2,512,256]{2,1,0:T(8,128)(2,1)}, u32[]{:S(2)}, u32[]{:S(2)}) collective-permute-start(bf16[2,512,256]{2,1,0:T(8,128)(2,1)S(1)} %get-tuple-element.35), channel_id=1, source_target_pairs={{0,16},{8,24},{16,32},{24,40},{32,48},{40,56},{48,64},{56,72},{64,... | collective-permute-start | bytes 1572872 | tf_op jit(solution)/shard_map/ppermute | solution.py:16
  54.7 4.5 %collective-permute-start.3 = (bf16[2,512,256]{2,1,0:T(8,128)(2,1)S(1)}, bf16[2,512,256]{2,1,0:T(8,128)(2,1)}, u32[]{:S(2)}, u32[]{:S(2)}) collective-permute-start(bf16[2,512,256]{2,1,0:T(8,128)(2,1)S(1)} %get-tuple-element.35), channel_id=1, source_target_pairs={{16,0},{24,8},{32,16},{40,24},{48,32},{56,40},{64,48},{72,56},{80,... | collective-permute-start | bytes 1572872 | tf_op jit(solution)/shard_map/ppermute | solution.py:16
  59.2 7.1 %all-to-all-start.2 = ((bf16[64,8,256]{2,0,1:T(8,128)(2,1)}), bf16[64,8,256]{2,0,1:T(8,128)(2,1)S(1)}, u32[]{:S(2)}, u32[]{:S(2)}) async-start(bf16[64,8,256]{2,0,1:T(8,128)(2,1)} %bitcast.121), calls=%async_computation.2 | async-start | bytes 524288 | tf_op jit(solution)/shard_map/all_to_all | solution.py:56
  66.4 0.8 copy.67
  67.3 1.6 %gather_fusion.1 = bf16[2,2,128,256]{3,2,1,0:T(8,128)(2,1)S(1)} fusion(bf16[2,4,128,256]{3,2,1,0:T(8,128)(2,1)} %bitcast.7, s32[1024]{0:T(1024)S(1)} %pad_clamp_fusion), kind=kCustom, calls=%fused_computation.1.clone | custom fusion | bytes 524296 | tf_op jit(solution)/shard_map/jit(_take)/gather | solution.py:23
  69.0 1.6 %gather_fusion = bf16[2,2,128,256]{3,2,1,0:T(8,128)(2,1)S(1)} fusion(bf16[2,4,128,256]{3,2,1,0:T(8,128)(2,1)} %bitcast.4, s32[1024]{0:T(1024)S(1)} %pad_clamp_fusion.1), kind=kCustom, calls=%fused_computation.clone | custom fusion | bytes 524296 | tf_op jit(solution)/shard_map/jit(_take)/gather | solution.py:23
  70.8 0.9 fusion.21
  71.8 0.9 fusion.19
  72.7 6.3 %all-to-all-done.2 = bf16[64,8,256]{2,0,1:T(8,128)(2,1)S(1)} async-done(((bf16[64,8,256]{2,0,1:T(8,128)(2,1)}), bf16[64,8,256]{2,0,1:T(8,128)(2,1)S(1)}, u32[]{:S(2)}, u32[]{:S(2)}) %all-to-all-start.2) | async-done | bytes 262176 | tf_op jit(solution)/shard_map/all_to_all | solution.py:56
  80.0 0.6 fusion.13
  81.1 0.6 fusion.5
  81.8 1.0 fusion.10
  84.4 0.6 fusion.16
  85.8 0.6 fusion.4
  86.4 1.0 fusion.9
  88.1 0.8 copy.51
  89.0 4.1 %all-to-all-start.3 = ((bf16[8,64,256]{2,1,0:T(8,128)(2,1)}), bf16[8,64,256]{2,1,0:T(8,128)(2,1)}, u32[]{:S(2)}, u32[]{:S(2)}) async-start(bf16[8,64,256]{2,1,0:T(8,128)(2,1)} %bitcast.27), calls=%async_computation.3 | async-start | bytes 524288 | tf_op jit(solution)/shard_map/all_to_all | solution.py:135
  93.1 0.8 copy.56
  94.3 2.4 %collective-permute-start.4 = (bf16[2,256,256]{1,2,0:T(8,128)(2,1)S(1)}, bf16[2,256,256]{1,2,0:T(8,128)(2,1)S(1)}, u32[]{:S(2)}, u32[]{:S(2)}) collective-permute-start(bf16[2,256,256]{1,2,0:T(8,128)(2,1)S(1)} %get-tuple-element.31), channel_id=1, source_target_pairs={{8,0},{16,8},{24,16},{32,24},{40,32},{48,40},{56,48},{64,56},{72,6... | collective-permute-start | bytes 786440 | tf_op jit(solution)/shard_map/ppermute | solution.py:16
  96.8 1.9 %collective-permute-start.5 = (bf16[2,256,256]{1,2,0:T(8,128)(2,1)S(1)}, bf16[2,256,256]{1,2,0:T(8,128)(2,1)S(1)}, u32[]{:S(2)}, u32[]{:S(2)}) collective-permute-start(bf16[2,256,256]{1,2,0:T(8,128)(2,1)S(1)} %get-tuple-element.32), channel_id=1, source_target_pairs={{0,8},{8,16},{16,24},{24,32},{32,40},{40,48},{48,56},{56,64},{64,7... | collective-permute-start | bytes 786440 | tf_op jit(solution)/shard_map/ppermute | solution.py:16
  99.2 3.0 %collective-permute-start.6 = (bf16[2,128,256]{1,2,0:T(8,128)(2,1)S(1)}, bf16[2,128,256]{1,2,0:T(8,128)(2,1)S(1)}, u32[]{:S(2)}, u32[]{:S(2)}) collective-permute-start(bf16[2,128,256]{1,2,0:T(8,128)(2,1)S(1)} %get-tuple-element.29), channel_id=1, source_target_pairs={{16,0},{24,8},{32,16},{40,24},{48,32},{56,40},{64,48},{72,56},{80,... | collective-permute-start | bytes 393224 | tf_op jit(solution)/shard_map/ppermute | solution.py:16
  102.2 2.8 %collective-permute-start.7 = (bf16[2,128,256]{1,2,0:T(8,128)(2,1)S(1)}, bf16[2,128,256]{1,2,0:T(8,128)(2,1)}, u32[]{:S(2)}, u32[]{:S(2)}) collective-permute-start(bf16[2,128,256]{1,2,0:T(8,128)(2,1)S(1)} %get-tuple-element.30), channel_id=1, source_target_pairs={{0,16},{8,24},{16,32},{24,40},{32,48},{40,56},{48,64},{56,72},{64,... | collective-permute-start | bytes 393224 | tf_op jit(solution)/shard_map/ppermute | solution.py:16
  105.1 1.5 collective-permute-done.5
  106.9 0.8 scatter_fusion
  107.9 6.9 %all-to-all-start.5 = ((bf16[8,64,256]{2,1,0:T(8,128)(2,1)}), bf16[8,64,256]{2,1,0:T(8,128)(2,1)S(1)}, u32[]{:S(2)}, u32[]{:S(2)}) async-start(bf16[8,64,256]{2,1,0:T(8,128)(2,1)} %bitcast.32), calls=%async_computation.5 | async-start | bytes 524288 | tf_op jit(solution)/shard_map/all_to_all | solution.py:136
  114.8 1.6 %add_select_fusion = f32[2,1,128,256]{2,3,0,1:T(8,128)S(1)} fusion(f32[2,1,128,256]{2,3,0,1:T(8,128)S(1)} %copy.69, bf16[2,128,256]{1,2,0:T(8,128)(2,1)} %collective-permute-done.7, bf16[2,128,256]{1,2,0:T(8,128)(2,1)S(1)} %collective-permute-done.6, pred[]{:T(512)} %and_reduce_fusion), kind=kLoop, calls=%fused_computation.36 | loop fusion | flops 327680 | bytes 786433 | tf_op jit(solution)/shard_map/select.1
  116.7 0.7 fusion.33
  117.4 9.9 %all-to-all-done.5 = bf16[8,64,256]{2,1,0:T(8,128)(2,1)S(1)} async-done(((bf16[8,64,256]{2,1,0:T(8,128)(2,1)}), bf16[8,64,256]{2,1,0:T(8,128)(2,1)S(1)}, u32[]{:S(2)}, u32[]{:S(2)}) %all-to-all-start.5) | async-done | bytes 262176 | tf_op jit(solution)/shard_map/all_to_all | solution.py:136
  127.3 14.8 %all_to_all.140 = bf16[8,64,256]{2,1,0:T(8,128)(2,1)S(1)} all-to-all(bf16[8,64,256]{2,1,0:T(8,128)(2,1)S(1)} %bitcast.142), channel_id=1, replica_groups=mesh['frame'=32,'head'=8] {'head'}, dimensions={0} | all-to-all | bytes 524288 | tf_op jit(solution)/shard_map/all_to_all | solution.py:137
  142.1 3.4 %all-to-all-start.7 = ((bf16[8,64,256]{2,1,0:T(8,128)(2,1)}), bf16[8,64,256]{2,1,0:T(8,128)(2,1)S(1)}, u32[]{:S(2)}, u32[]{:S(2)}) async-start(bf16[8,64,256]{2,1,0:T(8,128)(2,1)} %bitcast.45), calls=%async_computation.7 | async-start | bytes 524288 | tf_op jit(solution)/shard_map/all_to_all | solution.py:138
  145.5 1.7 %copy.74 = bf16[8,8,8,256]{3,2,0,1:T(8,128)(2,1)} copy(bf16[8,8,8,256]{3,2,1,0:T(8,128)(2,1)} %bitcast.61) | data formatting | bytes 524288 | tf_op jit(solution)/shard_map/all_to_all | solution.py:135
  147.2 0.7 copy.75
  147.9 0.7 copy.76
  148.6 9.1 %all-to-all-done.7 = bf16[8,64,256]{2,1,0:T(8,128)(2,1)S(1)} async-done(((bf16[8,64,256]{2,1,0:T(8,128)(2,1)}), bf16[8,64,256]{2,1,0:T(8,128)(2,1)S(1)}, u32[]{:S(2)}, u32[]{:S(2)}) %all-to-all-start.7) | async-done | bytes 262176 | tf_op jit(solution)/shard_map/all_to_all | solution.py:138
  157.7 0.7 copy.77
  (86 shorter events, 9.7 us)
Async XLA Ops:
  0.6 14.6 %copy-start.8 = (s32[4]{0:T(128)S(1)}, s32[4]{0:T(128)}, u32[]{:S(2)}) copy-start(s32[4]{0:T(128)} %constant.94.clone.1) | copy-start | bytes 52
  0.6 13.2 %copy-start.3 = (bf16[64,2048]{1,0:T(8,128)(2,1)S(1)}, bf16[64,2048]{1,0:T(8,128)(2,1)}, u32[]{:S(2)}) copy-start(bf16[64,2048]{1,0:T(8,128)(2,1)} %param.13) | copy-start | bytes 786436
  0.7 25.6 %copy-start.4 = (bf16[64,2048]{1,0:T(8,128)(2,1)S(1)}, bf16[64,2048]{1,0:T(8,128)(2,1)}, u32[]{:S(2)}) copy-start(bf16[64,2048]{1,0:T(8,128)(2,1)} %param.14) | copy-start | bytes 786436
  2.4 20.3 %all-to-all-start = ((bf16[64,8,256]{2,0,1:T(8,128)(2,1)}), bf16[64,8,256]{2,0,1:T(8,128)(2,1)S(1)}, u32[]{:S(2)}, u32[]{:S(2)}) async-start(bf16[64,8,256]{2,0,1:T(8,128)(2,1)} %bitcast.123), calls=%async_computation | async-start | bytes 524288 | tf_op jit(solution)/shard_map/all_to_all | solution.py:57
  22.7 13.8 %all-to-all-start.1 = ((bf16[64,8,256]{2,0,1:T(8,128)(2,1)}), bf16[64,8,256]{2,0,1:T(8,128)(2,1)S(1)}, u32[]{:S(2)}, u32[]{:S(2)}) async-start(bf16[64,8,256]{2,0,1:T(8,128)(2,1)} %bitcast.122), calls=%async_computation.1 | async-start | bytes 524288 | tf_op jit(solution)/shard_map/all_to_all | solution.py:58
  26.3 23.1 %copy-start.5 = (bf16[64,2048]{1,0:T(8,128)(2,1)S(1)}, bf16[64,2048]{1,0:T(8,128)(2,1)}, u32[]{:S(2)}) copy-start(bf16[64,2048]{1,0:T(8,128)(2,1)} %param.11) | copy-start | bytes 786436
  36.5 22.7 %all-to-all-start.4 = ((bf16[64,8,256]{2,0,1:T(8,128)(2,1)}), bf16[64,8,256]{2,0,1:T(8,128)(2,1)S(1)}, u32[]{:S(2)}, u32[]{:S(2)}) async-start(bf16[64,8,256]{2,0,1:T(8,128)(2,1)} %bitcast.120), calls=%async_computation.4 | async-start | bytes 524288 | tf_op jit(solution)/shard_map/all_to_all | solution.py:59
  40.0 27.2 %collective-permute-start.1 = (bf16[2,512,256]{2,1,0:T(8,128)(2,1)S(1)}, bf16[2,512,256]{2,1,0:T(8,128)(2,1)}, u32[]{:S(2)}, u32[]{:S(2)}) collective-permute-start(bf16[2,512,256]{2,1,0:T(8,128)(2,1)S(1)} %get-tuple-element.35), channel_id=1, source_target_pairs={{8,0},{16,8},{24,16},{32,24},{40,32},{48,40},{56,48},{64,56},{72,6... | collective-permute-start | bytes 1572872 | tf_op jit(solution)/shard_map/ppermute | solution.py:16
  42.0 27.0 %collective-permute-start = (bf16[2,512,256]{2,1,0:T(8,128)(2,1)S(1)}, bf16[2,512,256]{2,1,0:T(8,128)(2,1)}, u32[]{:S(2)}, u32[]{:S(2)}) collective-permute-start(bf16[2,512,256]{2,1,0:T(8,128)(2,1)S(1)} %get-tuple-element.35), channel_id=1, source_target_pairs={{0,8},{8,16},{16,24},{24,32},{32,40},{40,48},{48,56},{56,64},{64,7... | collective-permute-start | bytes 1572872 | tf_op jit(solution)/shard_map/ppermute | solution.py:16
  51.2 19.6 %collective-permute-start.2 = (bf16[2,512,256]{2,1,0:T(8,128)(2,1)S(1)}, bf16[2,512,256]{2,1,0:T(8,128)(2,1)}, u32[]{:S(2)}, u32[]{:S(2)}) collective-permute-start(bf16[2,512,256]{2,1,0:T(8,128)(2,1)S(1)} %get-tuple-element.35), channel_id=1, source_target_pairs={{0,16},{8,24},{16,32},{24,40},{32,48},{40,56},{48,64},{56,72},{64,... | collective-permute-start | bytes 1572872 | tf_op jit(solution)/shard_map/ppermute | solution.py:16
  54.7 17.0 %collective-permute-start.3 = (bf16[2,512,256]{2,1,0:T(8,128)(2,1)S(1)}, bf16[2,512,256]{2,1,0:T(8,128)(2,1)}, u32[]{:S(2)}, u32[]{:S(2)}) collective-permute-start(bf16[2,512,256]{2,1,0:T(8,128)(2,1)S(1)} %get-tuple-element.35), channel_id=1, source_target_pairs={{16,0},{24,8},{32,16},{40,24},{48,32},{56,40},{64,48},{72,56},{80,... | collective-permute-start | bytes 1572872 | tf_op jit(solution)/shard_map/ppermute | solution.py:16
  59.2 19.8 %all-to-all-start.2 = ((bf16[64,8,256]{2,0,1:T(8,128)(2,1)}), bf16[64,8,256]{2,0,1:T(8,128)(2,1)S(1)}, u32[]{:S(2)}, u32[]{:S(2)}) async-start(bf16[64,8,256]{2,0,1:T(8,128)(2,1)} %bitcast.121), calls=%async_computation.2 | async-start | bytes 524288 | tf_op jit(solution)/shard_map/all_to_all | solution.py:56
  79.0 4.4 %copy-start = (bf16[64,8,256]{2,0,1:T(8,128)(2,1)}, bf16[64,8,256]{2,0,1:T(8,128)(2,1)S(1)}, u32[]{:S(2)}) copy-start(bf16[64,8,256]{2,0,1:T(8,128)(2,1)S(1)} %all-to-all-done.2) | copy-start | bytes 786436
  84.4 0.9 copy-start.2
  86.4 1.1 copy-start.1
  88.1 5.0 %copy-start.6 = (bf16[512,128]{0,1:T(8,128)(2,1)S(1)}, bf16[512,128]{0,1:T(8,128)(2,1)}, u32[]{:S(2)}) copy-start(bf16[512,128]{0,1:T(8,128)(2,1)} %fusion.10) | copy-start | bytes 393220
  88.1 5.0 %copy-start.7 = (bf16[512,128]{0,1:T(8,128)(2,1)S(1)}, bf16[512,128]{0,1:T(8,128)(2,1)}, u32[]{:S(2)}) copy-start(bf16[512,128]{0,1:T(8,128)(2,1)} %fusion.9) | copy-start | bytes 393220
  89.0 18.9 %all-to-all-start.3 = ((bf16[8,64,256]{2,1,0:T(8,128)(2,1)}), bf16[8,64,256]{2,1,0:T(8,128)(2,1)}, u32[]{:S(2)}, u32[]{:S(2)}) async-start(bf16[8,64,256]{2,1,0:T(8,128)(2,1)} %bitcast.27), calls=%async_computation.3 | async-start | bytes 524288 | tf_op jit(solution)/shard_map/all_to_all | solution.py:135
  94.3 10.7 %collective-permute-start.4 = (bf16[2,256,256]{1,2,0:T(8,128)(2,1)S(1)}, bf16[2,256,256]{1,2,0:T(8,128)(2,1)S(1)}, u32[]{:S(2)}, u32[]{:S(2)}) collective-permute-start(bf16[2,256,256]{1,2,0:T(8,128)(2,1)S(1)} %get-tuple-element.31), channel_id=1, source_target_pairs={{8,0},{16,8},{24,16},{32,24},{40,32},{48,40},{56,48},{64,56},{72,6... | collective-permute-start | bytes 786440 | tf_op jit(solution)/shard_map/ppermute | solution.py:16
  96.8 9.8 %collective-permute-start.5 = (bf16[2,256,256]{1,2,0:T(8,128)(2,1)S(1)}, bf16[2,256,256]{1,2,0:T(8,128)(2,1)S(1)}, u32[]{:S(2)}, u32[]{:S(2)}) collective-permute-start(bf16[2,256,256]{1,2,0:T(8,128)(2,1)S(1)} %get-tuple-element.32), channel_id=1, source_target_pairs={{0,8},{8,16},{16,24},{24,32},{32,40},{40,48},{48,56},{56,64},{64,7... | collective-permute-start | bytes 786440 | tf_op jit(solution)/shard_map/ppermute | solution.py:16
  99.2 15.6 %collective-permute-start.6 = (bf16[2,128,256]{1,2,0:T(8,128)(2,1)S(1)}, bf16[2,128,256]{1,2,0:T(8,128)(2,1)S(1)}, u32[]{:S(2)}, u32[]{:S(2)}) collective-permute-start(bf16[2,128,256]{1,2,0:T(8,128)(2,1)S(1)} %get-tuple-element.29), channel_id=1, source_target_pairs={{16,0},{24,8},{32,16},{40,24},{48,32},{56,40},{64,48},{72,56},{80,... | collective-permute-start | bytes 393224 | tf_op jit(solution)/shard_map/ppermute | solution.py:16
  102.2 12.6 %collective-permute-start.7 = (bf16[2,128,256]{1,2,0:T(8,128)(2,1)S(1)}, bf16[2,128,256]{1,2,0:T(8,128)(2,1)}, u32[]{:S(2)}, u32[]{:S(2)}) collective-permute-start(bf16[2,128,256]{1,2,0:T(8,128)(2,1)S(1)} %get-tuple-element.30), channel_id=1, source_target_pairs={{0,16},{8,24},{16,32},{24,40},{32,48},{40,56},{48,64},{56,72},{64,... | collective-permute-start | bytes 393224 | tf_op jit(solution)/shard_map/ppermute | solution.py:16
  107.9 19.5 %all-to-all-start.5 = ((bf16[8,64,256]{2,1,0:T(8,128)(2,1)}), bf16[8,64,256]{2,1,0:T(8,128)(2,1)S(1)}, u32[]{:S(2)}, u32[]{:S(2)}) async-start(bf16[8,64,256]{2,1,0:T(8,128)(2,1)} %bitcast.32), calls=%async_computation.5 | async-start | bytes 524288 | tf_op jit(solution)/shard_map/all_to_all | solution.py:136
  142.1 15.6 %all-to-all-start.7 = ((bf16[8,64,256]{2,1,0:T(8,128)(2,1)}), bf16[8,64,256]{2,1,0:T(8,128)(2,1)S(1)}, u32[]{:S(2)}, u32[]{:S(2)}) async-start(bf16[8,64,256]{2,1,0:T(8,128)(2,1)} %bitcast.45), calls=%async_computation.7 | async-start | bytes 524288 | tf_op jit(solution)/shard_map/all_to_all | solution.py:138
where the time goes:
time: 160 us; the launch traced here: 158 us
  starting transfers between devices  59.3 us (37%)
  waiting for transfers between devices  43 us (27%)
  local copies, waits for them, and re-layouts  19.6 us (12%)
  blocking collectives  14.8 us (9%)
  matrix products  7.75 us (5%)
  between operations  7.1 us (4%)
  other arithmetic  6.93 us (4%)
    ppermute x8, starting transfers between devices, passed_along(): return lax.ppermute(array, axis, pairs)  22.4 us
    all_to_all x1, blocking collectives, local(): lax.all_to_all(key_grad_local, 'head', split_axis=0, concat_axis=1, tiled...  14.8 us
    all_to_all x1, waiting for transfers between devices, local(): lax.all_to_all(query_all, 'head', split_axis=0, concat_axis=1, tiled=True)  9.91 us
    all_to_all x1, waiting for transfers between devices, local(): lax.all_to_all(value_rows, 'head', split_axis=1, concat_axis=0, tiled=True)  9.53 us
    all_to_all x1, waiting for transfers between devices, local(): lax.all_to_all(value_grad_local, 'head', split_axis=0, concat_axis=1, til...  9.06 us
    all_to_all x1, starting transfers between devices, local(): lax.all_to_all(key_rows, 'head', split_axis=1, concat_axis=0, tiled=True)  8.47 us
    all_to_all x1, starting transfers between devices, local(): lax.all_to_all(query_rows, 'head', split_axis=1, concat_axis=0, tiled=True)  7.13 us
    all_to_all x1, starting transfers between devices, local(): lax.all_to_all(query_all, 'head', split_axis=0, concat_axis=1, tiled=True)  6.93 us
  transfers between devices with their start and end apart: 15, of which 6 were waited for; matrix products, arithmetic and copies ran while one was open for 14% of the time, Pallas kernels for 0%

commit v1 on v0

v1 whole, which is shorter than its diff:
```python
import functools
import math

import jax
import jax.numpy as jnp
from jax import lax
from jax.experimental import pallas as pl
from jax.experimental.pallas import tpu as pltpu
from jax.sharding import PartitionSpec as P

HD = 128
BLK = 128
BF16 = jnp.bfloat16
F32 = jnp.float32
SCALE = 1.0 / math.sqrt(HD)
LOG2E = 1.0 / math.log(2.0)
VMEM_BYTES = 48 * 1024 * 1024

VM = pl.BlockSpec(memory_space=pltpu.VMEM)
SM = pl.BlockSpec(memory_space=pltpu.SMEM)


def call(body, out_shape, in_specs, out_specs, name):
    return pl.pallas_call(
        body,
        out_shape=out_shape,
        in_specs=in_specs,
        out_specs=out_specs,
        name=name,
        compiler_params=pltpu.CompilerParams(vmem_limit_bytes=VMEM_BYTES),
    )


def shifted(array, by):
    length = lax.axis_size("frame")
    pairs = [(i, i + by) for i in range(length) if 0 <= i + by < length]
    return lax.ppermute(array, "frame", pairs)


def pack_pair(first, second, parts):
    rows, width = first.shape
    piece = width // parts

    def body(a_ref, b_ref, out_ref):
        for part in range(parts):
            out_ref[part, 0] = a_ref[:, part * piece : (part + 1) * piece]
            out_ref[part, 1] = b_ref[:, part * piece : (part + 1) * piece]

    shape = jax.ShapeDtypeStruct((parts, 2, rows, piece), first.dtype)
    return call(body, shape, [VM, VM], VM, "pack_pair")(first, second)


def unpack_pair(packed):
    parts, _, rows, piece = packed.shape

    def body(in_ref, a_ref, b_ref):
        for part in range(parts):
            a_ref[:, part * piece : (part + 1) * piece] = in_ref[part, 0]
            b_ref[:, part * piece : (part + 1) * piece] = in_ref[part, 1]

    shape = jax.ShapeDtypeStruct((rows, parts * piece), packed.dtype)
    return call(body, [shape, shape], [VM], [VM, VM], "unpack_pair")(packed)


def pick_blocks(block_order, pair):
    _, _, rows, width = pair.shape
    per = BLK // rows

    def body(order_ref, pair_ref, near_ref, far_ref):
        frame = lax.axis_index("frame")
        for rank in range(2):
            start = order_ref[frame, rank] * per
            for i in range(per):
                taken = pair_ref[start + i]
                near_ref[rank * per + i] = taken
                if rank == 0:
                    far_ref[i] = taken

    near = jax.ShapeDtypeStruct((2 * per, 2, rows, width), pair.dtype)
    far = jax.ShapeDtypeStruct((per, 2, rows, width), pair.dtype)
    return call(body, [near, far], [SM, VM], [VM, VM], "pick_blocks")(block_order, pair)


def dot(a, b, contract):
    return lax.dot_general(a, b, ((contract[:1], contract[1:]), ((), ())), preferred_element_type=F32)


def attention_body(frame_count, pair_ref, query_ref, l1_ref, u1_ref, l2_ref, u2_ref,
                   first_ref, own_ref, gl1_ref, gu1_ref, gl2_ref, gu2_ref):
    frame = lax.axis_index("frame")
    parts, _, rows, width = pair_ref.shape
    tokens = parts * rows
    hidden = [None] + [
        jnp.where(seen, 0.0, -jnp.inf).astype(F32)
        for seen in (frame >= 1, frame + 1 < frame_count, frame >= 2, frame + 2 < frame_count)
    ]
    sources = (pair_ref, l1_ref, u1_ref, l2_ref, u2_ref)
    targets = (None, gl1_ref, gu1_ref, gl2_ref, gu2_ref)
    for head in range(width // HD):
        cols = slice(head * HD, (head + 1) * HD)
        query = query_ref[:, 0, :, cols].reshape(tokens, HD)
        grad = query_ref[:, 1, :, cols].reshape(tokens, HD)
        keys = [s[:, 0, :, cols].reshape(-1, HD) for s in sources]
        values = [s[:, 1, :, cols].reshape(-1, HD) for s in sources]
        scores = []
        for key, bias in zip(keys, hidden):
            part = dot(key, query, (1, 1)) * (SCALE * LOG2E)
            scores.append(part if bias is None else part + bias)
        peak = functools.reduce(jnp.maximum, [jnp.max(s, axis=0, keepdims=True) for s in scores])
        powers = [jnp.exp2(s - peak) for s in scores]
        total = functools.reduce(jnp.add, [jnp.sum(p, axis=0, keepdims=True) for p in powers])
        inverse = 1.0 / total
        weights = [p * inverse for p in powers]
        lows = [w.astype(BF16) for w in weights]
        out_t = functools.reduce(jnp.add, [dot(v, w, (0, 0)) for v, w in zip(values, lows)])
        out = out_t.astype(BF16)
        grad_t = grad.astype(F32).T
        delta = jnp.sum(grad_t * out.astype(F32), axis=0, keepdims=True)
        first_ref[:, 0, :, cols] = out_t.T.astype(BF16).reshape(parts, rows, HD)
        score_grads = [
            (w * (dot(v, grad, (1, 1)) - delta)).astype(BF16) for w, v in zip(weights, values)
        ]
        query_t = functools.reduce(jnp.add, [dot(k, d, (0, 0)) for k, d in zip(keys, score_grads)])
        first_ref[:, 1, :, cols] = (query_t * SCALE).T.astype(BF16).reshape(parts, rows, HD)
        for low, score_grad, target in zip(lows, score_grads, targets):
            key_part = dot(score_grad, query, (1, 0)) * SCALE
            value_part = dot(low, grad, (1, 0))
            if target is None:
                own_ref[:, 0, :, cols] = key_part.reshape(parts, rows, HD)
                own_ref[:, 1, :, cols] = value_part.reshape(parts, rows, HD)
            else:
                target[:, 0, :, cols] = key_part.astype(BF16).reshape(-1, rows, HD)
                target[:, 1, :, cols] = value_part.astype(BF16).reshape(-1, rows, HD)


def attention(pair, query, panels):
    shape = jax.ShapeDtypeStruct
    outs = [shape(pair.shape, BF16), shape(pair.shape, F32)] + [shape(p.shape, BF16) for p in panels]
    body = functools.partial(attention_body, lax.axis_size("frame"))
    return call(body, outs, [VM] * 6, [VM] * 6, "attention")(pair, query, *panels)


def add_returned(block_order, own, returned):
    parts, _, rows, width = own.shape
    per = BLK // rows

    def body(order_ref, own_ref, a1_ref, b1_ref, a2_ref, b2_ref, out_ref):
        frame = lax.axis_index("frame")
        out_ref[...] = own_ref[...].astype(BF16)
        for rank in range(2):
            start = order_ref[frame, rank] * per
            for i in range(per):
                at = rank * per + i
                term = a1_ref[at].astype(F32) + b1_ref[at].astype(F32)
                if rank == 0:
                    term = term + (a2_ref[i].astype(F32) + b2_ref[i].astype(F32))
                out_ref[start + i] = (own_ref[start + i] + term).astype(BF16)

    return call(
        body, jax.ShapeDtypeStruct(own.shape, BF16), [SM] + [VM] * 5, VM, "add_returned"
    )(block_order, own, *returned)


def exchange(packed):
    return lax.all_to_all(packed, "head", 0, 0)


def local(query_rows, key_rows, value_rows, out_grad, block_order):
    parts = lax.axis_size("head")
    pair = exchange(pack_pair(key_rows, value_rows, parts))
    query = exchange(pack_pair(query_rows, out_grad, parts))
    near, far = pick_blocks(block_order, pair)
    panels = (shifted(near, 1), shifted(near, -1), shifted(far, 2), shifted(far, -2))
    first, own, low1, up1, low2, up2 = attention(pair, query, panels)
    returned = (shifted(low1, -1), shifted(up1, 1), shifted(low2, -2), shifted(up2, 2))
    attended, query_grad = unpack_pair(exchange(first))
    second = add_returned(block_order, own, returned)
    key_grad, value_grad = unpack_pair(exchange(second))
    return (attended, query_grad, key_grad, value_grad)


def solution(mesh):
    rows = P(("frame", "head"), None)
    return jax.shard_map(
        local,
        mesh=mesh,
        in_specs=(rows, rows, rows, rows, P()),
        out_specs=(rows, rows, rows, rows),
        check_vma=False,
    )
```

time: 160 us -> 112 us (0.70)
  local copies, waits for them, and re-layouts: 19.6 us -> 2.65 us
  blocking collectives: 14.8 us -> 0 us
  Pallas kernels: 0 us -> 11.9 us
  starting transfers between devices: 59.3 us -> 48.6 us
  matrix products: 7.75 us -> 0 us
  other arithmetic: 6.93 us -> 0 us
  between operations: 7.1 us -> 0.76 us
  waiting for transfers between devices: 43 us -> 46.5 us
    all_to_all x1 -> x0, blocking collectives: 14.8 us -> none  [local(): lax.all_to_all(key_grad_local, 'head', split_axis=0, concat_axis=1, tiled...]
    pallas_call x0 -> x7, Pallas kernels: none -> 11.9 us  [the longest x1 5.9 us: attention(): call(body, outs, [VM] * 6, [VM] * 6, 'attention')(pair, query, *panels)]
    all_to_all x7 -> x4, starting transfers between devices: 36.8 us -> 25.3 us  [exchange(): return lax.all_to_all(packed, 'head', 0, 0)]
    dot_general x12 -> x0, matrix products: 7.75 us -> none  [the longest x2 2.08 us: attend_tile(): jnp.dot(score_grad, key_head, preferred_element_type=jnp.float32)]
    all_to_all x8 -> x0, local copies, waits for them, and re-layouts: 7.72 us -> none  [the longest x1 1.73 us: local(): lax.all_to_all(key_rows, 'head', split_axis=1, concat_axis=0, tiled=True)]
    ppermute x8, waiting for transfers between devices: 1.5 us -> 6.35 us  [shifted(): return lax.ppermute(array, 'frame', pairs)]
    gather x2 -> x0, local copies, waits for them, and re-layouts: 3.21 us -> none  [pick_blocks(): taken = jnp.take(stacked, chosen, axis=1)]
    slice x10 -> x0, local copies, waits for them, and re-layouts: 3.05 us -> none  [the longest x1 0.74 us: local(): local_grads[1].reshape(token_count, feature_width).astype(jnp.bfloat16)]
  transfers between devices with their start and end apart: 15 -> 12, of which waited for: 6 -> 7; matrix products, arithmetic and copies ran while one was open for 14% -> 0% of each run, Pallas kernels for 0% -> 4%
where the time goes in v1:
time: 112 us; the launch traced here: 110 us
  starting transfers between devices  48.6 us (43%)
  waiting for transfers between devices  46.5 us (42%)
  Pallas kernels  11.9 us (11%)
  local copies, waits for them, and re-layouts  2.65 us (2%)
    all_to_all x4, waiting for transfers between devices, exchange(): return lax.all_to_all(packed, 'head', 0, 0)  40.2 us
    all_to_all x4, starting transfers between devices, exchange(): return lax.all_to_all(packed, 'head', 0, 0)  25.3 us
    ppermute x8, starting transfers between devices, shifted(): return lax.ppermute(array, 'frame', pairs)  23.3 us
    ppermute x8, waiting for transfers between devices, shifted(): return lax.ppermute(array, 'frame', pairs)  6.35 us
    pallas_call x1, Pallas kernels, attention(): call(body, outs, [VM] * 6, [VM] * 6, 'attention')(pair, query, *panels)  5.9 us
    unnamed x15, local copies, waits for them, and re-layouts  2.65 us
  transfers between devices with their start and end apart: 12, of which 7 were waited for; matrix products, arithmetic and copies ran while one was open for 0% of the time, Pallas kernels for 4%

profile of v1, /device:TPU:4, one launch (start us, length us, event | category | flops | bytes accessed | tf_op | source)
XLA Modules:
  0.0 110.4 jit_solution(6086037835113867403)
XLA Ops:
  0.6 0.0 copy-start
  0.6 0.9 copy-done
  1.6 0.0 copy-start.1
  1.6 0.9 copy-done.1
  2.5 0.8 pack_pair.2
  3.4 0.0 copy-start.2
  3.4 0.0 copy-start.3
  3.4 8.6 %all-to-all-start = ((bf16[8,2,64,256]{3,2,1,0:T(8,128)(2,1)}), bf16[8,2,64,256]{3,2,1,0:T(8,128)(2,1)S(1)}, u32[]{:S(2)}, u32[]{:S(2)}) async-start(bf16[8,2,64,256]{3,2,1,0:T(8,128)(2,1)} %pack_pair.2), calls=%async_computation | async-start | bytes 1048576 | tf_op jit(solution)/shard_map/all_to_all | solution.py:165
  12.0 0.0 copy-done.2
  12.0 0.0 copy-done.3
  12.0 0.8 pack_pair.3
  12.8 0.0 copy-start.6
  12.8 16.6 %all-to-all-done.pair_ref = bf16[8,2,64,256]{3,2,1,0:T(8,128)(2,1)S(1)} async-done(((bf16[8,2,64,256]{3,2,1,0:T(8,128)(2,1)}), bf16[8,2,64,256]{3,2,1,0:T(8,128)(2,1)S(1)}, u32[]{:S(2)}, u32[]{:S(2)}) %all-to-all-start) | async-done | bytes 524320 | tf_op jit(solution)/shard_map/all_to_all | solution.py:165
  29.5 3.5 %all-to-all-start.1 = ((bf16[8,2,64,256]{3,2,1,0:T(8,128)(2,1)}), bf16[8,2,64,256]{3,2,1,0:T(8,128)(2,1)S(1)}, u32[]{:S(2)}, u32[]{:S(2)}) async-start(bf16[8,2,64,256]{3,2,1,0:T(8,128)(2,1)} %pack_pair.3), calls=%async_computation.1 | async-start | bytes 1048576 | tf_op jit(solution)/shard_map/all_to_all | solution.py:165
  33.0 0.0 copy-done.6
  33.0 0.1 copy.9.order_ref
  33.1 0.8 pick_blocks.1
  33.9 4.5 %collective-permute-start.1 = (bf16[4,2,64,256]{3,2,1,0:T(8,128)(2,1)S(1)}, bf16[4,2,64,256]{3,2,1,0:T(8,128)(2,1)S(1)}, u32[]{:S(2)}, u32[]{:S(2)}) collective-permute-start(bf16[4,2,64,256]{3,2,1,0:T(8,128)(2,1)S(1)} %get-tuple-element.16), channel_id=1, source_target_pairs={{8,0},{16,8},{24,16},{32,24},{40,32},{48,40},{56,48},{64,56},{72,6... | collective-permute-start | bytes 786440 | tf_op jit(solution)/shard_map/ppermute | solution.py:37
  38.4 1.9 %collective-permute-start = (bf16[4,2,64,256]{3,2,1,0:T(8,128)(2,1)S(1)}, bf16[4,2,64,256]{3,2,1,0:T(8,128)(2,1)S(1)}, u32[]{:S(2)}, u32[]{:S(2)}) collective-permute-start(bf16[4,2,64,256]{3,2,1,0:T(8,128)(2,1)S(1)} %get-tuple-element.16), channel_id=1, source_target_pairs={{0,8},{8,16},{16,24},{24,32},{32,40},{40,48},{48,56},{56,64},{64,7... | collective-permute-start | bytes 786440 | tf_op jit(solution)/shard_map/ppermute | solution.py:37
  40.4 2.8 %collective-permute-start.3 = (bf16[2,2,64,256]{3,2,1,0:T(8,128)(2,1)S(1)}, bf16[2,2,64,256]{3,2,1,0:T(8,128)(2,1)S(1)}, u32[]{:S(2)}, u32[]{:S(2)}) collective-permute-start(bf16[2,2,64,256]{3,2,1,0:T(8,128)(2,1)S(1)} %get-tuple-element.17), channel_id=1, source_target_pairs={{16,0},{24,8},{32,16},{40,24},{48,32},{56,40},{64,48},{72,56},{80,... | collective-permute-start | bytes 393224 | tf_op jit(solution)/shard_map/ppermute | solution.py:37
  43.2 3.1 %collective-permute-start.2 = (bf16[2,2,64,256]{3,2,1,0:T(8,128)(2,1)S(1)}, bf16[2,2,64,256]{3,2,1,0:T(8,128)(2,1)S(1)}, u32[]{:S(2)}, u32[]{:S(2)}) collective-permute-start(bf16[2,2,64,256]{3,2,1,0:T(8,128)(2,1)S(1)} %get-tuple-element.17), channel_id=1, source_target_pairs={{0,16},{8,24},{16,32},{24,40},{32,48},{40,56},{48,64},{56,72},{64,... | collective-permute-start | bytes 393224 | tf_op jit(solution)/shard_map/ppermute | solution.py:37
  46.2 4.6 %all-to-all-done.1.query_ref = bf16[8,2,64,256]{3,2,1,0:T(8,128)(2,1)S(1)} async-done(((bf16[8,2,64,256]{3,2,1,0:T(8,128)(2,1)}), bf16[8,2,64,256]{3,2,1,0:T(8,128)(2,1)S(1)}, u32[]{:S(2)}, u32[]{:S(2)}) %all-to-all-start.1) | async-done | bytes 524320 | tf_op jit(solution)/shard_map/all_to_all | solution.py:165
  50.8 0.0 collective-permute-done.3.u2_ref
  50.8 1.3 %collective-permute-done.2.l2_ref = bf16[2,2,64,256]{3,2,1,0:T(8,128)(2,1)S(1)} collective-permute-done((bf16[2,2,64,256]{3,2,1,0:T(8,128)(2,1)S(1)}, bf16[2,2,64,256]{3,2,1,0:T(8,128)(2,1)S(1)}, u32[]{:S(2)}, u32[]{:S(2)}) %collective-permute-start.2) | collective-permute-done | bytes 131104 | tf_op jit(solution)/shard_map/ppermute | solution.py:37
  52.1 0.0 collective-permute-done.1.u1_ref
  52.1 0.0 collective-permute-done.l1_ref
  52.1 5.9 %attention.1 = (bf16[8,2,64,256]{3,2,1,0:T(8,128)(2,1)}, f32[8,2,64,256]{3,2,1,0:T(8,128)S(1)}, bf16[4,2,64,256]{3,2,1,0:T(8,128)(2,1)S(1)}, bf16[4,2,64,256]{3,...) custom-call(bf16[8,2,64,256]{3,2,1,0:T(8,128)(2,1)S(1)} %all-to-all-done.pair_ref, ...), custom_call_target="tpu_custom_call" | custom-call | tf_op jit(solution)/shard_map/attention/pallas_call | solution.py:140
  58.0 0.0 copy-start.4
  58.0 0.7 copy-done.4
  58.7 0.0 copy-start.5
  58.7 7.2 %all-to-all-start.2 = ((bf16[8,2,64,256]{3,2,1,0:T(8,128)(2,1)}), bf16[8,2,64,256]{3,2,1,0:T(8,128)(2,1)S(1)}, u32[]{:S(2)}, u32[]{:S(2)}) async-start(bf16[8,2,64,256]{3,2,1,0:T(8,128)(2,1)} %get-tuple-element.18), calls=%async_computation.2 | async-start | bytes 1048576 | tf_op jit(solution)/shard_map/all_to_all | solution.py:165
  65.9 2.7 %collective-permute-start.4 = (bf16[4,2,64,256]{3,2,1,0:T(8,128)(2,1)S(1)}, bf16[4,2,64,256]{3,2,1,0:T(8,128)(2,1)S(1)}, u32[]{:S(2)}, u32[]{:S(2)}) collective-permute-start(bf16[4,2,64,256]{3,2,1,0:T(8,128)(2,1)S(1)} %get-tuple-element.22), channel_id=1, source_target_pairs={{8,0},{16,8},{24,16},{32,24},{40,32},{48,40},{56,48},{64,56},{72,6... | collective-permute-start | bytes 786440 | tf_op jit(solution)/shard_map/ppermute | solution.py:37
  68.7 2.4 %collective-permute-start.5 = (bf16[4,2,64,256]{3,2,1,0:T(8,128)(2,1)S(1)}, bf16[4,2,64,256]{3,2,1,0:T(8,128)(2,1)S(1)}, u32[]{:S(2)}, u32[]{:S(2)}) collective-permute-start(bf16[4,2,64,256]{3,2,1,0:T(8,128)(2,1)S(1)} %get-tuple-element.23), channel_id=1, source_target_pairs={{0,8},{8,16},{16,24},{24,32},{32,40},{40,48},{48,56},{56,64},{64,7... | collective-permute-start | bytes 786440 | tf_op jit(solution)/shard_map/ppermute | solution.py:37
  71.1 0.0 copy-done.5
  71.1 1.9 %collective-permute-start.6 = (bf16[2,2,64,256]{3,2,1,0:T(8,128)(2,1)S(1)}, bf16[2,2,64,256]{3,2,1,0:T(8,128)(2,1)S(1)}, u32[]{:S(2)}, u32[]{:S(2)}) collective-permute-start(bf16[2,2,64,256]{3,2,1,0:T(8,128)(2,1)S(1)} %copy-done.5), channel_id=1, source_target_pairs={{16,0},{24,8},{32,16},{40,24},{48,32},{56,40},{64,48},{72,56},{80,... | collective-permute-start | bytes 393224 | tf_op jit(solution)/shard_map/ppermute | solution.py:37
  73.1 3.9 %collective-permute-start.7 = (bf16[2,2,64,256]{3,2,1,0:T(8,128)(2,1)S(1)}, bf16[2,2,64,256]{3,2,1,0:T(8,128)(2,1)S(1)}, u32[]{:S(2)}, u32[]{:S(2)}) collective-permute-start(bf16[2,2,64,256]{3,2,1,0:T(8,128)(2,1)S(1)} %get-tuple-element.25), channel_id=1, source_target_pairs={{0,16},{8,24},{16,32},{24,40},{32,48},{40,56},{48,64},{56,72},{64,... | collective-permute-start | bytes 393224 | tf_op jit(solution)/shard_map/ppermute | solution.py:37
  77.0 1.7 %collective-permute-done.6.a2_ref = bf16[2,2,64,256]{3,2,1,0:T(8,128)(2,1)S(1)} collective-permute-done((bf16[2,2,64,256]{3,2,1,0:T(8,128)(2,1)S(1)}, bf16[2,2,64,256]{3,2,1,0:T(8,128)(2,1)S(1)}, u32[]{:S(2)}, u32[]{:S(2)}) %collective-permute-start.6) | collective-permute-done | bytes 131104 | tf_op jit(solution)/shard_map/ppermute | solution.py:37
  78.7 3.4 %collective-permute-done.7.b2_ref = bf16[2,2,64,256]{3,2,1,0:T(8,128)(2,1)S(1)} collective-permute-done((bf16[2,2,64,256]{3,2,1,0:T(8,128)(2,1)S(1)}, bf16[2,2,64,256]{3,2,1,0:T(8,128)(2,1)S(1)}, u32[]{:S(2)}, u32[]{:S(2)}) %collective-permute-start.7) | collective-permute-done | bytes 131104 | tf_op jit(solution)/shard_map/ppermute | solution.py:37
  82.0 0.0 collective-permute-done.4.a1_ref
  82.0 0.0 collective-permute-done.5.b1_ref
  82.1 1.8 %add_returned.1 = bf16[8,2,64,256]{3,2,1,0:T(8,128)(2,1)} custom-call(s32[32,4]{1,0:T(8,128)S(1)} %copy.9.order_ref, f32[8,2,64,256]{3,2,1,0:T(8,128)S(1)} %get-tuple-element.21.own_ref, bf16[4,2,64,256]{3,2,1,0:T(8,128)(2,1)S(1)} %collective-permute-done.4.a1_ref, bf16[4,2,64,256]{3,2,1,0:T(8,128)(2,1)S(1)} %collective-permute-done.5.b1_ref, ...), custom_call_target="tpu_custom_call" | custom-call | tf_op jit(solution)/shard_map/add_returned/pallas_call | solution.py:159
  83.8 1.0 all-to-all-done.2.in_ref
  84.8 5.9 %all-to-all-start.3 = ((bf16[8,2,64,256]{3,2,1,0:T(8,128)(2,1)}), bf16[8,2,64,256]{3,2,1,0:T(8,128)(2,1)S(1)}, u32[]{:S(2)}, u32[]{:S(2)}) async-start(bf16[8,2,64,256]{3,2,1,0:T(8,128)(2,1)} %add_returned.1), calls=%async_computation.3 | async-start | bytes 1048576 | tf_op jit(solution)/shard_map/all_to_all | solution.py:165
  90.8 0.8 unpack_pair.2
  91.6 18.0 %all-to-all-done.3.in_ref = bf16[8,2,64,256]{3,2,1,0:T(8,128)(2,1)S(1)} async-done(((bf16[8,2,64,256]{3,2,1,0:T(8,128)(2,1)}), bf16[8,2,64,256]{3,2,1,0:T(8,128)(2,1)S(1)}, u32[]{:S(2)}, u32[]{:S(2)}) %all-to-all-start.3) | async-done | bytes 524320 | tf_op jit(solution)/shard_map/all_to_all | solution.py:165
  109.6 0.8 unpack_pair.3
Async XLA Ops:
  0.6 1.0 copy-start
  1.6 0.9 copy-start.1
  3.4 8.6 %copy-start.2 = (bf16[64,2048]{1,0:T(8,128)(2,1)S(1)}, bf16[64,2048]{1,0:T(8,128)(2,1)}, u32[]{:S(2)}) copy-start(bf16[64,2048]{1,0:T(8,128)(2,1)} %a_ref.3) | copy-start | bytes 786436
  3.4 8.6 %copy-start.3 = (bf16[64,2048]{1,0:T(8,128)(2,1)S(1)}, bf16[64,2048]{1,0:T(8,128)(2,1)}, u32[]{:S(2)}) copy-start(bf16[64,2048]{1,0:T(8,128)(2,1)} %b_ref.3) | copy-start | bytes 786436
  3.4 26.1 %all-to-all-start = ((bf16[8,2,64,256]{3,2,1,0:T(8,128)(2,1)}), bf16[8,2,64,256]{3,2,1,0:T(8,128)(2,1)S(1)}, u32[]{:S(2)}, u32[]{:S(2)}) async-start(bf16[8,2,64,256]{3,2,1,0:T(8,128)(2,1)} %pack_pair.2), calls=%async_computation | async-start | bytes 1048576 | tf_op jit(solution)/shard_map/all_to_all | solution.py:165
  12.8 20.1 %copy-start.6 = (s32[32,4]{0,1:T(4,128)S(1)}, s32[32,4]{0,1:T(4,128)}, u32[]{:S(2)}) copy-start(s32[32,4]{0,1:T(4,128)} %param.9) | copy-start | bytes 1540
  29.5 21.4 %all-to-all-start.1 = ((bf16[8,2,64,256]{3,2,1,0:T(8,128)(2,1)}), bf16[8,2,64,256]{3,2,1,0:T(8,128)(2,1)S(1)}, u32[]{:S(2)}, u32[]{:S(2)}) async-start(bf16[8,2,64,256]{3,2,1,0:T(8,128)(2,1)} %pack_pair.3), calls=%async_computation.1 | async-start | bytes 1048576 | tf_op jit(solution)/shard_map/all_to_all | solution.py:165
  33.9 18.2 %collective-permute-start.1 = (bf16[4,2,64,256]{3,2,1,0:T(8,128)(2,1)S(1)}, bf16[4,2,64,256]{3,2,1,0:T(8,128)(2,1)S(1)}, u32[]{:S(2)}, u32[]{:S(2)}) collective-permute-start(bf16[4,2,64,256]{3,2,1,0:T(8,128)(2,1)S(1)} %get-tuple-element.16), channel_id=1, source_target_pairs={{8,0},{16,8},{24,16},{32,24},{40,32},{48,40},{56,48},{64,56},{72,6... | collective-permute-start | bytes 786440 | tf_op jit(solution)/shard_map/ppermute | solution.py:37
  38.4 13.7 %collective-permute-start = (bf16[4,2,64,256]{3,2,1,0:T(8,128)(2,1)S(1)}, bf16[4,2,64,256]{3,2,1,0:T(8,128)(2,1)S(1)}, u32[]{:S(2)}, u32[]{:S(2)}) collective-permute-start(bf16[4,2,64,256]{3,2,1,0:T(8,128)(2,1)S(1)} %get-tuple-element.16), channel_id=1, source_target_pairs={{0,8},{8,16},{16,24},{24,32},{32,40},{40,48},{48,56},{56,64},{64,7... | collective-permute-start | bytes 786440 | tf_op jit(solution)/shard_map/ppermute | solution.py:37
  40.4 10.5 %collective-permute-start.3 = (bf16[2,2,64,256]{3,2,1,0:T(8,128)(2,1)S(1)}, bf16[2,2,64,256]{3,2,1,0:T(8,128)(2,1)S(1)}, u32[]{:S(2)}, u32[]{:S(2)}) collective-permute-start(bf16[2,2,64,256]{3,2,1,0:T(8,128)(2,1)S(1)} %get-tuple-element.17), channel_id=1, source_target_pairs={{16,0},{24,8},{32,16},{40,24},{48,32},{56,40},{64,48},{72,56},{80,... | collective-permute-start | bytes 393224 | tf_op jit(solution)/shard_map/ppermute | solution.py:37
  43.2 9.0 %collective-permute-start.2 = (bf16[2,2,64,256]{3,2,1,0:T(8,128)(2,1)S(1)}, bf16[2,2,64,256]{3,2,1,0:T(8,128)(2,1)S(1)}, u32[]{:S(2)}, u32[]{:S(2)}) collective-permute-start(bf16[2,2,64,256]{3,2,1,0:T(8,128)(2,1)S(1)} %get-tuple-element.17), channel_id=1, source_target_pairs={{0,16},{8,24},{16,32},{24,40},{32,48},{40,56},{48,64},{56,72},{64,... | collective-permute-start | bytes 393224 | tf_op jit(solution)/shard_map/ppermute | solution.py:37
  58.0 0.7 copy-start.4
  58.7 12.5 %copy-start.5 = (bf16[2,2,64,256]{3,2,1,0:T(8,128)(2,1)S(1)}, bf16[2,2,64,256]{3,2,1,0:T(8,128)(2,1)}, u32[]{:S(2)}) copy-start(bf16[2,2,64,256]{3,2,1,0:T(8,128)(2,1)} %copy-done.4) | copy-start | bytes 393220
  58.7 26.1 %all-to-all-start.2 = ((bf16[8,2,64,256]{3,2,1,0:T(8,128)(2,1)}), bf16[8,2,64,256]{3,2,1,0:T(8,128)(2,1)S(1)}, u32[]{:S(2)}, u32[]{:S(2)}) async-start(bf16[8,2,64,256]{3,2,1,0:T(8,128)(2,1)} %get-tuple-element.18), calls=%async_computation.2 | async-start | bytes 1048576 | tf_op jit(solution)/shard_map/all_to_all | solution.py:165
  65.9 16.1 %collective-permute-start.4 = (bf16[4,2,64,256]{3,2,1,0:T(8,128)(2,1)S(1)}, bf16[4,2,64,256]{3,2,1,0:T(8,128)(2,1)S(1)}, u32[]{:S(2)}, u32[]{:S(2)}) collective-permute-start(bf16[4,2,64,256]{3,2,1,0:T(8,128)(2,1)S(1)} %get-tuple-element.22), channel_id=1, source_target_pairs={{8,0},{16,8},{24,16},{32,24},{40,32},{48,40},{56,48},{64,56},{72,6... | collective-permute-start | bytes 786440 | tf_op jit(solution)/shard_map/ppermute | solution.py:37
  68.7 13.4 %collective-permute-start.5 = (bf16[4,2,64,256]{3,2,1,0:T(8,128)(2,1)S(1)}, bf16[4,2,64,256]{3,2,1,0:T(8,128)(2,1)S(1)}, u32[]{:S(2)}, u32[]{:S(2)}) collective-permute-start(bf16[4,2,64,256]{3,2,1,0:T(8,128)(2,1)S(1)} %get-tuple-element.23), channel_id=1, source_target_pairs={{0,8},{8,16},{16,24},{24,32},{32,40},{40,48},{48,56},{56,64},{64,7... | collective-permute-start | bytes 786440 | tf_op jit(solution)/shard_map/ppermute | solution.py:37
  71.1 7.5 %collective-permute-start.6 = (bf16[2,2,64,256]{3,2,1,0:T(8,128)(2,1)S(1)}, bf16[2,2,64,256]{3,2,1,0:T(8,128)(2,1)S(1)}, u32[]{:S(2)}, u32[]{:S(2)}) collective-permute-start(bf16[2,2,64,256]{3,2,1,0:T(8,128)(2,1)S(1)} %copy-done.5), channel_id=1, source_target_pairs={{16,0},{24,8},{32,16},{40,24},{48,32},{56,40},{64,48},{72,56},{80,... | collective-permute-start | bytes 393224 | tf_op jit(solution)/shard_map/ppermute | solution.py:37
  73.1 9.0 %collective-permute-start.7 = (bf16[2,2,64,256]{3,2,1,0:T(8,128)(2,1)S(1)}, bf16[2,2,64,256]{3,2,1,0:T(8,128)(2,1)S(1)}, u32[]{:S(2)}, u32[]{:S(2)}) collective-permute-start(bf16[2,2,64,256]{3,2,1,0:T(8,128)(2,1)S(1)} %get-tuple-element.25), channel_id=1, source_target_pairs={{0,16},{8,24},{16,32},{24,40},{32,48},{40,56},{48,64},{56,72},{64,... | collective-permute-start | bytes 393224 | tf_op jit(solution)/shard_map/ppermute | solution.py:37
  84.8 24.8 %all-to-all-start.3 = ((bf16[8,2,64,256]{3,2,1,0:T(8,128)(2,1)}), bf16[8,2,64,256]{3,2,1,0:T(8,128)(2,1)S(1)}, u32[]{:S(2)}, u32[]{:S(2)}) async-start(bf16[8,2,64,256]{3,2,1,0:T(8,128)(2,1)} %add_returned.1), calls=%async_computation.3 | async-start | bytes 1048576 | tf_op jit(solution)/shard_map/all_to_all | solution.py:165

commit v2 on v1

v2 whole, which is shorter than its diff:
```python
import functools
import math

import jax
import jax.numpy as jnp
from jax import lax
from jax.experimental import pallas as pl
from jax.experimental.pallas import tpu as pltpu
from jax.sharding import PartitionSpec as P

HD = 128
BLK = 128
BF16 = jnp.bfloat16
F32 = jnp.float32
SCALE = 1.0 / math.sqrt(HD)
LOG2E = 1.0 / math.log(2.0)
MIB = 1024 * 1024
MASKS = (0, 1, 7, 3, 2, 6, 5, 4)

VM = pl.BlockSpec(memory_space=pltpu.VMEM)
SM = pl.BlockSpec(memory_space=pltpu.SMEM)


def call(body, out_shape, in_specs, out_specs, name, mib, scratch_shapes=()):
    return pl.pallas_call(
        body,
        out_shape=out_shape,
        in_specs=in_specs,
        out_specs=out_specs,
        scratch_shapes=scratch_shapes,
        name=name,
        compiler_params=pltpu.CompilerParams(vmem_limit_bytes=mib * MIB),
    )


def swapped(array, distance, start):
    length = lax.axis_size("frame")
    pairs = []
    for first in range(start, length, 2 * distance):
        for low in range(first, min(first + distance, length - distance)):
            pairs += [(low, low + distance), (low + distance, low)]
    return lax.ppermute(array, "frame", pairs)


SWAPS = ((1, 0), (1, 1), (2, 0), (2, 2))


def has_partner(frame, length, distance, start):
    shifted = frame + (2 * distance - start)
    lower_half = lax.rem(shifted, 2 * distance) < distance
    partner = jnp.where(lower_half, frame + distance, frame - distance)
    return jnp.logical_and(jnp.logical_and(partner >= 0, partner < length), frame >= 0)


def head_swaps(pieces):
    length = lax.axis_size("head")
    return [
        lax.ppermute(piece, "head", [(i, i ^ mask) for i in range(length)]) if mask else piece
        for piece, mask in zip(pieces, MASKS)
    ]


def place_of(slot):
    return jnp.bitwise_xor(lax.axis_index("head"), MASKS[slot])


def columns_of(slot, piece):
    return pl.ds(pl.multiple_of(place_of(slot) * piece, piece), piece)


def pack(arrays, parts):
    rows, width = arrays[0].shape
    count = len(arrays)
    piece = width // parts

    def body(*refs):
        in_refs, out_refs, sem = refs[:count], refs[count:-1], refs[-1]
        copies = []
        for k, out_ref in enumerate(out_refs):
            for i, ref in enumerate(in_refs):
                copies.append(
                    pltpu.make_async_copy(ref.at[:, columns_of(k, piece)], out_ref.at[i], sem.at[k, i])
                )
        for copy in copies:
            copy.start()
        for copy in copies:
            copy.wait()

    shape = jax.ShapeDtypeStruct((count, rows, piece), arrays[0].dtype)
    anywhere = pl.BlockSpec(memory_space=pltpu.HBM)
    arrays = [pltpu.with_memory_space_constraint(array, pltpu.HBM) for array in arrays]
    sems = [pltpu.SemaphoreType.DMA((parts, count))]
    return call(body, [shape] * parts, [anywhere] * count, [VM] * parts, "pack", 4, sems)(*arrays)


def unpack(pieces):
    parts = len(pieces)
    count, rows, piece = pieces[0].shape

    def body(*refs):
        for i, ref in enumerate(refs[parts:]):
            for k in range(parts):
                ref[:, columns_of(k, piece)] = refs[k][i]

    shape = jax.ShapeDtypeStruct((rows, parts * piece), pieces[0].dtype)
    return call(body, [shape] * count, [VM] * parts, [VM] * count, "unpack", 8)(*pieces)


def pick_blocks(block_order, pieces):
    parts = len(pieces)
    _, rows, width = pieces[0].shape
    per = BLK // rows

    def body(order_ref, *refs):
        near_ref, far_ref, all_ref = refs[parts:]
        frame = lax.axis_index("frame")
        for k in range(parts):
            all_ref[place_of(k)] = refs[k][0:2]
        for rank in range(2):
            start = order_ref[rank, frame] * per
            for i in range(per):
                taken = all_ref[start + i]
                near_ref[rank * per + i] = taken
                if rank == 0:
                    far_ref[i] = taken

    near = jax.ShapeDtypeStruct((2 * per, 2, rows, width), BF16)
    far = jax.ShapeDtypeStruct((per, 2, rows, width), BF16)
    scratch = [pltpu.VMEM((parts, 2, rows, width), BF16)]
    return call(
        body, [near, far], [SM] + [VM] * parts, [VM, VM], "pick_blocks", 8, scratch
    )(block_order.T, *pieces)


def dot(a, b, contract):
    return lax.dot_general(a, b, ((contract[:1], contract[1:]), ((), ())), preferred_element_type=F32)


def attention_body(frame_count, parts, *refs):
    piece_refs, panel_refs = refs[:parts], refs[parts : parts + 4]
    first_ref, own_ref, *targets = refs[parts + 4 :]
    frame = lax.axis_index("frame")
    _, rows, width = piece_refs[0].shape
    hidden = [None] + [
        jnp.where(has_partner(frame, frame_count, *swap), 0.0, -jnp.inf).astype(F32) for swap in SWAPS
    ]
    for head in range(width // HD):
        cols = slice(head * HD, (head + 1) * HD)
        key, value, query, grad = [
            jnp.concatenate([ref[i, :, cols] for ref in piece_refs], axis=0) for i in range(4)
        ]
        keys = [key] + [ref[:, 0, :, cols].reshape(-1, HD) for ref in panel_refs]
        values = [value] + [ref[:, 1, :, cols].reshape(-1, HD) for ref in panel_refs]
        scores = []
        for key, bias in zip(keys, hidden):
            part = dot(key, query, (1, 1)) * (SCALE * LOG2E)
            scores.append(part if bias is None else part + bias)
        peak = functools.reduce(jnp.maximum, [jnp.max(s, axis=0, keepdims=True) for s in scores])
        powers = [jnp.exp2(s - peak) for s in scores]
        total = functools.reduce(jnp.add, [jnp.sum(p, axis=0, keepdims=True) for p in powers])
        inverse = 1.0 / total
        weights = [p * inverse for p in powers]
        lows = [w.astype(BF16) for w in weights]
        out_t = functools.reduce(jnp.add, [dot(v, w, (0, 0)) for v, w in zip(values, lows)])
        out = out_t.astype(BF16)
        grad_t = grad.astype(F32).T
        delta = jnp.sum(grad_t * out.astype(F32), axis=0, keepdims=True)
        first_ref[:, 0, :, cols] = out_t.T.astype(BF16).reshape(parts, rows, HD)
        score_grads = [
            (w * (dot(v, grad, (1, 1)) - delta)).astype(BF16) for w, v in zip(weights, values)
        ]
        query_t = functools.reduce(jnp.add, [dot(k, d, (0, 0)) for k, d in zip(keys, score_grads)])
        first_ref[:, 1, :, cols] = (query_t * SCALE).T.astype(BF16).reshape(parts, rows, HD)
        for low, score_grad, target in zip(lows, score_grads, [None] + targets):
            key_part = dot(score_grad, query, (1, 0)) * SCALE
            value_part = dot(low, grad, (1, 0))
            if target is None:
                own_ref[:, 0, :, cols] = key_part.reshape(parts, rows, HD)
                own_ref[:, 1, :, cols] = value_part.reshape(parts, rows, HD)
            else:
                target[:, 0, :, cols] = key_part.astype(BF16).reshape(-1, rows, HD)
                target[:, 1, :, cols] = value_part.astype(BF16).reshape(-1, rows, HD)


def attention(pieces, panels):
    parts = len(pieces)
    _, rows, width = pieces[0].shape
    shape = jax.ShapeDtypeStruct
    two = (parts, 2, rows, width)
    outs = [shape(two, BF16), shape(two, F32)] + [shape(p.shape, BF16) for p in panels]
    body = functools.partial(attention_body, lax.axis_size("frame"), parts)
    return call(body, outs, [VM] * (parts + 4), [VM] * 6, "attention", 32)(*pieces, *panels)


def add_returned(block_order, first, own, returned):
    parts, _, rows, width = own.shape
    per = BLK // rows

    def body(order_ref, first_ref, own_ref, a1_ref, b1_ref, a2_ref, b2_ref, *refs):
        out_refs, sum_ref = refs[:parts], refs[parts]
        frame = lax.axis_index("frame")
        for k in range(parts):
            sum_ref[place_of(k)] = own_ref[k]
        for rank in range(2):
            start = order_ref[rank, frame] * per
            for i in range(per):
                at = rank * per + i
                term = a1_ref[at].astype(F32) + b1_ref[at].astype(F32)
                if rank == 0:
                    term = term + (a2_ref[i].astype(F32) + b2_ref[i].astype(F32))
                sum_ref[start + i] = sum_ref[start + i] + term
        for k in range(parts):
            out_refs[k][0:2] = sum_ref[place_of(k)].astype(BF16)
            out_refs[k][2:4] = first_ref[k]

    shape = jax.ShapeDtypeStruct((4, rows, width), BF16)
    scratch = [pltpu.VMEM(own.shape, F32)]
    return call(
        body, [shape] * parts, [SM] + [VM] * 6, [VM] * parts, "add_returned", 10, scratch
    )(block_order.T, first, own, *returned)


def local(query_rows, key_rows, value_rows, out_grad, block_order):
    parts = lax.axis_size("head")
    arrived = head_swaps(pack((key_rows, value_rows, query_rows, out_grad), parts))
    near, far = pick_blocks(block_order, arrived)
    panels = [swapped(far if swap[0] == 2 else near, *swap) for swap in SWAPS]
    first, own, *parts_of_others = attention(arrived, panels)
    returned = [swapped(part, *swap) for part, swap in zip(parts_of_others, SWAPS)]
    leaving = add_returned(block_order, first, own, returned)
    key_grad, value_grad, attended, query_grad = unpack(head_swaps(leaving))
    return (attended, query_grad, key_grad, value_grad)


def solution(mesh):
    rows = P(("frame", "head"), None)
    return jax.shard_map(
        local,
        mesh=mesh,
        in_specs=(rows, rows, rows, rows, P()),
        out_specs=(rows, rows, rows, rows),
        check_vma=False,
    )
```

time: 112 us -> 96.9 us (0.87)
  waiting for transfers between devices: 46.5 us -> 35.2 us
  Pallas kernels: 11.9 us -> 9.16 us
  local copies, waits for them, and re-layouts: 2.65 us -> 0.01 us
  starting transfers between devices: 48.6 us -> 50.1 us
    all_to_all x4 -> x0, waiting for transfers between devices: 40.2 us -> none  [exchange(): return lax.all_to_all(packed, 'head', 0, 0)]
    ppermute x8 -> x22, waiting for transfers between devices: 6.35 us -> 35.2 us  [the longest x14 24.1 us: head_swaps(): lax.ppermute(piece, 'head', [(i, i ^ mask) for i in range(length)])]
    ppermute x8 -> x22, starting transfers between devices: 23.3 us -> 50.1 us  [the longest x14 34.5 us: head_swaps(): lax.ppermute(piece, 'head', [(i, i ^ mask) for i in range(length)])]
    all_to_all x4 -> x0, starting transfers between devices: 25.3 us -> none  [exchange(): return lax.all_to_all(packed, 'head', 0, 0)]
    pallas_call x7 -> x5, Pallas kernels: 11.9 us -> 9.16 us  [the longest x1 5.12 us: attention(): call(body, outs, [VM] * (parts + 4), [VM] * 6, 'attention', 32)]
    unnamed x15 -> x2, local copies, waits for them, and re-layouts: 2.65 us -> 0.01 us
  transfers between devices with their start and end apart: 12 -> 22, of which waited for: 7 -> 9; matrix products, arithmetic and copies ran while one was open for 0% -> 0% of each run, Pallas kernels for 4% -> 0%
where the time goes in v2:
time: 96.9 us; the launch traced here: 95.2 us
  starting transfers between devices  50.1 us (52%)
  waiting for transfers between devices  35.2 us (36%)
  Pallas kernels  9.16 us (9%)
    ppermute x14, starting transfers between devices, head_swaps(): lax.ppermute(piece, 'head', [(i, i ^ mask) for i in range(length)])  34.5 us
    ppermute x14, waiting for transfers between devices, head_swaps(): lax.ppermute(piece, 'head', [(i, i ^ mask) for i in range(length)])  24.1 us
    ppermute x8, starting transfers between devices, swapped(): return lax.ppermute(array, 'frame', pairs)  15.7 us
    ppermute x8, waiting for transfers between devices, swapped(): return lax.ppermute(array, 'frame', pairs)  11.1 us
    pallas_call x1, Pallas kernels, attention(): call(body, outs, [VM] * (parts + 4), [VM] * 6, 'attention', 32)  5.12 us
  transfers between devices with their start and end apart: 22, of which 9 were waited for; matrix products, arithmetic and copies ran while one was open for 0% of the time, Pallas kernels for 0%

profile of v2, /device:TPU:4, one launch (start us, length us, event | category | flops | bytes accessed | tf_op | source)
XLA Modules:
  0.0 95.2 jit_solution(8017861974872340431)
XLA Ops:
  0.6 1.5 %pack.1 = (bf16[4,64,256]{2,1,0:T(8,128)(2,1)S(1)}, bf16[4,64,256]{2,1,0:T(8,128)(2,1)S(1)}, bf16[4,64,256]{2,1,0:T(8,128)(2,1)S(1)}, bf16[4,64,256]{2,1,0:T(8,1...) custom-call(bf16[64,2048]{1,0:T(8,128)(2,1)} %refs_0_.1, ...), custom_call_target="tpu_custom_call" | custom-call | tf_op jit(solution)/shard_map/pack/pallas_call | solution.py:93
  2.1 2.0 %collective-permute-start = (bf16[4,64,256]{2,1,0:T(8,128)(2,1)S(1)}, bf16[4,64,256]{2,1,0:T(8,128)(2,1)S(1)}, u32[]{:S(2)}, u32[]{:S(2)}) collective-permute-start(bf16[4,64,256]{2,1,0:T(8,128)(2,1)S(1)} %get-tuple-element.33), channel_id=1, source_target_pairs={{0,1},{1,0},{2,3},{3,2},{4,5},{5,4},{6,7},{7,6},{8,9},{9,8},{10,11... | collective-permute-start | bytes 393224 | tf_op jit(solution)/shard_map/ppermute | solution.py:58
  4.1 4.9 %collective-permute-start.1 = (bf16[4,64,256]{2,1,0:T(8,128)(2,1)S(1)}, bf16[4,64,256]{2,1,0:T(8,128)(2,1)S(1)}, u32[]{:S(2)}, u32[]{:S(2)}) collective-permute-start(bf16[4,64,256]{2,1,0:T(8,128)(2,1)S(1)} %get-tuple-element.34), channel_id=1, source_target_pairs={{0,7},{1,6},{2,5},{3,4},{4,3},{5,2},{6,1},{7,0},{8,15},{9,14},{10,... | collective-permute-start | bytes 393224 | tf_op jit(solution)/shard_map/ppermute | solution.py:58
  9.1 1.9 %collective-permute-start.2 = (bf16[4,64,256]{2,1,0:T(8,128)(2,1)S(1)}, bf16[4,64,256]{2,1,0:T(8,128)(2,1)S(1)}, u32[]{:S(2)}, u32[]{:S(2)}) collective-permute-start(bf16[4,64,256]{2,1,0:T(8,128)(2,1)S(1)} %get-tuple-element.35), channel_id=1, source_target_pairs={{0,3},{1,2},{2,1},{3,0},{4,7},{5,6},{6,5},{7,4},{8,11},{9,10},{10,... | collective-permute-start | bytes 393224 | tf_op jit(solution)/shard_map/ppermute | solution.py:58
  11.0 1.5 %collective-permute-start.3 = (bf16[4,64,256]{2,1,0:T(8,128)(2,1)S(1)}, bf16[4,64,256]{2,1,0:T(8,128)(2,1)S(1)}, u32[]{:S(2)}, u32[]{:S(2)}) collective-permute-start(bf16[4,64,256]{2,1,0:T(8,128)(2,1)S(1)} %get-tuple-element.36), channel_id=1, source_target_pairs={{0,2},{1,3},{2,0},{3,1},{4,6},{5,7},{6,4},{7,5},{8,10},{9,11},{10,... | collective-permute-start | bytes 393224 | tf_op jit(solution)/shard_map/ppermute | solution.py:58
  12.4 0.4 collective-permute-start.4
  12.9 0.0 collective-permute-done.refs_1_
  12.9 4.1 %collective-permute-start.5 = (bf16[4,64,256]{2,1,0:T(8,128)(2,1)S(1)}, bf16[4,64,256]{2,1,0:T(8,128)(2,1)S(1)}, u32[]{:S(2)}, u32[]{:S(2)}) collective-permute-start(bf16[4,64,256]{2,1,0:T(8,128)(2,1)S(1)} %get-tuple-element.38), channel_id=1, source_target_pairs={{0,5},{1,4},{2,7},{3,6},{4,1},{5,0},{6,3},{7,2},{8,13},{9,12},{10,... | collective-permute-start | bytes 393224 | tf_op jit(solution)/shard_map/ppermute | solution.py:58
  17.0 0.0 collective-permute-done.1.refs_2_
  17.0 4.7 %collective-permute-start.6 = (bf16[4,64,256]{2,1,0:T(8,128)(2,1)S(1)}, bf16[4,64,256]{2,1,0:T(8,128)(2,1)S(1)}, u32[]{:S(2)}, u32[]{:S(2)}) collective-permute-start(bf16[4,64,256]{2,1,0:T(8,128)(2,1)S(1)} %get-tuple-element.39), channel_id=1, source_target_pairs={{0,4},{1,5},{2,6},{3,7},{4,0},{5,1},{6,2},{7,3},{8,12},{9,13},{10,... | collective-permute-start | bytes 393224 | tf_op jit(solution)/shard_map/ppermute | solution.py:58
  21.8 0.1 collective-permute-done.2.refs_3_
  21.9 9.4 %collective-permute-done.3.refs_4_ = bf16[4,64,256]{2,1,0:T(8,128)(2,1)S(1)} collective-permute-done((bf16[4,64,256]{2,1,0:T(8,128)(2,1)S(1)}, bf16[4,64,256]{2,1,0:T(8,128)(2,1)S(1)}, u32[]{:S(2)}, u32[]{:S(2)}) %collective-permute-start.3) | collective-permute-done | bytes 131104 | tf_op jit(solution)/shard_map/ppermute | solution.py:58
  31.3 0.0 collective-permute-done.4.refs_5_
  31.3 1.2 %collective-permute-done.5.refs_6_ = bf16[4,64,256]{2,1,0:T(8,128)(2,1)S(1)} collective-permute-done((bf16[4,64,256]{2,1,0:T(8,128)(2,1)S(1)}, bf16[4,64,256]{2,1,0:T(8,128)(2,1)S(1)}, u32[]{:S(2)}, u32[]{:S(2)}) %collective-permute-start.5) | collective-permute-done | bytes 131104 | tf_op jit(solution)/shard_map/ppermute | solution.py:58
  32.4 0.0 collective-permute-done.6.refs_7_
  32.4 0.6 pick_blocks.1
  33.1 2.3 %collective-permute-start.8 = (bf16[4,2,64,256]{3,2,1,0:T(8,128)(2,1)S(1)}, bf16[4,2,64,256]{3,2,1,0:T(8,128)(2,1)S(1)}, u32[]{:S(2)}, u32[]{:S(2)}) collective-permute-start(bf16[4,2,64,256]{3,2,1,0:T(8,128)(2,1)S(1)} %get-tuple-element.40), channel_id=1, source_target_pairs={{8,16},{16,8},{24,32},{32,24},{40,48},{48,40},{56,64},{64,56},{72,... | collective-permute-start | bytes 786440 | tf_op jit(solution)/shard_map/ppermute | solution.py:42
  35.4 1.4 %collective-permute-start.7 = (bf16[4,2,64,256]{3,2,1,0:T(8,128)(2,1)S(1)}, bf16[4,2,64,256]{3,2,1,0:T(8,128)(2,1)S(1)}, u32[]{:S(2)}, u32[]{:S(2)}) collective-permute-start(bf16[4,2,64,256]{3,2,1,0:T(8,128)(2,1)S(1)} %get-tuple-element.40), channel_id=1, source_target_pairs={{0,8},{8,0},{16,24},{24,16},{32,40},{40,32},{48,56},{56,48},{64,72... | collective-permute-start | bytes 786440 | tf_op jit(solution)/shard_map/ppermute | solution.py:42
  36.8 4.5 %collective-permute-start.10 = (bf16[2,2,64,256]{3,2,1,0:T(8,128)(2,1)S(1)}, bf16[2,2,64,256]{3,2,1,0:T(8,128)(2,1)S(1)}, u32[]{:S(2)}, u32[]{:S(2)}) collective-permute-start(bf16[2,2,64,256]{3,2,1,0:T(8,128)(2,1)S(1)} %get-tuple-element.41), channel_id=1, source_target_pairs={{16,32},{32,16},{24,40},{40,24},{48,64},{64,48},{56,72},{72,56},{8... | collective-permute-start | bytes 393224 | tf_op jit(solution)/shard_map/ppermute | solution.py:42
  41.2 0.4 collective-permute-start.9
  41.6 4.6 %collective-permute-done.10.refs_11_ = bf16[2,2,64,256]{3,2,1,0:T(8,128)(2,1)S(1)} collective-permute-done((bf16[2,2,64,256]{3,2,1,0:T(8,128)(2,1)S(1)}, bf16[2,2,64,256]{3,2,1,0:T(8,128)(2,1)S(1)}, u32[]{:S(2)}, u32[]{:S(2)}) %collective-permute-start.10) | collective-permute-done | bytes 131104 | tf_op jit(solution)/shard_map/ppermute | solution.py:42
  46.2 0.3 collective-permute-done.9.refs_10_
  46.5 0.0 collective-permute-done.8.refs_9_
  46.5 0.0 collective-permute-done.7.refs_8_
  46.5 5.1 %attention.1 = (bf16[8,2,64,256]{3,2,1,0:T(8,128)(2,1)S(1)}, f32[8,2,64,256]{3,2,1,0:T(8,128)S(1)}, bf16[4,2,64,256]{3,2,1,0:T(8,128)(2,1)S(1)}, bf16[4,2,64,256...) custom-call(bf16[4,64,256]{2,1,0:T(8,128)(2,1)S(1)} %get-tuple-element.32.refs_0_, ...), custom_call_target="tpu_custom_call" | custom-call | tf_op jit(solution)/shard_map/attention/pallas_call | solution.py:192
  51.6 0.1 collective-permute-start.11
  51.7 4.3 %collective-permute-start.12 = (bf16[4,2,64,256]{3,2,1,0:T(8,128)(2,1)S(1)}, bf16[4,2,64,256]{3,2,1,0:T(8,128)(2,1)S(1)}, u32[]{:S(2)}, u32[]{:S(2)}) collective-permute-start(bf16[4,2,64,256]{3,2,1,0:T(8,128)(2,1)S(1)} %get-tuple-element.45), channel_id=1, source_target_pairs={{8,16},{16,8},{24,32},{32,24},{40,48},{48,40},{56,64},{64,56},{72,... | collective-permute-start | bytes 786440 | tf_op jit(solution)/shard_map/ppermute | solution.py:42
  56.0 0.1 collective-permute-start.13
  56.1 2.7 %collective-permute-start.14 = (bf16[2,2,64,256]{3,2,1,0:T(8,128)(2,1)S(1)}, bf16[2,2,64,256]{3,2,1,0:T(8,128)(2,1)S(1)}, u32[]{:S(2)}, u32[]{:S(2)}) collective-permute-start(bf16[2,2,64,256]{3,2,1,0:T(8,128)(2,1)S(1)} %get-tuple-element.47), channel_id=1, source_target_pairs={{16,32},{32,16},{24,40},{40,24},{48,64},{64,48},{56,72},{72,56},{8... | collective-permute-start | bytes 393224 | tf_op jit(solution)/shard_map/ppermute | solution.py:42
  58.8 3.6 %collective-permute-done.13.a2_ref = bf16[2,2,64,256]{3,2,1,0:T(8,128)(2,1)S(1)} collective-permute-done((bf16[2,2,64,256]{3,2,1,0:T(8,128)(2,1)S(1)}, bf16[2,2,64,256]{3,2,1,0:T(8,128)(2,1)S(1)}, u32[]{:S(2)}, u32[]{:S(2)}) %collective-permute-start.13) | collective-permute-done | bytes 131104 | tf_op jit(solution)/shard_map/ppermute | solution.py:42
  62.4 2.7 %collective-permute-done.14.b2_ref = bf16[2,2,64,256]{3,2,1,0:T(8,128)(2,1)S(1)} collective-permute-done((bf16[2,2,64,256]{3,2,1,0:T(8,128)(2,1)S(1)}, bf16[2,2,64,256]{3,2,1,0:T(8,128)(2,1)S(1)}, u32[]{:S(2)}, u32[]{:S(2)}) %collective-permute-start.14) | collective-permute-done | bytes 131104 | tf_op jit(solution)/shard_map/ppermute | solution.py:42
  65.1 0.0 collective-permute-done.11.a1_ref
  65.1 0.0 collective-permute-done.12.b1_ref
  65.1 0.8 add_returned.1
  65.9 2.9 %collective-permute-start.15 = (bf16[4,64,256]{2,1,0:T(8,128)(2,1)S(1)}, bf16[4,64,256]{2,1,0:T(8,128)(2,1)S(1)}, u32[]{:S(2)}, u32[]{:S(2)}) collective-permute-start(bf16[4,64,256]{2,1,0:T(8,128)(2,1)S(1)} %get-tuple-element.49), channel_id=1, source_target_pairs={{0,1},{1,0},{2,3},{3,2},{4,5},{5,4},{6,7},{7,6},{8,9},{9,8},{10,11... | collective-permute-start | bytes 393224 | tf_op jit(solution)/shard_map/ppermute | solution.py:58
  68.9 2.2 %collective-permute-start.16 = (bf16[4,64,256]{2,1,0:T(8,128)(2,1)S(1)}, bf16[4,64,256]{2,1,0:T(8,128)(2,1)S(1)}, u32[]{:S(2)}, u32[]{:S(2)}) collective-permute-start(bf16[4,64,256]{2,1,0:T(8,128)(2,1)S(1)} %get-tuple-element.50), channel_id=1, source_target_pairs={{0,7},{1,6},{2,5},{3,4},{4,3},{5,2},{6,1},{7,0},{8,15},{9,14},{10,... | collective-permute-start | bytes 393224 | tf_op jit(solution)/shard_map/ppermute | solution.py:58
  71.1 0.4 collective-permute-start.17
  71.5 3.9 %collective-permute-start.18 = (bf16[4,64,256]{2,1,0:T(8,128)(2,1)S(1)}, bf16[4,64,256]{2,1,0:T(8,128)(2,1)S(1)}, u32[]{:S(2)}, u32[]{:S(2)}) collective-permute-start(bf16[4,64,256]{2,1,0:T(8,128)(2,1)S(1)} %get-tuple-element.52), channel_id=1, source_target_pairs={{0,2},{1,3},{2,0},{3,1},{4,6},{5,7},{6,4},{7,5},{8,10},{9,11},{10,... | collective-permute-start | bytes 393224 | tf_op jit(solution)/shard_map/ppermute | solution.py:58
  75.4 0.5 collective-permute-start.19
  75.9 0.0 collective-permute-done.15.refs_1_
  75.9 3.0 %collective-permute-start.20 = (bf16[4,64,256]{2,1,0:T(8,128)(2,1)S(1)}, bf16[4,64,256]{2,1,0:T(8,128)(2,1)S(1)}, u32[]{:S(2)}, u32[]{:S(2)}) collective-permute-start(bf16[4,64,256]{2,1,0:T(8,128)(2,1)S(1)} %get-tuple-element.54), channel_id=1, source_target_pairs={{0,5},{1,4},{2,7},{3,6},{4,1},{5,0},{6,3},{7,2},{8,13},{9,12},{10,... | collective-permute-start | bytes 393224 | tf_op jit(solution)/shard_map/ppermute | solution.py:58
  79.0 0.0 collective-permute-done.16.refs_2_
  79.0 1.8 %collective-permute-start.21 = (bf16[4,64,256]{2,1,0:T(8,128)(2,1)S(1)}, bf16[4,64,256]{2,1,0:T(8,128)(2,1)S(1)}, u32[]{:S(2)}, u32[]{:S(2)}) collective-permute-start(bf16[4,64,256]{2,1,0:T(8,128)(2,1)S(1)} %get-tuple-element.55), channel_id=1, source_target_pairs={{0,4},{1,5},{2,6},{3,7},{4,0},{5,1},{6,2},{7,3},{8,12},{9,13},{10,... | collective-permute-start | bytes 393224 | tf_op jit(solution)/shard_map/ppermute | solution.py:58
  80.8 4.9 %collective-permute-done.17.refs_3_ = bf16[4,64,256]{2,1,0:T(8,128)(2,1)S(1)} collective-permute-done((bf16[4,64,256]{2,1,0:T(8,128)(2,1)S(1)}, bf16[4,64,256]{2,1,0:T(8,128)(2,1)S(1)}, u32[]{:S(2)}, u32[]{:S(2)}) %collective-permute-start.17) | collective-permute-done | bytes 131104 | tf_op jit(solution)/shard_map/ppermute | solution.py:58
  85.7 8.4 %collective-permute-done.18.refs_4_ = bf16[4,64,256]{2,1,0:T(8,128)(2,1)S(1)} collective-permute-done((bf16[4,64,256]{2,1,0:T(8,128)(2,1)S(1)}, bf16[4,64,256]{2,1,0:T(8,128)(2,1)S(1)}, u32[]{:S(2)}, u32[]{:S(2)}) %collective-permute-start.18) | collective-permute-done | bytes 131104 | tf_op jit(solution)/shard_map/ppermute | solution.py:58
  94.1 0.0 collective-permute-done.19.refs_5_
  94.1 0.0 collective-permute-done.21.refs_7_
  94.1 1.1 %unpack.1 = (bf16[64,2048]{1,0:T(8,128)(2,1)}, bf16[64,2048]{1,0:T(8,128)(2,1)}, bf16[64,2048]{1,0:T(8,128)(2,1)}, bf16[64,2048]{1,0:T(8,128)(2,1)}) custom-call(bf16[4,64,256]{2,1,0:T(8,128)(2,1)S(1)} %get-tuple-element.48.refs_0_, bf16[4,64,256]{2,1,0:T(8,128)(2,1)S(1)} %collective-permute-done.15.refs_1_, ...), custom_call_target="tpu_custom_call" | custom-call | tf_op jit(solution)/shard_map/unpack/pallas_call | solution.py:106
  (3 shorter events, 0.0 us)
Async XLA Ops:
  2.1 10.8 %collective-permute-start = (bf16[4,64,256]{2,1,0:T(8,128)(2,1)S(1)}, bf16[4,64,256]{2,1,0:T(8,128)(2,1)S(1)}, u32[]{:S(2)}, u32[]{:S(2)}) collective-permute-start(bf16[4,64,256]{2,1,0:T(8,128)(2,1)S(1)} %get-tuple-element.33), channel_id=1, source_target_pairs={{0,1},{1,0},{2,3},{3,2},{4,5},{5,4},{6,7},{7,6},{8,9},{9,8},{10,11... | collective-permute-start | bytes 393224 | tf_op jit(solution)/shard_map/ppermute | solution.py:58
  4.1 12.9 %collective-permute-start.1 = (bf16[4,64,256]{2,1,0:T(8,128)(2,1)S(1)}, bf16[4,64,256]{2,1,0:T(8,128)(2,1)S(1)}, u32[]{:S(2)}, u32[]{:S(2)}) collective-permute-start(bf16[4,64,256]{2,1,0:T(8,128)(2,1)S(1)} %get-tuple-element.34), channel_id=1, source_target_pairs={{0,7},{1,6},{2,5},{3,4},{4,3},{5,2},{6,1},{7,0},{8,15},{9,14},{10,... | collective-permute-start | bytes 393224 | tf_op jit(solution)/shard_map/ppermute | solution.py:58
  9.1 12.8 %collective-permute-start.2 = (bf16[4,64,256]{2,1,0:T(8,128)(2,1)S(1)}, bf16[4,64,256]{2,1,0:T(8,128)(2,1)S(1)}, u32[]{:S(2)}, u32[]{:S(2)}) collective-permute-start(bf16[4,64,256]{2,1,0:T(8,128)(2,1)S(1)} %get-tuple-element.35), channel_id=1, source_target_pairs={{0,3},{1,2},{2,1},{3,0},{4,7},{5,6},{6,5},{7,4},{8,11},{9,10},{10,... | collective-permute-start | bytes 393224 | tf_op jit(solution)/shard_map/ppermute | solution.py:58
  11.0 20.3 %collective-permute-start.3 = (bf16[4,64,256]{2,1,0:T(8,128)(2,1)S(1)}, bf16[4,64,256]{2,1,0:T(8,128)(2,1)S(1)}, u32[]{:S(2)}, u32[]{:S(2)}) collective-permute-start(bf16[4,64,256]{2,1,0:T(8,128)(2,1)S(1)} %get-tuple-element.36), channel_id=1, source_target_pairs={{0,2},{1,3},{2,0},{3,1},{4,6},{5,7},{6,4},{7,5},{8,10},{9,11},{10,... | collective-permute-start | bytes 393224 | tf_op jit(solution)/shard_map/ppermute | solution.py:58
  12.4 18.8 %collective-permute-start.4 = (bf16[4,64,256]{2,1,0:T(8,128)(2,1)S(1)}, bf16[4,64,256]{2,1,0:T(8,128)(2,1)S(1)}, u32[]{:S(2)}, u32[]{:S(2)}) collective-permute-start(bf16[4,64,256]{2,1,0:T(8,128)(2,1)S(1)} %get-tuple-element.37), channel_id=1, source_target_pairs={{0,6},{1,7},{2,4},{3,5},{4,2},{5,3},{6,0},{7,1},{8,14},{9,15},{10,... | collective-permute-start | bytes 393224 | tf_op jit(solution)/shard_map/ppermute | solution.py:58
  12.9 19.5 %collective-permute-start.5 = (bf16[4,64,256]{2,1,0:T(8,128)(2,1)S(1)}, bf16[4,64,256]{2,1,0:T(8,128)(2,1)S(1)}, u32[]{:S(2)}, u32[]{:S(2)}) collective-permute-start(bf16[4,64,256]{2,1,0:T(8,128)(2,1)S(1)} %get-tuple-element.38), channel_id=1, source_target_pairs={{0,5},{1,4},{2,7},{3,6},{4,1},{5,0},{6,3},{7,2},{8,13},{9,12},{10,... | collective-permute-start | bytes 393224 | tf_op jit(solution)/shard_map/ppermute | solution.py:58
  17.0 15.4 %copy-start = (s32[32,4]{0,1:T(4,128)S(1)}, s32[32,4]{0,1:T(4,128)}, u32[]{:S(2)}) copy-start(s32[32,4]{0,1:T(4,128)} %param.9) | copy-start | bytes 1540
  17.0 15.4 %collective-permute-start.6 = (bf16[4,64,256]{2,1,0:T(8,128)(2,1)S(1)}, bf16[4,64,256]{2,1,0:T(8,128)(2,1)S(1)}, u32[]{:S(2)}, u32[]{:S(2)}) collective-permute-start(bf16[4,64,256]{2,1,0:T(8,128)(2,1)S(1)} %get-tuple-element.39), channel_id=1, source_target_pairs={{0,4},{1,5},{2,6},{3,7},{4,0},{5,1},{6,2},{7,3},{8,12},{9,13},{10,... | collective-permute-start | bytes 393224 | tf_op jit(solution)/shard_map/ppermute | solution.py:58
  33.1 13.4 %collective-permute-start.8 = (bf16[4,2,64,256]{3,2,1,0:T(8,128)(2,1)S(1)}, bf16[4,2,64,256]{3,2,1,0:T(8,128)(2,1)S(1)}, u32[]{:S(2)}, u32[]{:S(2)}) collective-permute-start(bf16[4,2,64,256]{3,2,1,0:T(8,128)(2,1)S(1)} %get-tuple-element.40), channel_id=1, source_target_pairs={{8,16},{16,8},{24,32},{32,24},{40,48},{48,40},{56,64},{64,56},{72,... | collective-permute-start | bytes 786440 | tf_op jit(solution)/shard_map/ppermute | solution.py:42
  35.4 11.1 %collective-permute-start.7 = (bf16[4,2,64,256]{3,2,1,0:T(8,128)(2,1)S(1)}, bf16[4,2,64,256]{3,2,1,0:T(8,128)(2,1)S(1)}, u32[]{:S(2)}, u32[]{:S(2)}) collective-permute-start(bf16[4,2,64,256]{3,2,1,0:T(8,128)(2,1)S(1)} %get-tuple-element.40), channel_id=1, source_target_pairs={{0,8},{8,0},{16,24},{24,16},{32,40},{40,32},{48,56},{56,48},{64,72... | collective-permute-start | bytes 786440 | tf_op jit(solution)/shard_map/ppermute | solution.py:42
  36.8 9.4 %collective-permute-start.10 = (bf16[2,2,64,256]{3,2,1,0:T(8,128)(2,1)S(1)}, bf16[2,2,64,256]{3,2,1,0:T(8,128)(2,1)S(1)}, u32[]{:S(2)}, u32[]{:S(2)}) collective-permute-start(bf16[2,2,64,256]{3,2,1,0:T(8,128)(2,1)S(1)} %get-tuple-element.41), channel_id=1, source_target_pairs={{16,32},{32,16},{24,40},{40,24},{48,64},{64,48},{56,72},{72,56},{8... | collective-permute-start | bytes 393224 | tf_op jit(solution)/shard_map/ppermute | solution.py:42
  41.2 5.2 %collective-permute-start.9 = (bf16[2,2,64,256]{3,2,1,0:T(8,128)(2,1)S(1)}, bf16[2,2,64,256]{3,2,1,0:T(8,128)(2,1)S(1)}, u32[]{:S(2)}, u32[]{:S(2)}) collective-permute-start(bf16[2,2,64,256]{3,2,1,0:T(8,128)(2,1)S(1)} %get-tuple-element.41), channel_id=1, source_target_pairs={{0,16},{16,0},{8,24},{24,8},{32,48},{48,32},{40,56},{56,40},{64,80... | collective-permute-start | bytes 393224 | tf_op jit(solution)/shard_map/ppermute | solution.py:42
  51.6 13.5 %collective-permute-start.11 = (bf16[4,2,64,256]{3,2,1,0:T(8,128)(2,1)S(1)}, bf16[4,2,64,256]{3,2,1,0:T(8,128)(2,1)S(1)}, u32[]{:S(2)}, u32[]{:S(2)}) collective-permute-start(bf16[4,2,64,256]{3,2,1,0:T(8,128)(2,1)S(1)} %get-tuple-element.44), channel_id=1, source_target_pairs={{0,8},{8,0},{16,24},{24,16},{32,40},{40,32},{48,56},{56,48},{64,72... | collective-permute-start | bytes 786440 | tf_op jit(solution)/shard_map/ppermute | solution.py:42
  51.7 13.4 %collective-permute-start.12 = (bf16[4,2,64,256]{3,2,1,0:T(8,128)(2,1)S(1)}, bf16[4,2,64,256]{3,2,1,0:T(8,128)(2,1)S(1)}, u32[]{:S(2)}, u32[]{:S(2)}) collective-permute-start(bf16[4,2,64,256]{3,2,1,0:T(8,128)(2,1)S(1)} %get-tuple-element.45), channel_id=1, source_target_pairs={{8,16},{16,8},{24,32},{32,24},{40,48},{48,40},{56,64},{64,56},{72,... | collective-permute-start | bytes 786440 | tf_op jit(solution)/shard_map/ppermute | solution.py:42
  56.0 6.4 %collective-permute-start.13 = (bf16[2,2,64,256]{3,2,1,0:T(8,128)(2,1)S(1)}, bf16[2,2,64,256]{3,2,1,0:T(8,128)(2,1)S(1)}, u32[]{:S(2)}, u32[]{:S(2)}) collective-permute-start(bf16[2,2,64,256]{3,2,1,0:T(8,128)(2,1)S(1)} %get-tuple-element.46), channel_id=1, source_target_pairs={{0,16},{16,0},{8,24},{24,8},{32,48},{48,32},{40,56},{56,40},{64,80... | collective-permute-start | bytes 393224 | tf_op jit(solution)/shard_map/ppermute | solution.py:42
  56.1 9.0 %collective-permute-start.14 = (bf16[2,2,64,256]{3,2,1,0:T(8,128)(2,1)S(1)}, bf16[2,2,64,256]{3,2,1,0:T(8,128)(2,1)S(1)}, u32[]{:S(2)}, u32[]{:S(2)}) collective-permute-start(bf16[2,2,64,256]{3,2,1,0:T(8,128)(2,1)S(1)} %get-tuple-element.47), channel_id=1, source_target_pairs={{16,32},{32,16},{24,40},{40,24},{48,64},{64,48},{56,72},{72,56},{8... | collective-permute-start | bytes 393224 | tf_op jit(solution)/shard_map/ppermute | solution.py:42
  65.9 10.0 %collective-permute-start.15 = (bf16[4,64,256]{2,1,0:T(8,128)(2,1)S(1)}, bf16[4,64,256]{2,1,0:T(8,128)(2,1)S(1)}, u32[]{:S(2)}, u32[]{:S(2)}) collective-permute-start(bf16[4,64,256]{2,1,0:T(8,128)(2,1)S(1)} %get-tuple-element.49), channel_id=1, source_target_pairs={{0,1},{1,0},{2,3},{3,2},{4,5},{5,4},{6,7},{7,6},{8,9},{9,8},{10,11... | collective-permute-start | bytes 393224 | tf_op jit(solution)/shard_map/ppermute | solution.py:58
  68.9 10.1 %collective-permute-start.16 = (bf16[4,64,256]{2,1,0:T(8,128)(2,1)S(1)}, bf16[4,64,256]{2,1,0:T(8,128)(2,1)S(1)}, u32[]{:S(2)}, u32[]{:S(2)}) collective-permute-start(bf16[4,64,256]{2,1,0:T(8,128)(2,1)S(1)} %get-tuple-element.50), channel_id=1, source_target_pairs={{0,7},{1,6},{2,5},{3,4},{4,3},{5,2},{6,1},{7,0},{8,15},{9,14},{10,... | collective-permute-start | bytes 393224 | tf_op jit(solution)/shard_map/ppermute | solution.py:58
  71.1 14.6 %collective-permute-start.17 = (bf16[4,64,256]{2,1,0:T(8,128)(2,1)S(1)}, bf16[4,64,256]{2,1,0:T(8,128)(2,1)S(1)}, u32[]{:S(2)}, u32[]{:S(2)}) collective-permute-start(bf16[4,64,256]{2,1,0:T(8,128)(2,1)S(1)} %get-tuple-element.51), channel_id=1, source_target_pairs={{0,3},{1,2},{2,1},{3,0},{4,7},{5,6},{6,5},{7,4},{8,11},{9,10},{10,... | collective-permute-start | bytes 393224 | tf_op jit(solution)/shard_map/ppermute | solution.py:58
  71.5 22.7 %collective-permute-start.18 = (bf16[4,64,256]{2,1,0:T(8,128)(2,1)S(1)}, bf16[4,64,256]{2,1,0:T(8,128)(2,1)S(1)}, u32[]{:S(2)}, u32[]{:S(2)}) collective-permute-start(bf16[4,64,256]{2,1,0:T(8,128)(2,1)S(1)} %get-tuple-element.52), channel_id=1, source_target_pairs={{0,2},{1,3},{2,0},{3,1},{4,6},{5,7},{6,4},{7,5},{8,10},{9,11},{10,... | collective-permute-start | bytes 393224 | tf_op jit(solution)/shard_map/ppermute | solution.py:58
  75.4 18.7 %collective-permute-start.19 = (bf16[4,64,256]{2,1,0:T(8,128)(2,1)S(1)}, bf16[4,64,256]{2,1,0:T(8,128)(2,1)S(1)}, u32[]{:S(2)}, u32[]{:S(2)}) collective-permute-start(bf16[4,64,256]{2,1,0:T(8,128)(2,1)S(1)} %get-tuple-element.53), channel_id=1, source_target_pairs={{0,6},{1,7},{2,4},{3,5},{4,2},{5,3},{6,0},{7,1},{8,14},{9,15},{10,... | collective-permute-start | bytes 393224 | tf_op jit(solution)/shard_map/ppermute | solution.py:58
  75.9 18.2 %collective-permute-start.20 = (bf16[4,64,256]{2,1,0:T(8,128)(2,1)S(1)}, bf16[4,64,256]{2,1,0:T(8,128)(2,1)S(1)}, u32[]{:S(2)}, u32[]{:S(2)}) collective-permute-start(bf16[4,64,256]{2,1,0:T(8,128)(2,1)S(1)} %get-tuple-element.54), channel_id=1, source_target_pairs={{0,5},{1,4},{2,7},{3,6},{4,1},{5,0},{6,3},{7,2},{8,13},{9,12},{10,... | collective-permute-start | bytes 393224 | tf_op jit(solution)/shard_map/ppermute | solution.py:58
  79.0 15.2 %collective-permute-start.21 = (bf16[4,64,256]{2,1,0:T(8,128)(2,1)S(1)}, bf16[4,64,256]{2,1,0:T(8,128)(2,1)S(1)}, u32[]{:S(2)}, u32[]{:S(2)}) collective-permute-start(bf16[4,64,256]{2,1,0:T(8,128)(2,1)S(1)} %get-tuple-element.55), channel_id=1, source_target_pairs={{0,4},{1,5},{2,6},{3,7},{4,0},{5,1},{6,2},{7,3},{8,12},{9,13},{10,... | collective-permute-start | bytes 393224 | tf_op jit(solution)/shard_map/ppermute | solution.py:58

commit v3 on v2

v3 whole, which is shorter than its diff:
```python
import functools
import math

import jax
import jax.numpy as jnp
from jax import lax
from jax.experimental import pallas as pl
from jax.experimental.pallas import tpu as pltpu
from jax.sharding import PartitionSpec as P

HD = 128
BLK = 128
BF16 = jnp.bfloat16
F32 = jnp.float32
SCALE = 1.0 / math.sqrt(HD)
LOG2E = 1.0 / math.log(2.0)
MIB = 1024 * 1024
SHIFTS = (0, 1, 7, 2, 6, 3, 5, 4)

VM = pl.BlockSpec(memory_space=pltpu.VMEM)
SM = pl.BlockSpec(memory_space=pltpu.SMEM)


def call(body, out_shape, in_specs, out_specs, name, mib, scratch_shapes=()):
    return pl.pallas_call(
        body,
        out_shape=out_shape,
        in_specs=in_specs,
        out_specs=out_specs,
        scratch_shapes=scratch_shapes,
        name=name,
        compiler_params=pltpu.CompilerParams(vmem_limit_bytes=mib * MIB),
    )


def swapped(array, distance, start):
    length = lax.axis_size("frame")
    pairs = []
    for first in range(start, length, 2 * distance):
        for low in range(first, min(first + distance, length - distance)):
            pairs += [(low, low + distance), (low + distance, low)]
    return lax.ppermute(array, "frame", pairs)


SWAPS = ((1, 0), (1, 1), (2, 0), (2, 2))


def has_partner(frame, length, distance, start):
    shifted = frame + (2 * distance - start)
    lower_half = lax.rem(shifted, 2 * distance) < distance
    partner = jnp.where(lower_half, frame + distance, frame - distance)
    return jnp.logical_and(jnp.logical_and(partner >= 0, partner < length), frame >= 0)


def head_shifts(pieces, sign):
    length = lax.axis_size("head")
    arrived = []
    for piece, by in zip(pieces, SHIFTS):
        if by:
            flat = piece.reshape(-1, piece.shape[-1])
            flat = lax.ppermute(flat, "head", [(i, (i + sign * by) % length) for i in range(length)])
            piece = flat.reshape(piece.shape)
        arrived.append(piece)
    return arrived


def place_above(slot):
    length = lax.axis_size("head")
    return lax.rem(lax.axis_index("head") + SHIFTS[slot], length)


def place_below(slot):
    length = lax.axis_size("head")
    return lax.rem(lax.axis_index("head") + (length - SHIFTS[slot]), length)


def columns_of(slot, piece):
    return pl.ds(pl.multiple_of(place_above(slot) * piece, piece), piece)


def pack(arrays, parts):
    rows, width = arrays[0].shape
    count = len(arrays)
    piece = width // parts

    def body(*refs):
        in_refs, out_refs, sem = refs[:count], refs[count:-1], refs[-1]
        copies = []
        for k, out_ref in enumerate(out_refs):
            for i, ref in enumerate(in_refs):
                copies.append(
                    pltpu.make_async_copy(ref.at[:, columns_of(k, piece)], out_ref.at[i], sem.at[k, i])
                )
        for copy in copies:
            copy.start()
        for copy in copies:
            copy.wait()

    shape = jax.ShapeDtypeStruct((count, rows, piece), arrays[0].dtype)
    anywhere = pl.BlockSpec(memory_space=pltpu.HBM)
    arrays = [pltpu.with_memory_space_constraint(array, pltpu.HBM) for array in arrays]
    sems = [pltpu.SemaphoreType.DMA((parts, count))]
    return call(body, [shape] * parts, [anywhere] * count, [VM] * parts, "pack", 4, sems)(*arrays)


def unpack(pieces):
    parts = len(pieces)
    count, rows, piece = pieces[0].shape

    def body(*refs):
        for i, ref in enumerate(refs[parts:]):
            for k in range(parts):
                ref[:, columns_of(k, piece)] = refs[k][i]

    shape = jax.ShapeDtypeStruct((rows, parts * piece), pieces[0].dtype)
    return call(body, [shape] * count, [VM] * parts, [VM] * count, "unpack", 8)(*pieces)


def pick_blocks(block_order, pieces):
    parts = len(pieces)
    _, rows, width = pieces[0].shape
    per = BLK // rows

    def body(order_ref, *refs):
        near_ref, far_ref, all_ref = refs[parts:]
        frame = lax.axis_index("frame")
        for k in range(parts):
            all_ref[place_below(k)] = refs[k][0:2]
        for rank in range(2):
            start = order_ref[rank, frame] * per
            for i in range(per):
                taken = all_ref[start + i]
                near_ref[rank * per + i] = taken
                if rank == 0:
                    far_ref[i] = taken

    near = jax.ShapeDtypeStruct((2 * per, 2, rows, width), BF16)
    far = jax.ShapeDtypeStruct((per, 2, rows, width), BF16)
    scratch = [pltpu.VMEM((parts, 2, rows, width), BF16)]
    return call(
        body, [near, far], [SM] + [VM] * parts, [VM, VM], "pick_blocks", 8, scratch
    )(block_order, *pieces)


def dot(a, b, contract):
    return lax.dot_general(a, b, ((contract[:1], contract[1:]), ((), ())), preferred_element_type=F32)


def columns(head):
    return slice(head * HD, (head + 1) * HD)


def rows_of(refs, i, head):
    return jnp.concatenate([ref[i, :, columns(head)] for ref in refs], axis=0)


def own_scores_body(*refs):
    piece_refs, (power_ref, weight_grad_ref, stats_ref) = refs[:-3], refs[-3:]
    for head in range(piece_refs[0].shape[-1] // HD):
        key, value, query, grad = [rows_of(piece_refs, i, head) for i in range(4)]
        scores = dot(key, query, (1, 1)) * (SCALE * LOG2E)
        weight_grad = dot(value, grad, (1, 1))
        peak = jnp.max(scores, axis=0, keepdims=True)
        power = jnp.exp2(scores - peak)
        power_ref[head] = power
        weight_grad_ref[head] = weight_grad
        stats_ref[head, 0:1] = peak
        stats_ref[head, 1:2] = jnp.sum(power, axis=0, keepdims=True)
        stats_ref[head, 2:3] = jnp.sum(power * weight_grad, axis=0, keepdims=True)


def own_scores(pieces):
    tokens = len(pieces) * pieces[0].shape[1]
    heads = pieces[0].shape[-1] // HD
    square = jax.ShapeDtypeStruct((heads, tokens, tokens), F32)
    stats = jax.ShapeDtypeStruct((heads, 8, tokens), F32)
    return call(
        own_scores_body, [square, square, stats], [VM] * len(pieces), [VM] * 3, "own_scores", 16
    )(*pieces)


def remote_part_body(frame_count, parts, *refs):
    piece_refs, panel_refs, stats_ref = refs[:parts], refs[parts : parts + 4], refs[parts + 4]
    joint_ref, *rest = refs[parts + 5 :]
    target_refs, low_refs, score_grad_refs = rest[:4], rest[4:8], rest[8:]
    frame = lax.axis_index("frame")
    rows = piece_refs[0].shape[1]
    heads = range(piece_refs[0].shape[-1] // HD)
    hidden = [
        jnp.where(has_partner(frame, frame_count, *swap), 0.0, -jnp.inf).astype(F32) for swap in SWAPS
    ]
    queries = [rows_of(piece_refs, 2, head) for head in heads]
    grads = [rows_of(piece_refs, 3, head) for head in heads]
    scores = [
        [
            dot(ref[:, 0, :, columns(head)].reshape(-1, HD), queries[head], (1, 1)) * (SCALE * LOG2E) + bias
            for ref, bias in zip(panel_refs, hidden)
        ]
        for head in heads
    ]
    weight_grads = [
        [dot(ref[:, 1, :, columns(head)].reshape(-1, HD), grads[head], (1, 1)) for ref in panel_refs]
        for head in heads
    ]
    for head in heads:
        own_peak = stats_ref[head, 0:1]
        peaks = [jnp.max(s, axis=0, keepdims=True) for s in scores[head]]
        peak = functools.reduce(jnp.maximum, peaks, own_peak)
        powers = [jnp.exp2(s - peak) for s in scores[head]]
        rescale = jnp.exp2(own_peak - peak)
        total = functools.reduce(
            jnp.add, [jnp.sum(p, axis=0, keepdims=True) for p in powers], stats_ref[head, 1:2] * rescale
        )
        moment = functools.reduce(
            jnp.add,
            [jnp.sum(p * g, axis=0, keepdims=True) for p, g in zip(powers, weight_grads[head])],
            stats_ref[head, 2:3] * rescale,
        )
        inverse = 1.0 / total
        delta = moment * inverse
        joint_ref[head, 0:1] = rescale * inverse
        joint_ref[head, 1:2] = delta
        for power, weight_grad, low_ref, score_grad_ref in zip(
            powers, weight_grads[head], low_refs, score_grad_refs
        ):
            weights = power * inverse
            low_ref[head] = weights.astype(BF16)
            score_grad_ref[head] = (weights * (weight_grad - delta)).astype(BF16)
    for head in heads:
        cols = columns(head)
        for target, low_ref, score_grad_ref in zip(target_refs, low_refs, score_grad_refs):
            key_part = dot(score_grad_ref[head], queries[head], (1, 0)) * SCALE
            value_part = dot(low_ref[head], grads[head], (1, 0))
            target[:, 0, :, cols] = key_part.astype(BF16).reshape(-1, rows, HD)
            target[:, 1, :, cols] = value_part.astype(BF16).reshape(-1, rows, HD)


def remote_part(pieces, panels, stats):
    parts = len(pieces)
    _, rows, width = pieces[0].shape
    shape = jax.ShapeDtypeStruct
    squares = [shape((width // HD, p.shape[0] * rows, parts * rows), BF16) for p in panels]
    outs = [shape(stats.shape, F32)] + [shape(p.shape, BF16) for p in panels] + squares + squares
    body = functools.partial(remote_part_body, lax.axis_size("frame"), parts)
    outs = call(body, outs, [VM] * (parts + 5), [VM] * 13, "remote_part", 24)(*pieces, *panels, stats)
    return outs[0], outs[1:5], outs[5:9], outs[9:]


def own_grads_body(parts, *refs):
    piece_refs, panel_refs, refs = refs[:parts], refs[parts : parts + 4], refs[parts + 4 :]
    power_ref, weight_grad_ref, joint_ref = refs[:3]
    low_refs, score_grad_refs, (first_ref, own_ref) = refs[3:7], refs[7:11], refs[11:]
    _, rows, width = piece_refs[0].shape
    for head in range(width // HD):
        cols = columns(head)
        key, value, query, grad = [rows_of(piece_refs, i, head) for i in range(4)]
        weights = power_ref[head] * joint_ref[head, 0:1]
        score_grad = (weights * (weight_grad_ref[head] - joint_ref[head, 1:2])).astype(BF16)
        low = weights.astype(BF16)
        own_ref[:, 0, :, cols] = (dot(score_grad, query, (1, 0)) * SCALE).reshape(parts, rows, HD)
        own_ref[:, 1, :, cols] = dot(low, grad, (1, 0)).reshape(parts, rows, HD)
        query_t = dot(key, score_grad, (0, 0))
        out_t = dot(value, low, (0, 0))
        for panel_ref, low_ref, score_grad_ref in zip(panel_refs, low_refs, score_grad_refs):
            query_t = query_t + dot(panel_ref[:, 0, :, cols].reshape(-1, HD), score_grad_ref[head], (0, 0))
            out_t = out_t + dot(panel_ref[:, 1, :, cols].reshape(-1, HD), low_ref[head], (0, 0))
        attended = out_t.T.astype(BF16)
        query_grad = (query_t * SCALE).T.astype(BF16)
        for slot in range(parts):
            first_ref[slot, 0, :, cols] = attended[slot * rows : (slot + 1) * rows]
            first_ref[slot, 1, :, cols] = query_grad[slot * rows : (slot + 1) * rows]


def own_grads(pieces, panels, power, weight_grad, joint, lows, score_grads):
    parts = len(pieces)
    _, rows, width = pieces[0].shape
    two = (parts, 2, rows, width)
    outs = [jax.ShapeDtypeStruct(two, BF16), jax.ShapeDtypeStruct(two, F32)]
    body = functools.partial(own_grads_body, parts)
    return call(body, outs, [VM] * (parts + 15), [VM] * 2, "own_grads", 16)(
        *pieces, *panels, power, weight_grad, joint, *lows, *score_grads
    )


def add_returned(block_order, first, own, returned):
    parts, _, rows, width = own.shape
    per = BLK // rows

    def body(order_ref, first_ref, own_ref, a1_ref, b1_ref, a2_ref, b2_ref, *refs):
        out_refs, sum_ref = refs[:parts], refs[parts]
        frame = lax.axis_index("frame")
        for k in range(parts):
            sum_ref[place_below(k)] = own_ref[k]
        for rank in range(2):
            start = order_ref[rank, frame] * per
            for i in range(per):
                at = rank * per + i
                term = a1_ref[at].astype(F32) + b1_ref[at].astype(F32)
                if rank == 0:
                    term = term + (a2_ref[i].astype(F32) + b2_ref[i].astype(F32))
                sum_ref[start + i] = sum_ref[start + i] + term
        for k in range(parts):
            out_refs[k][0:2] = sum_ref[place_below(k)].astype(BF16)
            out_refs[k][2:4] = first_ref[k]

    shape = jax.ShapeDtypeStruct((4, rows, width), BF16)
    scratch = [pltpu.VMEM(own.shape, F32)]
    return call(
        body, [shape] * parts, [SM] + [VM] * 6, [VM] * parts, "add_returned", 10, scratch
    )(block_order, first, own, *returned)


def local(query_rows, key_rows, value_rows, out_grad, block_order):
    parts = lax.axis_size("head")
    block_order = pltpu.with_memory_space_constraint(block_order.T, pltpu.HBM)
    arrived = head_shifts(pack((key_rows, value_rows, query_rows, out_grad), parts), 1)
    near, far = pick_blocks(block_order, arrived)
    panels = [swapped(far if swap[0] == 2 else near, *swap) for swap in SWAPS]
    power, weight_grad, stats = own_scores(arrived)
    joint, parts_of_others, lows, score_grads = remote_part(arrived, panels, stats)
    returned = [swapped(part, *swap) for part, swap in zip(parts_of_others, SWAPS)]
    first, own = own_grads(arrived, panels, power, weight_grad, joint, lows, score_grads)
    leaving = add_returned(block_order, first, own, returned)
    key_grad, value_grad, attended, query_grad = unpack(head_shifts(leaving, -1))
    return (attended, query_grad, key_grad, value_grad)


def solution(mesh):
    rows = P(("frame", "head"), None)
    return jax.shard_map(
        local,
        mesh=mesh,
        in_specs=(rows, rows, rows, rows, P()),
        out_specs=(rows, rows, rows, rows),
        check_vma=False,
    )
```

time: 96.9 us -> 92.5 us (0.955)
  waiting for transfers between devices: 35.2 us -> 32.5 us
  starting transfers between devices: 50.1 us -> 48.1 us
    ppermute x8, waiting for transfers between devices: 11.1 us -> 8.64 us  [swapped(): return lax.ppermute(array, 'frame', pairs)]
    ppermute x14, starting transfers between devices: 34.5 us -> 32.4 us  [head_shifts(): lax.ppermute(flat, 'head', [(i, (i + sign * by) % length) for i in range(...]
    pallas_call x1 -> x3, Pallas kernels: 5.12 us -> 5.53 us  [the longest x1 3.02 us: remote_part(): call(body, outs, [VM] * (parts + 5), [VM] * 13, 'remote_part', 24)]
  transfers between devices with their start and end apart: 22 -> 22, of which waited for: 9 -> 12; matrix products, arithmetic and copies ran while one was open for 0% -> 0% of each run, Pallas kernels for 0% -> 3%
where the time goes in v3:
time: 92.5 us; the launch traced here: 91.2 us
  starting transfers between devices  48.1 us (52%)
  waiting for transfers between devices  32.5 us (35%)
  Pallas kernels  9.83 us (11%)
    ppermute x14, starting transfers between devices, head_shifts(): lax.ppermute(flat, 'head', [(i, (i + sign * by) % length) for i in range(...  32.4 us
    ppermute x14, waiting for transfers between devices, head_shifts(): lax.ppermute(flat, 'head', [(i, (i + sign * by) % length) for i in range(...  23.8 us
    ppermute x8, starting transfers between devices, swapped(): return lax.ppermute(array, 'frame', pairs)  15.7 us
    ppermute x8, waiting for transfers between devices, swapped(): return lax.ppermute(array, 'frame', pairs)  8.64 us
    pallas_call x1, Pallas kernels, remote_part(): call(body, outs, [VM] * (parts + 5), [VM] * 13, 'remote_part', 24)  3.02 us
  transfers between devices with their start and end apart: 22, of which 12 were waited for; matrix products, arithmetic and copies ran while one was open for 0% of the time, Pallas kernels for 3%

profile of v3, /device:TPU:4, one launch (start us, length us, event | category | flops | bytes accessed | tf_op | source)
XLA Modules:
  0.0 91.2 jit_solution(5172314827880405477)
XLA Ops:
  0.6 1.5 %pack.1 = (bf16[4,64,256]{2,1,0:T(8,128)(2,1)S(1)}, bf16[4,64,256]{2,1,0:T(8,128)(2,1)S(1)}, bf16[4,64,256]{2,1,0:T(8,128)(2,1)S(1)}, bf16[4,64,256]{2,1,0:T(8,1...) custom-call(bf16[64,2048]{1,0:T(8,128)(2,1)} %refs_0_.1, ...), custom_call_target="tpu_custom_call" | custom-call | tf_op jit(solution)/shard_map/pack/pallas_call | solution.py:103
  2.1 5.9 %collective-permute-start.1 = (bf16[256,256]{1,0:T(8,128)(2,1)S(1)}, bf16[256,256]{1,0:T(8,128)(2,1)S(1)}, u32[]{:S(2)}, u32[]{:S(2)}) collective-permute-start(bf16[256,256]{1,0:T(8,128)(2,1)S(1)} %bitcast.77), channel_id=1, source_target_pairs={{0,7},{1,0},{2,1},{3,2},{4,3},{5,4},{6,5},{7,6},{8,15},{9,8},{10,9... | collective-permute-start | bytes 393224 | tf_op jit(solution)/shard_map/ppermute | solution.py:61
  8.1 4.1 %collective-permute-start.3 = (bf16[256,256]{1,0:T(8,128)(2,1)S(1)}, bf16[256,256]{1,0:T(8,128)(2,1)S(1)}, u32[]{:S(2)}, u32[]{:S(2)}) collective-permute-start(bf16[256,256]{1,0:T(8,128)(2,1)S(1)} %bitcast.72), channel_id=1, source_target_pairs={{0,6},{1,7},{2,0},{3,1},{4,2},{5,3},{6,4},{7,5},{8,14},{9,15},{10,... | collective-permute-start | bytes 393224 | tf_op jit(solution)/shard_map/ppermute | solution.py:61
  12.2 0.8 collective-permute-start.4
  13.0 0.0 collective-permute-done.1
  13.0 4.2 %collective-permute-start.5 = (bf16[256,256]{1,0:T(8,128)(2,1)S(1)}, bf16[256,256]{1,0:T(8,128)(2,1)S(1)}, u32[]{:S(2)}, u32[]{:S(2)}) collective-permute-start(bf16[256,256]{1,0:T(8,128)(2,1)S(1)} %bitcast.68), channel_id=1, source_target_pairs={{0,5},{1,6},{2,7},{3,0},{4,1},{5,2},{6,3},{7,4},{8,13},{9,14},{10,... | collective-permute-start | bytes 393224 | tf_op jit(solution)/shard_map/ppermute | solution.py:61
  17.2 0.5 collective-permute-done
  17.7 2.8 %collective-permute-start.6 = (bf16[256,256]{1,0:T(8,128)(2,1)S(1)}, bf16[256,256]{1,0:T(8,128)(2,1)S(1)}, u32[]{:S(2)}, u32[]{:S(2)}) collective-permute-start(bf16[256,256]{1,0:T(8,128)(2,1)S(1)} %bitcast.66), channel_id=1, source_target_pairs={{0,4},{1,5},{2,6},{3,7},{4,0},{5,1},{6,2},{7,3},{8,12},{9,13},{10,... | collective-permute-start | bytes 393224 | tf_op jit(solution)/shard_map/ppermute | solution.py:61
  20.6 1.1 %collective-permute-done.2 = bf16[256,256]{1,0:T(8,128)(2,1)S(1)} collective-permute-done((bf16[256,256]{1,0:T(8,128)(2,1)S(1)}, bf16[256,256]{1,0:T(8,128)(2,1)S(1)}, u32[]{:S(2)}, u32[]{:S(2)}) %collective-permute-start.2) | collective-permute-done | bytes 131104 | tf_op jit(solution)/shard_map/ppermute | solution.py:61
  21.7 0.0 collective-permute-done.3
  21.7 7.8 %collective-permute-done.4 = bf16[256,256]{1,0:T(8,128)(2,1)S(1)} collective-permute-done((bf16[256,256]{1,0:T(8,128)(2,1)S(1)}, bf16[256,256]{1,0:T(8,128)(2,1)S(1)}, u32[]{:S(2)}, u32[]{:S(2)}) %collective-permute-start.4) | collective-permute-done | bytes 131104 | tf_op jit(solution)/shard_map/ppermute | solution.py:61
  29.5 1.8 %collective-permute-done.5 = bf16[256,256]{1,0:T(8,128)(2,1)S(1)} collective-permute-done((bf16[256,256]{1,0:T(8,128)(2,1)S(1)}, bf16[256,256]{1,0:T(8,128)(2,1)S(1)}, u32[]{:S(2)}, u32[]{:S(2)}) %collective-permute-start.5) | collective-permute-done | bytes 131104 | tf_op jit(solution)/shard_map/ppermute | solution.py:61
  31.3 0.8 pick_blocks.1
  32.0 1.9 %collective-permute-start.8 = (bf16[4,2,64,256]{3,2,1,0:T(8,128)(2,1)S(1)}, bf16[4,2,64,256]{3,2,1,0:T(8,128)(2,1)S(1)}, u32[]{:S(2)}, u32[]{:S(2)}) collective-permute-start(bf16[4,2,64,256]{3,2,1,0:T(8,128)(2,1)S(1)} %get-tuple-element.52), channel_id=1, source_target_pairs={{8,16},{16,8},{24,32},{32,24},{40,48},{48,40},{56,64},{64,56},{72,... | collective-permute-start | bytes 786440 | tf_op jit(solution)/shard_map/ppermute | solution.py:42
  34.0 1.8 %collective-permute-start.7 = (bf16[4,2,64,256]{3,2,1,0:T(8,128)(2,1)S(1)}, bf16[4,2,64,256]{3,2,1,0:T(8,128)(2,1)S(1)}, u32[]{:S(2)}, u32[]{:S(2)}) collective-permute-start(bf16[4,2,64,256]{3,2,1,0:T(8,128)(2,1)S(1)} %get-tuple-element.52), channel_id=1, source_target_pairs={{0,8},{8,0},{16,24},{24,16},{32,40},{40,32},{48,56},{56,48},{64,72... | collective-permute-start | bytes 786440 | tf_op jit(solution)/shard_map/ppermute | solution.py:42
  35.7 4.5 %collective-permute-start.10 = (bf16[2,2,64,256]{3,2,1,0:T(8,128)(2,1)S(1)}, bf16[2,2,64,256]{3,2,1,0:T(8,128)(2,1)S(1)}, u32[]{:S(2)}, u32[]{:S(2)}) collective-permute-start(bf16[2,2,64,256]{3,2,1,0:T(8,128)(2,1)S(1)} %get-tuple-element.53), channel_id=1, source_target_pairs={{16,32},{32,16},{24,40},{40,24},{48,64},{64,48},{56,72},{72,56},{8... | collective-permute-start | bytes 393224 | tf_op jit(solution)/shard_map/ppermute | solution.py:42
  40.2 0.4 collective-permute-start.9
  40.6 0.9 own_scores.1
  41.5 3.7 %collective-permute-done.10.refs_11_ = bf16[2,2,64,256]{3,2,1,0:T(8,128)(2,1)S(1)} collective-permute-done((bf16[2,2,64,256]{3,2,1,0:T(8,128)(2,1)S(1)}, bf16[2,2,64,256]{3,2,1,0:T(8,128)(2,1)S(1)}, u32[]{:S(2)}, u32[]{:S(2)}) %collective-permute-start.10) | collective-permute-done | bytes 131104 | tf_op jit(solution)/shard_map/ppermute | solution.py:42
  45.2 0.3 collective-permute-done.9.refs_10_
  45.4 0.0 collective-permute-done.8.refs_9_
  45.4 0.0 collective-permute-done.7.refs_8_
  45.4 3.0 %remote_part.1 = (f32[2,8,512]{2,1,0:T(8,128)S(1)}, bf16[4,2,64,256]{3,2,1,0:T(8,128)(2,1)S(1)}, bf16[4,2,64,256]{3,2,1,0:T(8,128)(2,1)S(1)}, bf16[2,2,64,256]{3...) custom-call(bf16[4,64,256]{2,1,0:T(8,128)(2,1)S(1)} %get-tuple-eleme, ...), custom_call_target="tpu_custom_call" | custom-call | tf_op jit(solution)/shard_map/remote_part/pallas_call | solution.py:245
  48.5 0.1 collective-permute-start.11
  48.6 4.3 %collective-permute-start.12 = (bf16[4,2,64,256]{3,2,1,0:T(8,128)(2,1)S(1)}, bf16[4,2,64,256]{3,2,1,0:T(8,128)(2,1)S(1)}, u32[]{:S(2)}, u32[]{:S(2)}) collective-permute-start(bf16[4,2,64,256]{3,2,1,0:T(8,128)(2,1)S(1)} %get-tuple-element.69), channel_id=1, source_target_pairs={{8,16},{16,8},{24,32},{32,24},{40,48},{48,40},{56,64},{64,56},{72,... | collective-permute-start | bytes 786440 | tf_op jit(solution)/shard_map/ppermute | solution.py:42
  52.9 0.1 collective-permute-start.13
  53.0 2.7 %collective-permute-start.14 = (bf16[2,2,64,256]{3,2,1,0:T(8,128)(2,1)S(1)}, bf16[2,2,64,256]{3,2,1,0:T(8,128)(2,1)S(1)}, u32[]{:S(2)}, u32[]{:S(2)}) collective-permute-start(bf16[2,2,64,256]{3,2,1,0:T(8,128)(2,1)S(1)} %get-tuple-element.71), channel_id=1, source_target_pairs={{16,32},{32,16},{24,40},{40,24},{48,64},{64,48},{56,72},{72,56},{8... | collective-permute-start | bytes 393224 | tf_op jit(solution)/shard_map/ppermute | solution.py:42
  55.6 1.6 %own_grads.1 = (bf16[8,2,64,256]{3,2,1,0:T(8,128)(2,1)S(1)}, f32[8,2,64,256]{3,2,1,0:T(8,128)S(1)}) custom-call(bf16[4,64,256]{2,1,0:T(8,128)(2,1)S(1)} %get-tuple-element.44.refs_0_, bf16[4,64,256]{2,1,0:T(8,128)(2,1)S(1)} %bitcast.36, bf16[4,64,256]{2,1,0:T(8,128)(2,1)S(1)} %bitcast.32, bf16[4,64,256]{2,1,0:T(8,128)(2,1)S(1)} %bitcast.40, ...), custom_call_target="tpu_custom_call" | custom-call | tf_op jit(solution)/shard_map/own_grads/pallas_call | solution.py:280
  57.3 2.0 %collective-permute-done.13.a2_ref = bf16[2,2,64,256]{3,2,1,0:T(8,128)(2,1)S(1)} collective-permute-done((bf16[2,2,64,256]{3,2,1,0:T(8,128)(2,1)S(1)}, bf16[2,2,64,256]{3,2,1,0:T(8,128)(2,1)S(1)}, u32[]{:S(2)}, u32[]{:S(2)}) %collective-permute-start.13) | collective-permute-done | bytes 131104 | tf_op jit(solution)/shard_map/ppermute | solution.py:42
  59.3 2.7 %collective-permute-done.14.b2_ref = bf16[2,2,64,256]{3,2,1,0:T(8,128)(2,1)S(1)} collective-permute-done((bf16[2,2,64,256]{3,2,1,0:T(8,128)(2,1)S(1)}, bf16[2,2,64,256]{3,2,1,0:T(8,128)(2,1)S(1)}, u32[]{:S(2)}, u32[]{:S(2)}) %collective-permute-start.14) | collective-permute-done | bytes 131104 | tf_op jit(solution)/shard_map/ppermute | solution.py:42
  62.0 0.0 collective-permute-done.11.a1_ref
  62.0 0.0 collective-permute-done.12.b1_ref
  62.0 1.0 %add_returned.1 = (bf16[4,64,256]{2,1,0:T(8,128)(2,1)S(1)}, bf16[4,64,256]{2,1,0:T(8,128)(2,1)S(1)}, bf16[4,64,256]{2,1,0:T(8,128)(2,1)S(1)}, bf16[4,64,256]{2,1...) custom-call(s32[4,32]{1,0:T(4,128)} %bitcast.79, ...), custom_call_target="tpu_custom_call" | custom-call | tf_op jit(solution)/shard_map/add_returned/pallas_call | solution.py:308
  62.9 2.3 %collective-permute-start.15 = (bf16[256,256]{1,0:T(8,128)(2,1)S(1)}, bf16[256,256]{1,0:T(8,128)(2,1)S(1)}, u32[]{:S(2)}, u32[]{:S(2)}) collective-permute-start(bf16[256,256]{1,0:T(8,128)(2,1)S(1)} %bitcast.76), channel_id=1, source_target_pairs={{0,7},{1,0},{2,1},{3,2},{4,3},{5,4},{6,5},{7,6},{8,15},{9,8},{10,9... | collective-permute-start | bytes 393224 | tf_op jit(solution)/shard_map/ppermute | solution.py:61
  65.2 2.6 %collective-permute-start.16 = (bf16[256,256]{1,0:T(8,128)(2,1)S(1)}, bf16[256,256]{1,0:T(8,128)(2,1)S(1)}, u32[]{:S(2)}, u32[]{:S(2)}) collective-permute-start(bf16[256,256]{1,0:T(8,128)(2,1)S(1)} %bitcast.74), channel_id=1, source_target_pairs={{0,1},{1,2},{2,3},{3,4},{4,5},{5,6},{6,7},{7,0},{8,9},{9,10},{10,1... | collective-permute-start | bytes 393224 | tf_op jit(solution)/shard_map/ppermute | solution.py:61
  67.8 1.6 %collective-permute-start.17 = (bf16[256,256]{1,0:T(8,128)(2,1)S(1)}, bf16[256,256]{1,0:T(8,128)(2,1)S(1)}, u32[]{:S(2)}, u32[]{:S(2)}) collective-permute-start(bf16[256,256]{1,0:T(8,128)(2,1)S(1)} %bitcast.71), channel_id=1, source_target_pairs={{0,6},{1,7},{2,0},{3,1},{4,2},{5,3},{6,4},{7,5},{8,14},{9,15},{10,... | collective-permute-start | bytes 393224 | tf_op jit(solution)/shard_map/ppermute | solution.py:61
  69.3 1.4 %collective-permute-start.18 = (bf16[256,256]{1,0:T(8,128)(2,1)S(1)}, bf16[256,256]{1,0:T(8,128)(2,1)S(1)}, u32[]{:S(2)}, u32[]{:S(2)}) collective-permute-start(bf16[256,256]{1,0:T(8,128)(2,1)S(1)} %bitcast.69), channel_id=1, source_target_pairs={{0,2},{1,3},{2,4},{3,5},{4,6},{5,7},{6,0},{7,1},{8,10},{9,11},{10,... | collective-permute-start | bytes 393224 | tf_op jit(solution)/shard_map/ppermute | solution.py:61
  70.7 2.7 %collective-permute-start.19 = (bf16[256,256]{1,0:T(8,128)(2,1)S(1)}, bf16[256,256]{1,0:T(8,128)(2,1)S(1)}, u32[]{:S(2)}, u32[]{:S(2)}) collective-permute-start(bf16[256,256]{1,0:T(8,128)(2,1)S(1)} %bitcast.67), channel_id=1, source_target_pairs={{0,5},{1,6},{2,7},{3,0},{4,1},{5,2},{6,3},{7,4},{8,13},{9,14},{10,... | collective-permute-start | bytes 393224 | tf_op jit(solution)/shard_map/ppermute | solution.py:61
  73.4 0.0 collective-permute-done.15
  73.4 1.2 %collective-permute-start.20 = (bf16[256,256]{1,0:T(8,128)(2,1)S(1)}, bf16[256,256]{1,0:T(8,128)(2,1)S(1)}, u32[]{:S(2)}, u32[]{:S(2)}) collective-permute-start(bf16[256,256]{1,0:T(8,128)(2,1)S(1)} %bitcast.65), channel_id=1, source_target_pairs={{0,3},{1,4},{2,5},{3,6},{4,7},{5,0},{6,1},{7,2},{8,11},{9,12},{10,... | collective-permute-start | bytes 393224 | tf_op jit(solution)/shard_map/ppermute | solution.py:61
  74.6 0.0 collective-permute-done.16
  74.6 2.8 %collective-permute-start.21 = (bf16[256,256]{1,0:T(8,128)(2,1)S(1)}, bf16[256,256]{1,0:T(8,128)(2,1)S(1)}, u32[]{:S(2)}, u32[]{:S(2)}) collective-permute-start(bf16[256,256]{1,0:T(8,128)(2,1)S(1)} %bitcast.64), channel_id=1, source_target_pairs={{0,4},{1,5},{2,6},{3,7},{4,0},{5,1},{6,2},{7,3},{8,12},{9,13},{10,... | collective-permute-start | bytes 393224 | tf_op jit(solution)/shard_map/ppermute | solution.py:61
  77.4 2.7 %collective-permute-done.17 = bf16[256,256]{1,0:T(8,128)(2,1)S(1)} collective-permute-done((bf16[256,256]{1,0:T(8,128)(2,1)S(1)}, bf16[256,256]{1,0:T(8,128)(2,1)S(1)}, u32[]{:S(2)}, u32[]{:S(2)}) %collective-permute-start.17) | collective-permute-done | bytes 131104 | tf_op jit(solution)/shard_map/ppermute | solution.py:61
  80.1 1.1 %collective-permute-done.18 = bf16[256,256]{1,0:T(8,128)(2,1)S(1)} collective-permute-done((bf16[256,256]{1,0:T(8,128)(2,1)S(1)}, bf16[256,256]{1,0:T(8,128)(2,1)S(1)}, u32[]{:S(2)}, u32[]{:S(2)}) %collective-permute-start.18) | collective-permute-done | bytes 131104 | tf_op jit(solution)/shard_map/ppermute | solution.py:61
  81.2 5.5 %collective-permute-done.19 = bf16[256,256]{1,0:T(8,128)(2,1)S(1)} collective-permute-done((bf16[256,256]{1,0:T(8,128)(2,1)S(1)}, bf16[256,256]{1,0:T(8,128)(2,1)S(1)}, u32[]{:S(2)}, u32[]{:S(2)}) %collective-permute-start.19) | collective-permute-done | bytes 131104 | tf_op jit(solution)/shard_map/ppermute | solution.py:61
  86.6 3.4 %collective-permute-done.20 = bf16[256,256]{1,0:T(8,128)(2,1)S(1)} collective-permute-done((bf16[256,256]{1,0:T(8,128)(2,1)S(1)}, bf16[256,256]{1,0:T(8,128)(2,1)S(1)}, u32[]{:S(2)}, u32[]{:S(2)}) %collective-permute-start.20) | collective-permute-done | bytes 131104 | tf_op jit(solution)/shard_map/ppermute | solution.py:61
  90.0 0.0 collective-permute-done.21
  90.0 1.1 %unpack.1 = (bf16[64,2048]{1,0:T(8,128)(2,1)}, bf16[64,2048]{1,0:T(8,128)(2,1)}, bf16[64,2048]{1,0:T(8,128)(2,1)}, bf16[64,2048]{1,0:T(8,128)(2,1)}) custom-call(bf16[4,64,256]{2,1,0:T(8,128)(2,1)S(1)} %get-tuple-element.72.refs_0_, bf16[4,64,256]{2,1,0:T(8,128)(2,1)S(1)} %bitcast.57, bf16[4,64,256]{2,1,0:T(8,128)(2,1)S(1)} %bitcast.58, ...), custom_call_target="tpu_custom_call" | custom-call | tf_op jit(solution)/shard_map/unpack/pallas_call | solution.py:116
  (3 shorter events, 0.0 us)
Async XLA Ops:
  2.1 10.9 %collective-permute-start.1 = (bf16[256,256]{1,0:T(8,128)(2,1)S(1)}, bf16[256,256]{1,0:T(8,128)(2,1)S(1)}, u32[]{:S(2)}, u32[]{:S(2)}) collective-permute-start(bf16[256,256]{1,0:T(8,128)(2,1)S(1)} %bitcast.77), channel_id=1, source_target_pairs={{0,7},{1,0},{2,1},{3,2},{4,3},{5,4},{6,5},{7,6},{8,15},{9,8},{10,9... | collective-permute-start | bytes 393224 | tf_op jit(solution)/shard_map/ppermute | solution.py:61
  8.0 9.7 %collective-permute-start = (bf16[256,256]{1,0:T(8,128)(2,1)S(1)}, bf16[256,256]{1,0:T(8,128)(2,1)S(1)}, u32[]{:S(2)}, u32[]{:S(2)}) collective-permute-start(bf16[256,256]{1,0:T(8,128)(2,1)S(1)} %bitcast.75), channel_id=1, source_target_pairs={{0,1},{1,2},{2,3},{3,4},{4,5},{5,6},{6,7},{7,0},{8,9},{9,10},{10,1... | collective-permute-start | bytes 393224 | tf_op jit(solution)/shard_map/ppermute | solution.py:61
  8.1 13.6 %collective-permute-start.2 = (bf16[256,256]{1,0:T(8,128)(2,1)S(1)}, bf16[256,256]{1,0:T(8,128)(2,1)S(1)}, u32[]{:S(2)}, u32[]{:S(2)}) collective-permute-start(bf16[256,256]{1,0:T(8,128)(2,1)S(1)} %bitcast.73), channel_id=1, source_target_pairs={{0,2},{1,3},{2,4},{3,5},{4,6},{5,7},{6,0},{7,1},{8,10},{9,11},{10,... | collective-permute-start | bytes 393224 | tf_op jit(solution)/shard_map/ppermute | solution.py:61
  8.1 13.6 %collective-permute-start.3 = (bf16[256,256]{1,0:T(8,128)(2,1)S(1)}, bf16[256,256]{1,0:T(8,128)(2,1)S(1)}, u32[]{:S(2)}, u32[]{:S(2)}) collective-permute-start(bf16[256,256]{1,0:T(8,128)(2,1)S(1)} %bitcast.72), channel_id=1, source_target_pairs={{0,6},{1,7},{2,0},{3,1},{4,2},{5,3},{6,4},{7,5},{8,14},{9,15},{10,... | collective-permute-start | bytes 393224 | tf_op jit(solution)/shard_map/ppermute | solution.py:61
  12.2 17.3 %collective-permute-start.4 = (bf16[256,256]{1,0:T(8,128)(2,1)S(1)}, bf16[256,256]{1,0:T(8,128)(2,1)S(1)}, u32[]{:S(2)}, u32[]{:S(2)}) collective-permute-start(bf16[256,256]{1,0:T(8,128)(2,1)S(1)} %bitcast.70), channel_id=1, source_target_pairs={{0,3},{1,4},{2,5},{3,6},{4,7},{5,0},{6,1},{7,2},{8,11},{9,12},{10,... | collective-permute-start | bytes 393224 | tf_op jit(solution)/shard_map/ppermute | solution.py:61
  13.0 18.3 %collective-permute-start.5 = (bf16[256,256]{1,0:T(8,128)(2,1)S(1)}, bf16[256,256]{1,0:T(8,128)(2,1)S(1)}, u32[]{:S(2)}, u32[]{:S(2)}) collective-permute-start(bf16[256,256]{1,0:T(8,128)(2,1)S(1)} %bitcast.68), channel_id=1, source_target_pairs={{0,5},{1,6},{2,7},{3,0},{4,1},{5,2},{6,3},{7,4},{8,13},{9,14},{10,... | collective-permute-start | bytes 393224 | tf_op jit(solution)/shard_map/ppermute | solution.py:61
  17.7 13.5 %collective-permute-start.6 = (bf16[256,256]{1,0:T(8,128)(2,1)S(1)}, bf16[256,256]{1,0:T(8,128)(2,1)S(1)}, u32[]{:S(2)}, u32[]{:S(2)}) collective-permute-start(bf16[256,256]{1,0:T(8,128)(2,1)S(1)} %bitcast.66), channel_id=1, source_target_pairs={{0,4},{1,5},{2,6},{3,7},{4,0},{5,1},{6,2},{7,3},{8,12},{9,13},{10,... | collective-permute-start | bytes 393224 | tf_op jit(solution)/shard_map/ppermute | solution.py:61
  32.0 13.4 %collective-permute-start.8 = (bf16[4,2,64,256]{3,2,1,0:T(8,128)(2,1)S(1)}, bf16[4,2,64,256]{3,2,1,0:T(8,128)(2,1)S(1)}, u32[]{:S(2)}, u32[]{:S(2)}) collective-permute-start(bf16[4,2,64,256]{3,2,1,0:T(8,128)(2,1)S(1)} %get-tuple-element.52), channel_id=1, source_target_pairs={{8,16},{16,8},{24,32},{32,24},{40,48},{48,40},{56,64},{64,56},{72,... | collective-permute-start | bytes 786440 | tf_op jit(solution)/shard_map/ppermute | solution.py:42
  34.0 11.5 %collective-permute-start.7 = (bf16[4,2,64,256]{3,2,1,0:T(8,128)(2,1)S(1)}, bf16[4,2,64,256]{3,2,1,0:T(8,128)(2,1)S(1)}, u32[]{:S(2)}, u32[]{:S(2)}) collective-permute-start(bf16[4,2,64,256]{3,2,1,0:T(8,128)(2,1)S(1)} %get-tuple-element.52), channel_id=1, source_target_pairs={{0,8},{8,0},{16,24},{24,16},{32,40},{40,32},{48,56},{56,48},{64,72... | collective-permute-start | bytes 786440 | tf_op jit(solution)/shard_map/ppermute | solution.py:42
  35.7 9.4 %collective-permute-start.10 = (bf16[2,2,64,256]{3,2,1,0:T(8,128)(2,1)S(1)}, bf16[2,2,64,256]{3,2,1,0:T(8,128)(2,1)S(1)}, u32[]{:S(2)}, u32[]{:S(2)}) collective-permute-start(bf16[2,2,64,256]{3,2,1,0:T(8,128)(2,1)S(1)} %get-tuple-element.53), channel_id=1, source_target_pairs={{16,32},{32,16},{24,40},{40,24},{48,64},{64,48},{56,72},{72,56},{8... | collective-permute-start | bytes 393224 | tf_op jit(solution)/shard_map/ppermute | solution.py:42
  40.2 5.2 %collective-permute-start.9 = (bf16[2,2,64,256]{3,2,1,0:T(8,128)(2,1)S(1)}, bf16[2,2,64,256]{3,2,1,0:T(8,128)(2,1)S(1)}, u32[]{:S(2)}, u32[]{:S(2)}) collective-permute-start(bf16[2,2,64,256]{3,2,1,0:T(8,128)(2,1)S(1)} %get-tuple-element.53), channel_id=1, source_target_pairs={{0,16},{16,0},{8,24},{24,8},{32,48},{48,32},{40,56},{56,40},{64,80... | collective-permute-start | bytes 393224 | tf_op jit(solution)/shard_map/ppermute | solution.py:42
  48.5 13.5 %collective-permute-start.11 = (bf16[4,2,64,256]{3,2,1,0:T(8,128)(2,1)S(1)}, bf16[4,2,64,256]{3,2,1,0:T(8,128)(2,1)S(1)}, u32[]{:S(2)}, u32[]{:S(2)}) collective-permute-start(bf16[4,2,64,256]{3,2,1,0:T(8,128)(2,1)S(1)} %get-tuple-element.68), channel_id=1, source_target_pairs={{0,8},{8,0},{16,24},{24,16},{32,40},{40,32},{48,56},{56,48},{64,72... | collective-permute-start | bytes 786440 | tf_op jit(solution)/shard_map/ppermute | solution.py:42
  48.6 13.4 %collective-permute-start.12 = (bf16[4,2,64,256]{3,2,1,0:T(8,128)(2,1)S(1)}, bf16[4,2,64,256]{3,2,1,0:T(8,128)(2,1)S(1)}, u32[]{:S(2)}, u32[]{:S(2)}) collective-permute-start(bf16[4,2,64,256]{3,2,1,0:T(8,128)(2,1)S(1)} %get-tuple-element.69), channel_id=1, source_target_pairs={{8,16},{16,8},{24,32},{32,24},{40,48},{48,40},{56,64},{64,56},{72,... | collective-permute-start | bytes 786440 | tf_op jit(solution)/shard_map/ppermute | solution.py:42
  52.9 6.4 %collective-permute-start.13 = (bf16[2,2,64,256]{3,2,1,0:T(8,128)(2,1)S(1)}, bf16[2,2,64,256]{3,2,1,0:T(8,128)(2,1)S(1)}, u32[]{:S(2)}, u32[]{:S(2)}) collective-permute-start(bf16[2,2,64,256]{3,2,1,0:T(8,128)(2,1)S(1)} %get-tuple-element.70), channel_id=1, source_target_pairs={{0,16},{16,0},{8,24},{24,8},{32,48},{48,32},{40,56},{56,40},{64,80... | collective-permute-start | bytes 393224 | tf_op jit(solution)/shard_map/ppermute | solution.py:42
  53.0 9.0 %collective-permute-start.14 = (bf16[2,2,64,256]{3,2,1,0:T(8,128)(2,1)S(1)}, bf16[2,2,64,256]{3,2,1,0:T(8,128)(2,1)S(1)}, u32[]{:S(2)}, u32[]{:S(2)}) collective-permute-start(bf16[2,2,64,256]{3,2,1,0:T(8,128)(2,1)S(1)} %get-tuple-element.71), channel_id=1, source_target_pairs={{16,32},{32,16},{24,40},{40,24},{48,64},{64,48},{56,72},{72,56},{8... | collective-permute-start | bytes 393224 | tf_op jit(solution)/shard_map/ppermute | solution.py:42
  62.9 10.5 %collective-permute-start.15 = (bf16[256,256]{1,0:T(8,128)(2,1)S(1)}, bf16[256,256]{1,0:T(8,128)(2,1)S(1)}, u32[]{:S(2)}, u32[]{:S(2)}) collective-permute-start(bf16[256,256]{1,0:T(8,128)(2,1)S(1)} %bitcast.76), channel_id=1, source_target_pairs={{0,7},{1,0},{2,1},{3,2},{4,3},{5,4},{6,5},{7,6},{8,15},{9,8},{10,9... | collective-permute-start | bytes 393224 | tf_op jit(solution)/shard_map/ppermute | solution.py:61
  65.2 9.4 %collective-permute-start.16 = (bf16[256,256]{1,0:T(8,128)(2,1)S(1)}, bf16[256,256]{1,0:T(8,128)(2,1)S(1)}, u32[]{:S(2)}, u32[]{:S(2)}) collective-permute-start(bf16[256,256]{1,0:T(8,128)(2,1)S(1)} %bitcast.74), channel_id=1, source_target_pairs={{0,1},{1,2},{2,3},{3,4},{4,5},{5,6},{6,7},{7,0},{8,9},{9,10},{10,1... | collective-permute-start | bytes 393224 | tf_op jit(solution)/shard_map/ppermute | solution.py:61
  67.8 12.3 %collective-permute-start.17 = (bf16[256,256]{1,0:T(8,128)(2,1)S(1)}, bf16[256,256]{1,0:T(8,128)(2,1)S(1)}, u32[]{:S(2)}, u32[]{:S(2)}) collective-permute-start(bf16[256,256]{1,0:T(8,128)(2,1)S(1)} %bitcast.71), channel_id=1, source_target_pairs={{0,6},{1,7},{2,0},{3,1},{4,2},{5,3},{6,4},{7,5},{8,14},{9,15},{10,... | collective-permute-start | bytes 393224 | tf_op jit(solution)/shard_map/ppermute | solution.py:61
  69.3 11.8 %collective-permute-start.18 = (bf16[256,256]{1,0:T(8,128)(2,1)S(1)}, bf16[256,256]{1,0:T(8,128)(2,1)S(1)}, u32[]{:S(2)}, u32[]{:S(2)}) collective-permute-start(bf16[256,256]{1,0:T(8,128)(2,1)S(1)} %bitcast.69), channel_id=1, source_target_pairs={{0,2},{1,3},{2,4},{3,5},{4,6},{5,7},{6,0},{7,1},{8,10},{9,11},{10,... | collective-permute-start | bytes 393224 | tf_op jit(solution)/shard_map/ppermute | solution.py:61
  70.7 15.9 %collective-permute-start.19 = (bf16[256,256]{1,0:T(8,128)(2,1)S(1)}, bf16[256,256]{1,0:T(8,128)(2,1)S(1)}, u32[]{:S(2)}, u32[]{:S(2)}) collective-permute-start(bf16[256,256]{1,0:T(8,128)(2,1)S(1)} %bitcast.67), channel_id=1, source_target_pairs={{0,5},{1,6},{2,7},{3,0},{4,1},{5,2},{6,3},{7,4},{8,13},{9,14},{10,... | collective-permute-start | bytes 393224 | tf_op jit(solution)/shard_map/ppermute | solution.py:61
  73.4 16.6 %collective-permute-start.20 = (bf16[256,256]{1,0:T(8,128)(2,1)S(1)}, bf16[256,256]{1,0:T(8,128)(2,1)S(1)}, u32[]{:S(2)}, u32[]{:S(2)}) collective-permute-start(bf16[256,256]{1,0:T(8,128)(2,1)S(1)} %bitcast.65), channel_id=1, source_target_pairs={{0,3},{1,4},{2,5},{3,6},{4,7},{5,0},{6,1},{7,2},{8,11},{9,12},{10,... | collective-permute-start | bytes 393224 | tf_op jit(solution)/shard_map/ppermute | solution.py:61
  74.6 15.5 %collective-permute-start.21 = (bf16[256,256]{1,0:T(8,128)(2,1)S(1)}, bf16[256,256]{1,0:T(8,128)(2,1)S(1)}, u32[]{:S(2)}, u32[]{:S(2)}) collective-permute-start(bf16[256,256]{1,0:T(8,128)(2,1)S(1)} %bitcast.64), channel_id=1, source_target_pairs={{0,4},{1,5},{2,6},{3,7},{4,0},{5,1},{6,2},{7,3},{8,12},{9,13},{10,... | collective-permute-start | bytes 393224 | tf_op jit(solution)/shard_map/ppermute | solution.py:61

commit v4 on v3

--- a/solution.py
+++ b/solution.py
@@ -16,6 +16,8 @@
 LOG2E = 1.0 / math.log(2.0)
 MIB = 1024 * 1024
 SHIFTS = (0, 1, 7, 2, 6, 3, 5, 4)
+
+LOWEST = -1e30
 
 VM = pl.BlockSpec(memory_space=pltpu.VMEM)
 SM = pl.BlockSpec(memory_space=pltpu.SMEM)
@@ -53,25 +55,32 @@
 
 
 def head_shifts(pieces, sign):
-    length = lax.axis_size("head")
+    frames, length = lax.axis_size("frame"), lax.axis_size("head")
     arrived = []
     for piece, by in zip(pieces, SHIFTS):
         if by:
+            pairs = []
+            for frame in range(frames):
+                step = -sign * by if frame % 2 else sign * by
+                pairs += [(frame * length + i, frame * length + (i + step) % length) for i in range(length)]
             flat = piece.reshape(-1, piece.shape[-1])
-            flat = lax.ppermute(flat, "head", [(i, (i + sign * by) % length) for i in range(length)])
-            piece = flat.reshape(piece.shape)
+            piece = lax.ppermute(flat, ("frame", "head"), pairs).reshape(piece.shape)
         arrived.append(piece)
     return arrived
 
 
+def moved(step):
+    length = lax.axis_size("head")
+    odd = lax.rem(lax.axis_index("frame"), 2)
+    return lax.rem(lax.axis_index("head") + length + step * (1 - 2 * odd), length)
+
+
 def place_above(slot):
-    length = lax.axis_size("head")
-    return lax.rem(lax.axis_index("head") + SHIFTS[slot], length)
+    return moved(SHIFTS[slot])
 
 
 def place_below(slot):
-    length = lax.axis_size("head")
-    return lax.rem(lax.axis_index("head") + (length - SHIFTS[slot]), length)
+    return moved(-SHIFTS[slot])
 
 
 def columns_of(slot, piece):
@@ -154,14 +163,18 @@
     return jnp.concatenate([ref[i, :, columns(head)] for ref in refs], axis=0)
 
 
+def panel_rows(refs, i, head):
+    return jnp.concatenate([ref[:, i, :, columns(head)].reshape(-1, HD) for ref in refs], axis=0)
+
+
 def own_scores_body(*refs):
     piece_refs, (power_ref, weight_grad_ref, stats_ref) = refs[:-3], refs[-3:]
     for head in range(piece_refs[0].shape[-1] // HD):
         key, value, query, grad = [rows_of(piece_refs, i, head) for i in range(4)]
-        scores = dot(key, query, (1, 1)) * (SCALE * LOG2E)
+        scores = dot(key, query, (1, 1))
         weight_grad = dot(value, grad, (1, 1))
         peak = jnp.max(scores, axis=0, keepdims=True)
-        power = jnp.exp2(scores - peak)
+        power = jnp.exp2((scores - peak) * (SCALE * LOG2E))
         power_ref[head] = power
         weight_grad_ref[head] = weight_grad
         stats_ref[head, 0:1] = peak
@@ -179,77 +192,106 @@
     )(*pieces)
 
 
+def near_scores_body(frame_count, parts, *refs):
+    piece_refs, panel_refs, (power_ref, weight_grad_ref, stats_ref) = refs[:parts], refs[parts:-3], refs[-3:]
+    hidden, spans = hidden_and_spans(frame_count, panel_refs, SWAPS[: len(panel_refs)])
+    for head in range(piece_refs[0].shape[-1] // HD):
+        query, grad = [rows_of(piece_refs, i, head) for i in (2, 3)]
+        scores = dot(panel_rows(panel_refs, 0, head), query, (1, 1))
+        weight_grad = dot(panel_rows(panel_refs, 1, head), grad, (1, 1))
+        weight_grad_ref[head] = weight_grad
+        peaks = [jnp.max(scores[span], axis=0, keepdims=True) + bias for span, bias in zip(spans, hidden)]
+        peak = jnp.maximum(functools.reduce(jnp.maximum, peaks), LOWEST)
+        total = moment = 0.0
+        for span, bias in zip(spans, hidden):
+            power = jnp.exp2((scores[span] - (peak - bias)) * (SCALE * LOG2E))
+            power_ref[head, span] = power
+            total = total + jnp.sum(power, axis=0, keepdims=True)
+            moment = moment + jnp.sum(power * weight_grad[span], axis=0, keepdims=True)
+        stats_ref[head, 0:1] = peak
+        stats_ref[head, 1:2] = total
+        stats_ref[head, 2:3] = moment
+
+
+def near_scores(pieces, panels):
+    parts = len(pieces)
+    _, rows, width = pieces[0].shape
+    tokens = parts * rows
+    square = jax.ShapeDtypeStruct((width // HD, sum(p.shape[0] for p in panels) * rows, tokens), F32)
+    stats = jax.ShapeDtypeStruct((width // HD, 8, tokens), F32)
+    body = functools.partial(near_scores_body, lax.axis_size("frame"), parts)
+    return call(
+        body, [square, square, stats], [VM] * (parts + len(panels)), [VM] * 3, "near_scores", 16
+    )(*pieces, *panels)
+
+
+def hidden_and_spans(frame_count, panel_refs, swaps):
+    frame = lax.axis_index("frame")
+    hidden = [jnp.where(has_partner(frame, frame_count, *swap), 0.0, -jnp.inf).astype(F32) for swap in swaps]
+    sizes = [ref.shape[0] * ref.shape[2] for ref in panel_refs]
+    return hidden, [slice(sum(sizes[:i]), sum(sizes[: i + 1])) for i in range(len(sizes))]
+
+
 def remote_part_body(frame_count, parts, *refs):
-    piece_refs, panel_refs, stats_ref = refs[:parts], refs[parts : parts + 4], refs[parts + 4]
-    joint_ref, *rest = refs[parts + 5 :]
-    target_refs, low_refs, score_grad_refs = rest[:4], rest[4:8], rest[8:]
-    frame = lax.axis_index("frame")
+    piece_refs, far_refs, refs = refs[:parts], refs[parts : parts + 2], refs[parts + 2 :]
+    stats_ref, near_stats_ref, power_ref, weight_grad_ref, joint_ref, *target_refs, low_ref, score_grad_ref = refs
     rows = piece_refs[0].shape[1]
-    heads = range(piece_refs[0].shape[-1] // HD)
-    hidden = [
-        jnp.where(has_partner(frame, frame_count, *swap), 0.0, -jnp.inf).astype(F32) for swap in SWAPS
-    ]
-    queries = [rows_of(piece_refs, 2, head) for head in heads]
-    grads = [rows_of(piece_refs, 3, head) for head in heads]
-    scores = [
-        [
-            dot(ref[:, 0, :, columns(head)].reshape(-1, HD), queries[head], (1, 1)) * (SCALE * LOG2E) + bias
-            for ref, bias in zip(panel_refs, hidden)
+    hidden, spans = hidden_and_spans(frame_count, far_refs, SWAPS[2:])
+    near = power_ref.shape[1]
+    for head in range(piece_refs[0].shape[-1] // HD):
+        query, grad = [rows_of(piece_refs, i, head) for i in (2, 3)]
+        scores = dot(panel_rows(far_refs, 0, head), query, (1, 1))
+        weight_grad = dot(panel_rows(far_refs, 1, head), grad, (1, 1))
+        parts_before = (stats_ref, near_stats_ref)
+        peaks = [jnp.max(scores[span], axis=0, keepdims=True) + bias for span, bias in zip(spans, hidden)]
+        peak = functools.reduce(jnp.maximum, peaks + [ref[head, 0:1] for ref in parts_before])
+        rescales = [jnp.exp2((ref[head, 0:1] - peak) * (SCALE * LOG2E)) for ref in parts_before]
+        powers = [
+            jnp.exp2((scores[span] - (peak - bias)) * (SCALE * LOG2E)) for span, bias in zip(spans, hidden)
         ]
-        for head in heads
-    ]
-    weight_grads = [
-        [dot(ref[:, 1, :, columns(head)].reshape(-1, HD), grads[head], (1, 1)) for ref in panel_refs]
-        for head in heads
-    ]
-    for head in heads:
-        own_peak = stats_ref[head, 0:1]
-        peaks = [jnp.max(s, axis=0, keepdims=True) for s in scores[head]]
-        peak = functools.reduce(jnp.maximum, peaks, own_peak)
-        powers = [jnp.exp2(s - peak) for s in scores[head]]
-        rescale = jnp.exp2(own_peak - peak)
-        total = functools.reduce(
-            jnp.add, [jnp.sum(p, axis=0, keepdims=True) for p in powers], stats_ref[head, 1:2] * rescale
+        totals = [jnp.sum(p, axis=0, keepdims=True) for p in powers]
+        totals += [ref[head, 1:2] * by for ref, by in zip(parts_before, rescales)]
+        moments = [jnp.sum(p * weight_grad[span], axis=0, keepdims=True) for p, span in zip(powers, spans)]
+        moments += [ref[head, 2:3] * by for ref, by in zip(parts_before, rescales)]
+        inverse = 1.0 / functools.reduce(jnp.add, totals)
+        delta = functools.reduce(jnp.add, moments) * inverse
+        joint_ref[head, 0:1] = rescales[0] * inverse
+        joint_ref[head, 1:2] = delta
+        near_weights = power_ref[head] * (rescales[1] * inverse)
+        weights = [near_weights] + [p * inverse for p in powers]
+        weight_grads = [weight_grad_ref[head]] + [weight_grad[span] for span in spans]
+        low = jnp.concatenate([w.astype(BF16) for w in weights], axis=0)
+        score_grad = jnp.concatenate(
+            [(w * (g - delta)).astype(BF16) for w, g in zip(weights, weight_grads)], axis=0
         )
-        moment = functools.reduce(
-            jnp.add,
-            [jnp.sum(p * g, axis=0, keepdims=True) for p, g in zip(powers, weight_grads[head])],
-            stats_ref[head, 2:3] * rescale,
-        )
-        inverse = 1.0 / total
-        delta = moment * inverse
-        joint_ref[head, 0:1] = rescale * inverse
-        joint_ref[head, 1:2] = delta
-        for power, weight_grad, low_ref, score_grad_ref in zip(
-            powers, weight_grads[head], low_refs, score_grad_refs
-        ):
-            weights = power * inverse
-            low_ref[head] = weights.astype(BF16)
-            score_grad_ref[head] = (weights * (weight_grad - delta)).astype(BF16)
-    for head in heads:
-        cols = columns(head)
-        for target, low_ref, score_grad_ref in zip(target_refs, low_refs, score_grad_refs):
-            key_part = dot(score_grad_ref[head], queries[head], (1, 0)) * SCALE
-            value_part = dot(low_ref[head], grads[head], (1, 0))
-            target[:, 0, :, cols] = key_part.astype(BF16).reshape(-1, rows, HD)
-            target[:, 1, :, cols] = value_part.astype(BF16).reshape(-1, rows, HD)
-
-
-def remote_part(pieces, panels, stats):
+        low_ref[head] = low
+        score_grad_ref[head] = score_grad
+        key_part = (dot(score_grad, query, (1, 0)) * SCALE).astype(BF16)
+        value_part = dot(low, grad, (1, 0)).astype(BF16)
+        start = 0
+        for target in target_refs:
+            size = target.shape[0] * rows
+            target[:, 0, :, columns(head)] = key_part[start : start + size].reshape(-1, rows, HD)
+            target[:, 1, :, columns(head)] = value_part[start : start + size].reshape(-1, rows, HD)
+            start += size
+
+
+def remote_part(pieces, panels, stats, near_stats, near_power, near_weight_grad):
     parts = len(pieces)
     _, rows, width = pieces[0].shape
     shape = jax.ShapeDtypeStruct
-    squares = [shape((width // HD, p.shape[0] * rows, parts * rows), BF16) for p in panels]
-    outs = [shape(stats.shape, F32)] + [shape(p.shape, BF16) for p in panels] + squares + squares
+    square = shape((width // HD, sum(p.shape[0] for p in panels) * rows, parts * rows), BF16)
+    outs = [shape(stats.shape, F32)] + [shape(p.shape, BF16) for p in panels] + [square, square]
     body = functools.partial(remote_part_body, lax.axis_size("frame"), parts)
-    outs = call(body, outs, [VM] * (parts + 5), [VM] * 13, "remote_part", 24)(*pieces, *panels, stats)
-    return outs[0], outs[1:5], outs[5:9], outs[9:]
+    outs = call(body, outs, [VM] * (parts + 6), [VM] * 7, "remote_part", 24)(
+        *pieces, *panels[2:], stats, near_stats, near_power, near_weight_grad
+    )
+    return outs[0], outs[1:5], outs[5], outs[6]
 
 
 def own_grads_body(parts, *refs):
     piece_refs, panel_refs, refs = refs[:parts], refs[parts : parts + 4], refs[parts + 4 :]
-    power_ref, weight_grad_ref, joint_ref = refs[:3]
-    low_refs, score_grad_refs, (first_ref, own_ref) = refs[3:7], refs[7:11], refs[11:]
+    power_ref, weight_grad_ref, joint_ref, low_ref, score_grad_ref, first_ref, own_ref = refs
     _, rows, width = piece_refs[0].shape
     for head in range(width // HD):
         cols = columns(head)
@@ -259,11 +301,16 @@
         low = weights.astype(BF16)
         own_ref[:, 0, :, cols] = (dot(score_grad, query, (1, 0)) * SCALE).reshape(parts, rows, HD)
         own_ref[:, 1, :, cols] = dot(low, grad, (1, 0)).reshape(parts, rows, HD)
-        query_t = dot(key, score_grad, (0, 0))
-        out_t = dot(value, low, (0, 0))
-        for panel_ref, low_ref, score_grad_ref in zip(panel_refs, low_refs, score_grad_refs):
-            query_t = query_t + dot(panel_ref[:, 0, :, cols].reshape(-1, HD), score_grad_ref[head], (0, 0))
-            out_t = out_t + dot(panel_ref[:, 1, :, cols].reshape(-1, HD), low_ref[head], (0, 0))
+        query_t = dot(
+            jnp.concatenate([key, panel_rows(panel_refs, 0, head)], axis=0),
+            jnp.concatenate([score_grad, score_grad_ref[head]], axis=0),
+            (0, 0),
+        )
+        out_t = dot(
+            jnp.concatenate([value, panel_rows(panel_refs, 1, head)], axis=0),
+            jnp.concatenate([low, low_ref[head]], axis=0),
+            (0, 0),
+        )
         attended = out_t.T.astype(BF16)
         query_grad = (query_t * SCALE).T.astype(BF16)
         for slot in range(parts):
@@ -277,8 +324,8 @@
     two = (parts, 2, rows, width)
     outs = [jax.ShapeDtypeStruct(two, BF16), jax.ShapeDtypeStruct(two, F32)]
     body = functools.partial(own_grads_body, parts)
-    return call(body, outs, [VM] * (parts + 15), [VM] * 2, "own_grads", 16)(
-        *pieces, *panels, power, weight_grad, joint, *lows, *score_grads
+    return call(body, outs, [VM] * (parts + 9), [VM] * 2, "own_grads", 16)(
+        *pieces, *panels, power, weight_grad, joint, lows, score_grads
     )
 
 
@@ -317,7 +364,10 @@
     near, far = pick_blocks(block_order, arrived)
     panels = [swapped(far if swap[0] == 2 else near, *swap) for swap in SWAPS]
     power, weight_grad, stats = own_scores(arrived)
-    joint, parts_of_others, lows, score_grads = remote_part(arrived, panels, stats)
+    near_power, near_weight_grad, near_stats = near_scores(arrived, panels[:2])
+    joint, parts_of_others, lows, score_grads = remote_part(
+        arrived, panels, stats, near_stats, near_power, near_weight_grad
+    )
     returned = [swapped(part, *swap) for part, swap in zip(parts_of_others, SWAPS)]
     first, own = own_grads(arrived, panels, power, weight_grad, joint, lows, score_grads)
     leaving = add_returned(block_order, first, own, returned)

time: 92.5 us -> 92.8 us (level)
  the two profiles are of different devices: /device:TPU:4 before, /device:TPU:61 now
where the time goes in v4:
time: 92.8 us; the launch traced here: 92.5 us
  starting transfers between devices  41.5 us (45%)
  waiting for transfers between devices  40.8 us (44%)
  Pallas kernels  9.4 us (10%)
    ppermute x14, waiting for transfers between devices, head_shifts(): piece = lax.ppermute(flat, ('frame', 'head'), pairs).reshape(piece.shape)  31.7 us
    ppermute x14, starting transfers between devices, head_shifts(): piece = lax.ppermute(flat, ('frame', 'head'), pairs).reshape(piece.shape)  26.1 us
    ppermute x8, starting transfers between devices, swapped(): return lax.ppermute(array, 'frame', pairs)  15.4 us
    ppermute x8, waiting for transfers between devices, swapped(): return lax.ppermute(array, 'frame', pairs)  9.16 us
    pallas_call x1, Pallas kernels, remote_part(): call(body, outs, [VM] * (parts + 6), [VM] * 7, 'remote_part', 24)  1.94 us
  transfers between devices with their start and end apart: 22, of which 10 were waited for; matrix products, arithmetic and copies ran while one was open for 0% of the time, Pallas kernels for 3%

profile of v4, /device:TPU:61, one launch (start us, length us, event | category | flops | bytes accessed | tf_op | source)
XLA Modules:
  0.0 92.5 jit_solution(17777886163467889041)
XLA Ops:
  0.6 1.5 %pack.1 = (bf16[4,64,256]{2,1,0:T(8,128)(2,1)S(1)}, bf16[4,64,256]{2,1,0:T(8,128)(2,1)S(1)}, bf16[4,64,256]{2,1,0:T(8,128)(2,1)S(1)}, bf16[4,64,256]{2,1,0:T(8,1...) custom-call(bf16[64,2048]{1,0:T(8,128)(2,1)} %refs_0_.1, ...), custom_call_target="tpu_custom_call" | custom-call | tf_op jit(solution)/shard_map/pack/pallas_call | solution.py:112
  2.1 0.1 collective-permute-start
  2.2 1.7 %collective-permute-start.1 = (bf16[256,256]{1,0:T(8,128)(2,1)S(1)}, bf16[256,256]{1,0:T(8,128)(2,1)S(1)}, u32[]{:S(2)}, u32[]{:S(2)}) collective-permute-start(bf16[256,256]{1,0:T(8,128)(2,1)S(1)} %bitcast.82), channel_id=1, source_target_pairs={{0,7},{1,0},{2,1},{3,2},{4,3},{5,4},{6,5},{7,6},{8,9},{9,10},{10,1... | collective-permute-start | bytes 393224 | tf_op jit(solution)/shard_map/ppermute | solution.py:67
  3.9 6.1 %collective-permute-start.2 = (bf16[256,256]{1,0:T(8,128)(2,1)S(1)}, bf16[256,256]{1,0:T(8,128)(2,1)S(1)}, u32[]{:S(2)}, u32[]{:S(2)}) collective-permute-start(bf16[256,256]{1,0:T(8,128)(2,1)S(1)} %bitcast.80), channel_id=1, source_target_pairs={{0,2},{1,3},{2,4},{3,5},{4,6},{5,7},{6,0},{7,1},{8,14},{9,15},{10,... | collective-permute-start | bytes 393224 | tf_op jit(solution)/shard_map/ppermute | solution.py:67
  10.0 0.0 collective-permute-start.3
  10.0 2.8 %collective-permute-start.4 = (bf16[256,256]{1,0:T(8,128)(2,1)S(1)}, bf16[256,256]{1,0:T(8,128)(2,1)S(1)}, u32[]{:S(2)}, u32[]{:S(2)}) collective-permute-start(bf16[256,256]{1,0:T(8,128)(2,1)S(1)} %bitcast.77), channel_id=1, source_target_pairs={{0,3},{1,4},{2,5},{3,6},{4,7},{5,0},{6,1},{7,2},{8,13},{9,14},{10,... | collective-permute-start | bytes 393224 | tf_op jit(solution)/shard_map/ppermute | solution.py:67
  12.8 1.7 %collective-permute-start.5 = (bf16[256,256]{1,0:T(8,128)(2,1)S(1)}, bf16[256,256]{1,0:T(8,128)(2,1)S(1)}, u32[]{:S(2)}, u32[]{:S(2)}) collective-permute-start(bf16[256,256]{1,0:T(8,128)(2,1)S(1)} %bitcast.75), channel_id=1, source_target_pairs={{0,5},{1,6},{2,7},{3,0},{4,1},{5,2},{6,3},{7,4},{8,11},{9,12},{10,... | collective-permute-start | bytes 393224 | tf_op jit(solution)/shard_map/ppermute | solution.py:67
  14.5 2.1 %collective-permute-start.6 = (bf16[256,256]{1,0:T(8,128)(2,1)S(1)}, bf16[256,256]{1,0:T(8,128)(2,1)S(1)}, u32[]{:S(2)}, u32[]{:S(2)}) collective-permute-start(bf16[256,256]{1,0:T(8,128)(2,1)S(1)} %bitcast.73), channel_id=1, source_target_pairs={{0,4},{1,5},{2,6},{3,7},{4,0},{5,1},{6,2},{7,3},{8,12},{9,13},{10,... | collective-permute-start | bytes 393224 | tf_op jit(solution)/shard_map/ppermute | solution.py:67
  16.6 0.0 collective-permute-done.2
  16.6 2.8 %collective-permute-done.3 = bf16[256,256]{1,0:T(8,128)(2,1)S(1)} collective-permute-done((bf16[256,256]{1,0:T(8,128)(2,1)S(1)}, bf16[256,256]{1,0:T(8,128)(2,1)S(1)}, u32[]{:S(2)}, u32[]{:S(2)}) %collective-permute-start.3) | collective-permute-done | bytes 131104 | tf_op jit(solution)/shard_map/ppermute | solution.py:67
  19.3 0.0 collective-permute-done.4
  19.4 5.3 %collective-permute-done.5 = bf16[256,256]{1,0:T(8,128)(2,1)S(1)} collective-permute-done((bf16[256,256]{1,0:T(8,128)(2,1)S(1)}, bf16[256,256]{1,0:T(8,128)(2,1)S(1)}, u32[]{:S(2)}, u32[]{:S(2)}) %collective-permute-start.5) | collective-permute-done | bytes 131104 | tf_op jit(solution)/shard_map/ppermute | solution.py:67
  24.7 7.3 %collective-permute-done.6 = bf16[256,256]{1,0:T(8,128)(2,1)S(1)} collective-permute-done((bf16[256,256]{1,0:T(8,128)(2,1)S(1)}, bf16[256,256]{1,0:T(8,128)(2,1)S(1)}, u32[]{:S(2)}, u32[]{:S(2)}) %collective-permute-start.6) | collective-permute-done | bytes 131104 | tf_op jit(solution)/shard_map/ppermute | solution.py:67
  32.0 0.8 pick_blocks.1
  32.8 1.9 %collective-permute-start.7 = (bf16[4,2,64,256]{3,2,1,0:T(8,128)(2,1)S(1)}, bf16[4,2,64,256]{3,2,1,0:T(8,128)(2,1)S(1)}, u32[]{:S(2)}, u32[]{:S(2)}) collective-permute-start(bf16[4,2,64,256]{3,2,1,0:T(8,128)(2,1)S(1)} %get-tuple-element.49), channel_id=1, source_target_pairs={{0,8},{8,0},{16,24},{24,16},{32,40},{40,32},{48,56},{56,48},{64,72... | collective-permute-start | bytes 786440 | tf_op jit(solution)/shard_map/ppermute | solution.py:44
  34.6 2.4 %collective-permute-start.8 = (bf16[4,2,64,256]{3,2,1,0:T(8,128)(2,1)S(1)}, bf16[4,2,64,256]{3,2,1,0:T(8,128)(2,1)S(1)}, u32[]{:S(2)}, u32[]{:S(2)}) collective-permute-start(bf16[4,2,64,256]{3,2,1,0:T(8,128)(2,1)S(1)} %get-tuple-element.49), channel_id=1, source_target_pairs={{8,16},{16,8},{24,32},{32,24},{40,48},{48,40},{56,64},{64,56},{72,... | collective-permute-start | bytes 786440 | tf_op jit(solution)/shard_map/ppermute | solution.py:44
  37.0 1.0 %collective-permute-start.9 = (bf16[2,2,64,256]{3,2,1,0:T(8,128)(2,1)S(1)}, bf16[2,2,64,256]{3,2,1,0:T(8,128)(2,1)S(1)}, u32[]{:S(2)}, u32[]{:S(2)}) collective-permute-start(bf16[2,2,64,256]{3,2,1,0:T(8,128)(2,1)S(1)} %get-tuple-element.50), channel_id=1, source_target_pairs={{0,16},{16,0},{8,24},{24,8},{32,48},{48,32},{40,56},{56,40},{64,80... | collective-permute-start | bytes 393224 | tf_op jit(solution)/shard_map/ppermute | solution.py:44
  38.0 3.6 %collective-permute-start.10 = (bf16[2,2,64,256]{3,2,1,0:T(8,128)(2,1)S(1)}, bf16[2,2,64,256]{3,2,1,0:T(8,128)(2,1)S(1)}, u32[]{:S(2)}, u32[]{:S(2)}) collective-permute-start(bf16[2,2,64,256]{3,2,1,0:T(8,128)(2,1)S(1)} %get-tuple-element.50), channel_id=1, source_target_pairs={{16,32},{32,16},{24,40},{40,24},{48,64},{64,48},{56,72},{72,56},{8... | collective-permute-start | bytes 393224 | tf_op jit(solution)/shard_map/ppermute | solution.py:44
  41.6 0.9 own_scores.1
  42.5 1.9 %collective-permute-done.8.refs_9_ = bf16[4,2,64,256]{3,2,1,0:T(8,128)(2,1)S(1)} collective-permute-done((bf16[4,2,64,256]{3,2,1,0:T(8,128)(2,1)S(1)}, bf16[4,2,64,256]{3,2,1,0:T(8,128)(2,1)S(1)}, u32[]{:S(2)}, u32[]{:S(2)}) %collective-permute-start.8) | collective-permute-done | bytes 262176 | tf_op jit(solution)/shard_map/ppermute | solution.py:44
  44.4 0.9 near_scores.1
  45.3 1.9 %collective-permute-done.10.refs_9_.refs_11_ = bf16[2,2,64,256]{3,2,1,0:T(8,128)(2,1)S(1)} collective-permute-done((bf16[2,2,64,256]{3,2,1,0:T(8,128)(2,1)S(1)}, bf16[2,2,64,256]{3,2,1,0:T(8,128)(2,1)S(1)}, u32[]{:S(2)}, u32[]{:S(2)}) %collective-permute-start.10) | collective-permute-done | bytes 131104 | tf_op jit(solution)/shard_map/ppermute | solution.py:44
  47.2 1.9 %remote_part.1 = (f32[2,8,512]{2,1,0:T(8,128)S(1)}, bf16[4,2,64,256]{3,2,1,0:T(8,128)(2,1)S(1)}, bf16[4,2,64,256]{3,2,1,0:T(8,128)(2,1)S(1)}, bf16[2,2,64,256]{3...) custom-call(bf16[4,64,256]{2,1,0:T(8,128)(2,1)S(1)} %get-tuple-eleme, ...), custom_call_target="tpu_custom_call" | custom-call | tf_op jit(solution)/shard_map/remote_part/pallas_call | solution.py:286
  49.2 0.8 collective-permute-start.11
  50.0 3.5 %collective-permute-start.12 = (bf16[4,2,64,256]{3,2,1,0:T(8,128)(2,1)S(1)}, bf16[4,2,64,256]{3,2,1,0:T(8,128)(2,1)S(1)}, u32[]{:S(2)}, u32[]{:S(2)}) collective-permute-start(bf16[4,2,64,256]{3,2,1,0:T(8,128)(2,1)S(1)} %get-tuple-element.63), channel_id=1, source_target_pairs={{8,16},{16,8},{24,32},{32,24},{40,48},{48,40},{56,64},{64,56},{72,... | collective-permute-start | bytes 786440 | tf_op jit(solution)/shard_map/ppermute | solution.py:44
  53.5 0.1 collective-permute-start.13
  53.6 2.2 %collective-permute-start.14 = (bf16[2,2,64,256]{3,2,1,0:T(8,128)(2,1)S(1)}, bf16[2,2,64,256]{3,2,1,0:T(8,128)(2,1)S(1)}, u32[]{:S(2)}, u32[]{:S(2)}) collective-permute-start(bf16[2,2,64,256]{3,2,1,0:T(8,128)(2,1)S(1)} %get-tuple-element.65), channel_id=1, source_target_pairs={{16,32},{32,16},{24,40},{40,24},{48,64},{64,48},{56,72},{72,56},{8... | collective-permute-start | bytes 393224 | tf_op jit(solution)/shard_map/ppermute | solution.py:44
  55.8 1.5 %own_grads.1 = (bf16[8,2,64,256]{3,2,1,0:T(8,128)(2,1)S(1)}, f32[8,2,64,256]{3,2,1,0:T(8,128)S(1)}) custom-call(bf16[4,64,256]{2,1,0:T(8,128)(2,1)S(1)} %get-tuple-element.41.refs_0_, bf16[4,64,256]{2,1,0:T(8,128)(2,1)S(1)} %bitcast.33, bf16[4,64,256]{2,1,0:T(8,128)(2,1)S(1)} %bitcast.38, bf16[4,64,256]{2,1,0:T(8,128)(2,1)S(1)} %bitcast.43, ...), custom_call_target="tpu_custom_call" | custom-call | tf_op jit(solution)/shard_map/own_grads/pallas_call | solution.py:327
  57.3 2.8 %collective-permute-done.13.a2_ref = bf16[2,2,64,256]{3,2,1,0:T(8,128)(2,1)S(1)} collective-permute-done((bf16[2,2,64,256]{3,2,1,0:T(8,128)(2,1)S(1)}, bf16[2,2,64,256]{3,2,1,0:T(8,128)(2,1)S(1)}, u32[]{:S(2)}, u32[]{:S(2)}) %collective-permute-start.13) | collective-permute-done | bytes 131104 | tf_op jit(solution)/shard_map/ppermute | solution.py:44
  60.1 2.5 %collective-permute-done.14.b2_ref = bf16[2,2,64,256]{3,2,1,0:T(8,128)(2,1)S(1)} collective-permute-done((bf16[2,2,64,256]{3,2,1,0:T(8,128)(2,1)S(1)}, bf16[2,2,64,256]{3,2,1,0:T(8,128)(2,1)S(1)}, u32[]{:S(2)}, u32[]{:S(2)}) %collective-permute-start.14) | collective-permute-done | bytes 131104 | tf_op jit(solution)/shard_map/ppermute | solution.py:44
  62.6 0.0 collective-permute-done.11.a1_ref
  62.6 0.0 collective-permute-done.12.b1_ref
  62.6 1.0 %add_returned.1 = (bf16[4,64,256]{2,1,0:T(8,128)(2,1)S(1)}, bf16[4,64,256]{2,1,0:T(8,128)(2,1)S(1)}, bf16[4,64,256]{2,1,0:T(8,128)(2,1)S(1)}, bf16[4,64,256]{2,1...) custom-call(s32[4,32]{1,0:T(4,128)} %bitcast.86, ...), custom_call_target="tpu_custom_call" | custom-call | tf_op jit(solution)/shard_map/add_returned/pallas_call | solution.py:355
  63.5 0.9 %collective-permute-start.15 = (bf16[256,256]{1,0:T(8,128)(2,1)S(1)}, bf16[256,256]{1,0:T(8,128)(2,1)S(1)}, u32[]{:S(2)}, u32[]{:S(2)}) collective-permute-start(bf16[256,256]{1,0:T(8,128)(2,1)S(1)} %bitcast.83), channel_id=1, source_target_pairs={{0,7},{1,0},{2,1},{3,2},{4,3},{5,4},{6,5},{7,6},{8,9},{9,10},{10,1... | collective-permute-start | bytes 393224 | tf_op jit(solution)/shard_map/ppermute | solution.py:67
  64.5 0.6 collective-permute-start.16
  65.1 0.7 collective-permute-start.17
  65.7 2.9 %collective-permute-start.18 = (bf16[256,256]{1,0:T(8,128)(2,1)S(1)}, bf16[256,256]{1,0:T(8,128)(2,1)S(1)}, u32[]{:S(2)}, u32[]{:S(2)}) collective-permute-start(bf16[256,256]{1,0:T(8,128)(2,1)S(1)} %bitcast.76), channel_id=1, source_target_pairs={{0,2},{1,3},{2,4},{3,5},{4,6},{5,7},{6,0},{7,1},{8,14},{9,15},{10,... | collective-permute-start | bytes 393224 | tf_op jit(solution)/shard_map/ppermute | solution.py:67
  68.6 0.9 %collective-permute-start.19 = (bf16[256,256]{1,0:T(8,128)(2,1)S(1)}, bf16[256,256]{1,0:T(8,128)(2,1)S(1)}, u32[]{:S(2)}, u32[]{:S(2)}) collective-permute-start(bf16[256,256]{1,0:T(8,128)(2,1)S(1)} %bitcast.74), channel_id=1, source_target_pairs={{0,5},{1,6},{2,7},{3,0},{4,1},{5,2},{6,3},{7,4},{8,11},{9,12},{10,... | collective-permute-start | bytes 393224 | tf_op jit(solution)/shard_map/ppermute | solution.py:67
  69.6 0.0 collective-permute-done.15
  69.6 3.5 %collective-permute-start.20 = (bf16[256,256]{1,0:T(8,128)(2,1)S(1)}, bf16[256,256]{1,0:T(8,128)(2,1)S(1)}, u32[]{:S(2)}, u32[]{:S(2)}) collective-permute-start(bf16[256,256]{1,0:T(8,128)(2,1)S(1)} %bitcast.72), channel_id=1, source_target_pairs={{0,3},{1,4},{2,5},{3,6},{4,7},{5,0},{6,1},{7,2},{8,13},{9,14},{10,... | collective-permute-start | bytes 393224 | tf_op jit(solution)/shard_map/ppermute | solution.py:67
  73.1 0.0 collective-permute-done.16
  73.1 2.1 %collective-permute-start.21 = (bf16[256,256]{1,0:T(8,128)(2,1)S(1)}, bf16[256,256]{1,0:T(8,128)(2,1)S(1)}, u32[]{:S(2)}, u32[]{:S(2)}) collective-permute-start(bf16[256,256]{1,0:T(8,128)(2,1)S(1)} %bitcast.71), channel_id=1, source_target_pairs={{0,4},{1,5},{2,6},{3,7},{4,0},{5,1},{6,2},{7,3},{8,12},{9,13},{10,... | collective-permute-start | bytes 393224 | tf_op jit(solution)/shard_map/ppermute | solution.py:67
  75.2 0.0 collective-permute-done.17
  75.2 0.0 collective-permute-done.18
  75.3 6.8 %collective-permute-done.19 = bf16[256,256]{1,0:T(8,128)(2,1)S(1)} collective-permute-done((bf16[256,256]{1,0:T(8,128)(2,1)S(1)}, bf16[256,256]{1,0:T(8,128)(2,1)S(1)}, u32[]{:S(2)}, u32[]{:S(2)}) %collective-permute-start.19) | collective-permute-done | bytes 131104 | tf_op jit(solution)/shard_map/ppermute | solution.py:67
  82.0 1.6 %collective-permute-done.20 = bf16[256,256]{1,0:T(8,128)(2,1)S(1)} collective-permute-done((bf16[256,256]{1,0:T(8,128)(2,1)S(1)}, bf16[256,256]{1,0:T(8,128)(2,1)S(1)}, u32[]{:S(2)}, u32[]{:S(2)}) %collective-permute-start.20) | collective-permute-done | bytes 131104 | tf_op jit(solution)/shard_map/ppermute | solution.py:67
  83.7 7.8 %collective-permute-done.21 = bf16[256,256]{1,0:T(8,128)(2,1)S(1)} collective-permute-done((bf16[256,256]{1,0:T(8,128)(2,1)S(1)}, bf16[256,256]{1,0:T(8,128)(2,1)S(1)}, u32[]{:S(2)}, u32[]{:S(2)}) %collective-permute-start.21) | collective-permute-done | bytes 131104 | tf_op jit(solution)/shard_map/ppermute | solution.py:67
  91.5 1.0 %unpack.1 = (bf16[64,2048]{1,0:T(8,128)(2,1)}, bf16[64,2048]{1,0:T(8,128)(2,1)}, bf16[64,2048]{1,0:T(8,128)(2,1)}, bf16[64,2048]{1,0:T(8,128)(2,1)}) custom-call(bf16[4,64,256]{2,1,0:T(8,128)(2,1)S(1)} %get-tuple-element.66.refs_0_, bf16[4,64,256]{2,1,0:T(8,128)(2,1)S(1)} %bitcast.64, bf16[4,64,256]{2,1,0:T(8,128)(2,1)S(1)} %bitcast.65, ...), custom_call_target="tpu_custom_call" | custom-call | tf_op jit(solution)/shard_map/unpack/pallas_call | solution.py:125
  (4 shorter events, 0.0 us)
Async XLA Ops:
  2.1 10.7 %collective-permute-start = (bf16[256,256]{1,0:T(8,128)(2,1)S(1)}, bf16[256,256]{1,0:T(8,128)(2,1)S(1)}, u32[]{:S(2)}, u32[]{:S(2)}) collective-permute-start(bf16[256,256]{1,0:T(8,128)(2,1)S(1)} %bitcast.84), channel_id=1, source_target_pairs={{0,1},{1,2},{2,3},{3,4},{4,5},{5,6},{6,7},{7,0},{8,15},{9,8},{10,9... | collective-permute-start | bytes 393224 | tf_op jit(solution)/shard_map/ppermute | solution.py:67
  2.2 12.3 %collective-permute-start.1 = (bf16[256,256]{1,0:T(8,128)(2,1)S(1)}, bf16[256,256]{1,0:T(8,128)(2,1)S(1)}, u32[]{:S(2)}, u32[]{:S(2)}) collective-permute-start(bf16[256,256]{1,0:T(8,128)(2,1)S(1)} %bitcast.82), channel_id=1, source_target_pairs={{0,7},{1,0},{2,1},{3,2},{4,3},{5,4},{6,5},{7,6},{8,9},{9,10},{10,1... | collective-permute-start | bytes 393224 | tf_op jit(solution)/shard_map/ppermute | solution.py:67
  3.9 12.6 %collective-permute-start.2 = (bf16[256,256]{1,0:T(8,128)(2,1)S(1)}, bf16[256,256]{1,0:T(8,128)(2,1)S(1)}, u32[]{:S(2)}, u32[]{:S(2)}) collective-permute-start(bf16[256,256]{1,0:T(8,128)(2,1)S(1)} %bitcast.80), channel_id=1, source_target_pairs={{0,2},{1,3},{2,4},{3,5},{4,6},{5,7},{6,0},{7,1},{8,14},{9,15},{10,... | collective-permute-start | bytes 393224 | tf_op jit(solution)/shard_map/ppermute | solution.py:67
  10.0 9.4 %collective-permute-start.3 = (bf16[256,256]{1,0:T(8,128)(2,1)S(1)}, bf16[256,256]{1,0:T(8,128)(2,1)S(1)}, u32[]{:S(2)}, u32[]{:S(2)}) collective-permute-start(bf16[256,256]{1,0:T(8,128)(2,1)S(1)} %bitcast.79), channel_id=1, source_target_pairs={{0,6},{1,7},{2,0},{3,1},{4,2},{5,3},{6,4},{7,5},{8,10},{9,11},{10,... | collective-permute-start | bytes 393224 | tf_op jit(solution)/shard_map/ppermute | solution.py:67
  10.0 9.4 %collective-permute-start.4 = (bf16[256,256]{1,0:T(8,128)(2,1)S(1)}, bf16[256,256]{1,0:T(8,128)(2,1)S(1)}, u32[]{:S(2)}, u32[]{:S(2)}) collective-permute-start(bf16[256,256]{1,0:T(8,128)(2,1)S(1)} %bitcast.77), channel_id=1, source_target_pairs={{0,3},{1,4},{2,5},{3,6},{4,7},{5,0},{6,1},{7,2},{8,13},{9,14},{10,... | collective-permute-start | bytes 393224 | tf_op jit(solution)/shard_map/ppermute | solution.py:67
  12.8 11.9 %collective-permute-start.5 = (bf16[256,256]{1,0:T(8,128)(2,1)S(1)}, bf16[256,256]{1,0:T(8,128)(2,1)S(1)}, u32[]{:S(2)}, u32[]{:S(2)}) collective-permute-start(bf16[256,256]{1,0:T(8,128)(2,1)S(1)} %bitcast.75), channel_id=1, source_target_pairs={{0,5},{1,6},{2,7},{3,0},{4,1},{5,2},{6,3},{7,4},{8,11},{9,12},{10,... | collective-permute-start | bytes 393224 | tf_op jit(solution)/shard_map/ppermute | solution.py:67
  14.5 17.5 %collective-permute-start.6 = (bf16[256,256]{1,0:T(8,128)(2,1)S(1)}, bf16[256,256]{1,0:T(8,128)(2,1)S(1)}, u32[]{:S(2)}, u32[]{:S(2)}) collective-permute-start(bf16[256,256]{1,0:T(8,128)(2,1)S(1)} %bitcast.73), channel_id=1, source_target_pairs={{0,4},{1,5},{2,6},{3,7},{4,0},{5,1},{6,2},{7,3},{8,12},{9,13},{10,... | collective-permute-start | bytes 393224 | tf_op jit(solution)/shard_map/ppermute | solution.py:67
  32.8 9.7 %collective-permute-start.7 = (bf16[4,2,64,256]{3,2,1,0:T(8,128)(2,1)S(1)}, bf16[4,2,64,256]{3,2,1,0:T(8,128)(2,1)S(1)}, u32[]{:S(2)}, u32[]{:S(2)}) collective-permute-start(bf16[4,2,64,256]{3,2,1,0:T(8,128)(2,1)S(1)} %get-tuple-element.49), channel_id=1, source_target_pairs={{0,8},{8,0},{16,24},{24,16},{32,40},{40,32},{48,56},{56,48},{64,72... | collective-permute-start | bytes 786440 | tf_op jit(solution)/shard_map/ppermute | solution.py:44
  34.6 9.8 %collective-permute-start.8 = (bf16[4,2,64,256]{3,2,1,0:T(8,128)(2,1)S(1)}, bf16[4,2,64,256]{3,2,1,0:T(8,128)(2,1)S(1)}, u32[]{:S(2)}, u32[]{:S(2)}) collective-permute-start(bf16[4,2,64,256]{3,2,1,0:T(8,128)(2,1)S(1)} %get-tuple-element.49), channel_id=1, source_target_pairs={{8,16},{16,8},{24,32},{32,24},{40,48},{48,40},{56,64},{64,56},{72,... | collective-permute-start | bytes 786440 | tf_op jit(solution)/shard_map/ppermute | solution.py:44
  37.0 8.3 %collective-permute-start.9 = (bf16[2,2,64,256]{3,2,1,0:T(8,128)(2,1)S(1)}, bf16[2,2,64,256]{3,2,1,0:T(8,128)(2,1)S(1)}, u32[]{:S(2)}, u32[]{:S(2)}) collective-permute-start(bf16[2,2,64,256]{3,2,1,0:T(8,128)(2,1)S(1)} %get-tuple-element.50), channel_id=1, source_target_pairs={{0,16},{16,0},{8,24},{24,8},{32,48},{48,32},{40,56},{56,40},{64,80... | collective-permute-start | bytes 393224 | tf_op jit(solution)/shard_map/ppermute | solution.py:44
  38.0 9.2 %collective-permute-start.10 = (bf16[2,2,64,256]{3,2,1,0:T(8,128)(2,1)S(1)}, bf16[2,2,64,256]{3,2,1,0:T(8,128)(2,1)S(1)}, u32[]{:S(2)}, u32[]{:S(2)}) collective-permute-start(bf16[2,2,64,256]{3,2,1,0:T(8,128)(2,1)S(1)} %get-tuple-element.50), channel_id=1, source_target_pairs={{16,32},{32,16},{24,40},{40,24},{48,64},{64,48},{56,72},{72,56},{8... | collective-permute-start | bytes 393224 | tf_op jit(solution)/shard_map/ppermute | solution.py:44
  49.2 13.4 %collective-permute-start.11 = (bf16[4,2,64,256]{3,2,1,0:T(8,128)(2,1)S(1)}, bf16[4,2,64,256]{3,2,1,0:T(8,128)(2,1)S(1)}, u32[]{:S(2)}, u32[]{:S(2)}) collective-permute-start(bf16[4,2,64,256]{3,2,1,0:T(8,128)(2,1)S(1)} %get-tuple-element.62), channel_id=1, source_target_pairs={{0,8},{8,0},{16,24},{24,16},{32,40},{40,32},{48,56},{56,48},{64,72... | collective-permute-start | bytes 786440 | tf_op jit(solution)/shard_map/ppermute | solution.py:44
  50.0 12.6 %collective-permute-start.12 = (bf16[4,2,64,256]{3,2,1,0:T(8,128)(2,1)S(1)}, bf16[4,2,64,256]{3,2,1,0:T(8,128)(2,1)S(1)}, u32[]{:S(2)}, u32[]{:S(2)}) collective-permute-start(bf16[4,2,64,256]{3,2,1,0:T(8,128)(2,1)S(1)} %get-tuple-element.63), channel_id=1, source_target_pairs={{8,16},{16,8},{24,32},{32,24},{40,48},{48,40},{56,64},{64,56},{72,... | collective-permute-start | bytes 786440 | tf_op jit(solution)/shard_map/ppermute | solution.py:44
  53.5 6.6 %collective-permute-start.13 = (bf16[2,2,64,256]{3,2,1,0:T(8,128)(2,1)S(1)}, bf16[2,2,64,256]{3,2,1,0:T(8,128)(2,1)S(1)}, u32[]{:S(2)}, u32[]{:S(2)}) collective-permute-start(bf16[2,2,64,256]{3,2,1,0:T(8,128)(2,1)S(1)} %get-tuple-element.64), channel_id=1, source_target_pairs={{0,16},{16,0},{8,24},{24,8},{32,48},{48,32},{40,56},{56,40},{64,80... | collective-permute-start | bytes 393224 | tf_op jit(solution)/shard_map/ppermute | solution.py:44
  53.6 9.0 %collective-permute-start.14 = (bf16[2,2,64,256]{3,2,1,0:T(8,128)(2,1)S(1)}, bf16[2,2,64,256]{3,2,1,0:T(8,128)(2,1)S(1)}, u32[]{:S(2)}, u32[]{:S(2)}) collective-permute-start(bf16[2,2,64,256]{3,2,1,0:T(8,128)(2,1)S(1)} %get-tuple-element.65), channel_id=1, source_target_pairs={{16,32},{32,16},{24,40},{40,24},{48,64},{64,48},{56,72},{72,56},{8... | collective-permute-start | bytes 393224 | tf_op jit(solution)/shard_map/ppermute | solution.py:44
  63.5 6.1 %collective-permute-start.15 = (bf16[256,256]{1,0:T(8,128)(2,1)S(1)}, bf16[256,256]{1,0:T(8,128)(2,1)S(1)}, u32[]{:S(2)}, u32[]{:S(2)}) collective-permute-start(bf16[256,256]{1,0:T(8,128)(2,1)S(1)} %bitcast.83), channel_id=1, source_target_pairs={{0,7},{1,0},{2,1},{3,2},{4,3},{5,4},{6,5},{7,6},{8,9},{9,10},{10,1... | collective-permute-start | bytes 393224 | tf_op jit(solution)/shard_map/ppermute | solution.py:67
  64.5 8.7 %collective-permute-start.16 = (bf16[256,256]{1,0:T(8,128)(2,1)S(1)}, bf16[256,256]{1,0:T(8,128)(2,1)S(1)}, u32[]{:S(2)}, u32[]{:S(2)}) collective-permute-start(bf16[256,256]{1,0:T(8,128)(2,1)S(1)} %bitcast.81), channel_id=1, source_target_pairs={{0,1},{1,2},{2,3},{3,4},{4,5},{5,6},{6,7},{7,0},{8,15},{9,8},{10,9... | collective-permute-start | bytes 393224 | tf_op jit(solution)/shard_map/ppermute | solution.py:67
  65.1 10.2 %collective-permute-start.17 = (bf16[256,256]{1,0:T(8,128)(2,1)S(1)}, bf16[256,256]{1,0:T(8,128)(2,1)S(1)}, u32[]{:S(2)}, u32[]{:S(2)}) collective-permute-start(bf16[256,256]{1,0:T(8,128)(2,1)S(1)} %bitcast.78), channel_id=1, source_target_pairs={{0,6},{1,7},{2,0},{3,1},{4,2},{5,3},{6,4},{7,5},{8,10},{9,11},{10,... | collective-permute-start | bytes 393224 | tf_op jit(solution)/shard_map/ppermute | solution.py:67
  65.7 9.5 %collective-permute-start.18 = (bf16[256,256]{1,0:T(8,128)(2,1)S(1)}, bf16[256,256]{1,0:T(8,128)(2,1)S(1)}, u32[]{:S(2)}, u32[]{:S(2)}) collective-permute-start(bf16[256,256]{1,0:T(8,128)(2,1)S(1)} %bitcast.76), channel_id=1, source_target_pairs={{0,2},{1,3},{2,4},{3,5},{4,6},{5,7},{6,0},{7,1},{8,14},{9,15},{10,... | collective-permute-start | bytes 393224 | tf_op jit(solution)/shard_map/ppermute | solution.py:67
  68.6 13.4 %collective-permute-start.19 = (bf16[256,256]{1,0:T(8,128)(2,1)S(1)}, bf16[256,256]{1,0:T(8,128)(2,1)S(1)}, u32[]{:S(2)}, u32[]{:S(2)}) collective-permute-start(bf16[256,256]{1,0:T(8,128)(2,1)S(1)} %bitcast.74), channel_id=1, source_target_pairs={{0,5},{1,6},{2,7},{3,0},{4,1},{5,2},{6,3},{7,4},{8,11},{9,12},{10,... | collective-permute-start | bytes 393224 | tf_op jit(solution)/shard_map/ppermute | solution.py:67
  69.6 14.1 %collective-permute-start.20 = (bf16[256,256]{1,0:T(8,128)(2,1)S(1)}, bf16[256,256]{1,0:T(8,128)(2,1)S(1)}, u32[]{:S(2)}, u32[]{:S(2)}) collective-permute-start(bf16[256,256]{1,0:T(8,128)(2,1)S(1)} %bitcast.72), channel_id=1, source_target_pairs={{0,3},{1,4},{2,5},{3,6},{4,7},{5,0},{6,1},{7,2},{8,13},{9,14},{10,... | collective-permute-start | bytes 393224 | tf_op jit(solution)/shard_map/ppermute | solution.py:67
  73.1 18.3 %collective-permute-start.21 = (bf16[256,256]{1,0:T(8,128)(2,1)S(1)}, bf16[256,256]{1,0:T(8,128)(2,1)S(1)}, u32[]{:S(2)}, u32[]{:S(2)}) collective-permute-start(bf16[256,256]{1,0:T(8,128)(2,1)S(1)} %bitcast.71), channel_id=1, source_target_pairs={{0,4},{1,5},{2,6},{3,7},{4,0},{5,1},{6,2},{7,3},{8,12},{9,13},{10,... | collective-permute-start | bytes 393224 | tf_op jit(solution)/shard_map/ppermute | solution.py:67

commit v5 on v3

--- a/solution.py
+++ b/solution.py
@@ -84,23 +84,20 @@
     piece = width // parts
 
     def body(*refs):
-        in_refs, out_refs, sem = refs[:count], refs[count:-1], refs[-1]
-        copies = []
-        for k, out_ref in enumerate(out_refs):
-            for i, ref in enumerate(in_refs):
-                copies.append(
-                    pltpu.make_async_copy(ref.at[:, columns_of(k, piece)], out_ref.at[i], sem.at[k, i])
-                )
+        in_refs, out_refs, (held, sem) = refs[:count], refs[count:-2], refs[-2:]
+        copies = [pltpu.make_async_copy(ref, held.at[i], sem.at[i]) for i, ref in enumerate(in_refs)]
         for copy in copies:
             copy.start()
-        for copy in copies:
+        for i, copy in enumerate(copies):
             copy.wait()
+            for k, out_ref in enumerate(out_refs):
+                out_ref[i] = held[i, :, columns_of(k, piece)]
 
     shape = jax.ShapeDtypeStruct((count, rows, piece), arrays[0].dtype)
     anywhere = pl.BlockSpec(memory_space=pltpu.HBM)
     arrays = [pltpu.with_memory_space_constraint(array, pltpu.HBM) for array in arrays]
-    sems = [pltpu.SemaphoreType.DMA((parts, count))]
-    return call(body, [shape] * parts, [anywhere] * count, [VM] * parts, "pack", 4, sems)(*arrays)
+    scratch = [pltpu.VMEM((count, rows, width), arrays[0].dtype), pltpu.SemaphoreType.DMA((count,))]
+    return call(body, [shape] * parts, [anywhere] * count, [VM] * parts, "pack", 4, scratch)(*arrays)
 
 
 def unpack(pieces):

time: 92.5 us -> 92.2 us (level)
  no operation moved by 1% of the time
where the time goes in v5:
time: 92.2 us; the launch traced here: 90.9 us
  starting transfers between devices  48.1 us (52%)
  waiting for transfers between devices  32.4 us (35%)
  Pallas kernels  9.62 us (10%)
    ppermute x14, starting transfers between devices, head_shifts(): lax.ppermute(flat, 'head', [(i, (i + sign * by) % length) for i in range(...  32.4 us
    ppermute x14, waiting for transfers between devices, head_shifts(): lax.ppermute(flat, 'head', [(i, (i + sign * by) % length) for i in range(...  23.8 us
    ppermute x8, starting transfers between devices, swapped(): return lax.ppermute(array, 'frame', pairs)  15.7 us
    ppermute x8, waiting for transfers between devices, swapped(): return lax.ppermute(array, 'frame', pairs)  8.62 us
    pallas_call x1, Pallas kernels, remote_part(): call(body, outs, [VM] * (parts + 5), [VM] * 13, 'remote_part', 24)  3.03 us
  transfers between devices with their start and end apart: 22, of which 12 were waited for; matrix products, arithmetic and copies ran while one was open for 0% of the time, Pallas kernels for 3%

profile of v5, /device:TPU:4, one launch (start us, length us, event | category | flops | bytes accessed | tf_op | source)
XLA Modules:
  0.0 90.9 jit_solution(13222299886174401181)
XLA Ops:
  0.6 1.3 %pack.1 = (bf16[4,64,256]{2,1,0:T(8,128)(2,1)S(1)}, bf16[4,64,256]{2,1,0:T(8,128)(2,1)S(1)}, bf16[4,64,256]{2,1,0:T(8,128)(2,1)S(1)}, bf16[4,64,256]{2,1,0:T(8,1...) custom-call(bf16[64,2048]{1,0:T(8,128)(2,1)} %refs_0_.1, ...), custom_call_target="tpu_custom_call" | custom-call | tf_op jit(solution)/shard_map/pack/pallas_call | solution.py:100
  1.9 5.9 %collective-permute-start.1 = (bf16[256,256]{1,0:T(8,128)(2,1)S(1)}, bf16[256,256]{1,0:T(8,128)(2,1)S(1)}, u32[]{:S(2)}, u32[]{:S(2)}) collective-permute-start(bf16[256,256]{1,0:T(8,128)(2,1)S(1)} %bitcast.77), channel_id=1, source_target_pairs={{0,7},{1,0},{2,1},{3,2},{4,3},{5,4},{6,5},{7,6},{8,15},{9,8},{10,9... | collective-permute-start | bytes 393224 | tf_op jit(solution)/shard_map/ppermute | solution.py:61
  7.8 0.0 collective-permute-start.2
  7.8 4.1 %collective-permute-start.3 = (bf16[256,256]{1,0:T(8,128)(2,1)S(1)}, bf16[256,256]{1,0:T(8,128)(2,1)S(1)}, u32[]{:S(2)}, u32[]{:S(2)}) collective-permute-start(bf16[256,256]{1,0:T(8,128)(2,1)S(1)} %bitcast.72), channel_id=1, source_target_pairs={{0,6},{1,7},{2,0},{3,1},{4,2},{5,3},{6,4},{7,5},{8,14},{9,15},{10,... | collective-permute-start | bytes 393224 | tf_op jit(solution)/shard_map/ppermute | solution.py:61
  12.0 0.8 collective-permute-start.4
  12.8 4.2 %collective-permute-start.5 = (bf16[256,256]{1,0:T(8,128)(2,1)S(1)}, bf16[256,256]{1,0:T(8,128)(2,1)S(1)}, u32[]{:S(2)}, u32[]{:S(2)}) collective-permute-start(bf16[256,256]{1,0:T(8,128)(2,1)S(1)} %bitcast.68), channel_id=1, source_target_pairs={{0,5},{1,6},{2,7},{3,0},{4,1},{5,2},{6,3},{7,4},{8,13},{9,14},{10,... | collective-permute-start | bytes 393224 | tf_op jit(solution)/shard_map/ppermute | solution.py:61
  17.0 0.5 collective-permute-done
  17.5 2.9 %collective-permute-start.6 = (bf16[256,256]{1,0:T(8,128)(2,1)S(1)}, bf16[256,256]{1,0:T(8,128)(2,1)S(1)}, u32[]{:S(2)}, u32[]{:S(2)}) collective-permute-start(bf16[256,256]{1,0:T(8,128)(2,1)S(1)} %bitcast.66), channel_id=1, source_target_pairs={{0,4},{1,5},{2,6},{3,7},{4,0},{5,1},{6,2},{7,3},{8,12},{9,13},{10,... | collective-permute-start | bytes 393224 | tf_op jit(solution)/shard_map/ppermute | solution.py:61
  20.4 1.1 %collective-permute-done.2 = bf16[256,256]{1,0:T(8,128)(2,1)S(1)} collective-permute-done((bf16[256,256]{1,0:T(8,128)(2,1)S(1)}, bf16[256,256]{1,0:T(8,128)(2,1)S(1)}, u32[]{:S(2)}, u32[]{:S(2)}) %collective-permute-start.2) | collective-permute-done | bytes 131104 | tf_op jit(solution)/shard_map/ppermute | solution.py:61
  21.5 0.0 collective-permute-done.3
  21.5 7.8 %collective-permute-done.4 = bf16[256,256]{1,0:T(8,128)(2,1)S(1)} collective-permute-done((bf16[256,256]{1,0:T(8,128)(2,1)S(1)}, bf16[256,256]{1,0:T(8,128)(2,1)S(1)}, u32[]{:S(2)}, u32[]{:S(2)}) %collective-permute-start.4) | collective-permute-done | bytes 131104 | tf_op jit(solution)/shard_map/ppermute | solution.py:61
  29.3 1.8 %collective-permute-done.5 = bf16[256,256]{1,0:T(8,128)(2,1)S(1)} collective-permute-done((bf16[256,256]{1,0:T(8,128)(2,1)S(1)}, bf16[256,256]{1,0:T(8,128)(2,1)S(1)}, u32[]{:S(2)}, u32[]{:S(2)}) %collective-permute-start.5) | collective-permute-done | bytes 131104 | tf_op jit(solution)/shard_map/ppermute | solution.py:61
  31.1 0.0 collective-permute-done.6
  31.1 0.8 pick_blocks.1
  31.8 1.9 %collective-permute-start.8 = (bf16[4,2,64,256]{3,2,1,0:T(8,128)(2,1)S(1)}, bf16[4,2,64,256]{3,2,1,0:T(8,128)(2,1)S(1)}, u32[]{:S(2)}, u32[]{:S(2)}) collective-permute-start(bf16[4,2,64,256]{3,2,1,0:T(8,128)(2,1)S(1)} %get-tuple-element.52), channel_id=1, source_target_pairs={{8,16},{16,8},{24,32},{32,24},{40,48},{48,40},{56,64},{64,56},{72,... | collective-permute-start | bytes 786440 | tf_op jit(solution)/shard_map/ppermute | solution.py:42
  33.8 1.8 %collective-permute-start.7 = (bf16[4,2,64,256]{3,2,1,0:T(8,128)(2,1)S(1)}, bf16[4,2,64,256]{3,2,1,0:T(8,128)(2,1)S(1)}, u32[]{:S(2)}, u32[]{:S(2)}) collective-permute-start(bf16[4,2,64,256]{3,2,1,0:T(8,128)(2,1)S(1)} %get-tuple-element.52), channel_id=1, source_target_pairs={{0,8},{8,0},{16,24},{24,16},{32,40},{40,32},{48,56},{56,48},{64,72... | collective-permute-start | bytes 786440 | tf_op jit(solution)/shard_map/ppermute | solution.py:42
  35.5 4.5 %collective-permute-start.10 = (bf16[2,2,64,256]{3,2,1,0:T(8,128)(2,1)S(1)}, bf16[2,2,64,256]{3,2,1,0:T(8,128)(2,1)S(1)}, u32[]{:S(2)}, u32[]{:S(2)}) collective-permute-start(bf16[2,2,64,256]{3,2,1,0:T(8,128)(2,1)S(1)} %get-tuple-element.53), channel_id=1, source_target_pairs={{16,32},{32,16},{24,40},{40,24},{48,64},{64,48},{56,72},{72,56},{8... | collective-permute-start | bytes 393224 | tf_op jit(solution)/shard_map/ppermute | solution.py:42
  40.0 0.4 collective-permute-start.9
  40.4 0.9 own_scores.1
  41.2 3.7 %collective-permute-done.10.refs_11_ = bf16[2,2,64,256]{3,2,1,0:T(8,128)(2,1)S(1)} collective-permute-done((bf16[2,2,64,256]{3,2,1,0:T(8,128)(2,1)S(1)}, bf16[2,2,64,256]{3,2,1,0:T(8,128)(2,1)S(1)}, u32[]{:S(2)}, u32[]{:S(2)}) %collective-permute-start.10) | collective-permute-done | bytes 131104 | tf_op jit(solution)/shard_map/ppermute | solution.py:42
  44.9 0.3 collective-permute-done.9.refs_10_
  45.2 0.0 collective-permute-done.8.refs_9_
  45.2 0.0 collective-permute-done.7.refs_8_
  45.2 3.0 %remote_part.1 = (f32[2,8,512]{2,1,0:T(8,128)S(1)}, bf16[4,2,64,256]{3,2,1,0:T(8,128)(2,1)S(1)}, bf16[4,2,64,256]{3,2,1,0:T(8,128)(2,1)S(1)}, bf16[2,2,64,256]{3...) custom-call(bf16[4,64,256]{2,1,0:T(8,128)(2,1)S(1)} %get-tuple-eleme, ...), custom_call_target="tpu_custom_call" | custom-call | tf_op jit(solution)/shard_map/remote_part/pallas_call | solution.py:242
  48.3 0.1 collective-permute-start.11
  48.4 4.3 %collective-permute-start.12 = (bf16[4,2,64,256]{3,2,1,0:T(8,128)(2,1)S(1)}, bf16[4,2,64,256]{3,2,1,0:T(8,128)(2,1)S(1)}, u32[]{:S(2)}, u32[]{:S(2)}) collective-permute-start(bf16[4,2,64,256]{3,2,1,0:T(8,128)(2,1)S(1)} %get-tuple-element.69), channel_id=1, source_target_pairs={{8,16},{16,8},{24,32},{32,24},{40,48},{48,40},{56,64},{64,56},{72,... | collective-permute-start | bytes 786440 | tf_op jit(solution)/shard_map/ppermute | solution.py:42
  52.7 0.1 collective-permute-start.13
  52.8 2.7 %collective-permute-start.14 = (bf16[2,2,64,256]{3,2,1,0:T(8,128)(2,1)S(1)}, bf16[2,2,64,256]{3,2,1,0:T(8,128)(2,1)S(1)}, u32[]{:S(2)}, u32[]{:S(2)}) collective-permute-start(bf16[2,2,64,256]{3,2,1,0:T(8,128)(2,1)S(1)} %get-tuple-element.71), channel_id=1, source_target_pairs={{16,32},{32,16},{24,40},{40,24},{48,64},{64,48},{56,72},{72,56},{8... | collective-permute-start | bytes 393224 | tf_op jit(solution)/shard_map/ppermute | solution.py:42
  55.4 1.6 %own_grads.1 = (bf16[8,2,64,256]{3,2,1,0:T(8,128)(2,1)S(1)}, f32[8,2,64,256]{3,2,1,0:T(8,128)S(1)}) custom-call(bf16[4,64,256]{2,1,0:T(8,128)(2,1)S(1)} %get-tuple-element.44.refs_0_, bf16[4,64,256]{2,1,0:T(8,128)(2,1)S(1)} %bitcast.36, bf16[4,64,256]{2,1,0:T(8,128)(2,1)S(1)} %bitcast.32, bf16[4,64,256]{2,1,0:T(8,128)(2,1)S(1)} %bitcast.40, ...), custom_call_target="tpu_custom_call" | custom-call | tf_op jit(solution)/shard_map/own_grads/pallas_call | solution.py:277
  57.1 2.0 %collective-permute-done.13.a2_ref = bf16[2,2,64,256]{3,2,1,0:T(8,128)(2,1)S(1)} collective-permute-done((bf16[2,2,64,256]{3,2,1,0:T(8,128)(2,1)S(1)}, bf16[2,2,64,256]{3,2,1,0:T(8,128)(2,1)S(1)}, u32[]{:S(2)}, u32[]{:S(2)}) %collective-permute-start.13) | collective-permute-done | bytes 131104 | tf_op jit(solution)/shard_map/ppermute | solution.py:42
  59.1 2.7 %collective-permute-done.14.b2_ref = bf16[2,2,64,256]{3,2,1,0:T(8,128)(2,1)S(1)} collective-permute-done((bf16[2,2,64,256]{3,2,1,0:T(8,128)(2,1)S(1)}, bf16[2,2,64,256]{3,2,1,0:T(8,128)(2,1)S(1)}, u32[]{:S(2)}, u32[]{:S(2)}) %collective-permute-start.14) | collective-permute-done | bytes 131104 | tf_op jit(solution)/shard_map/ppermute | solution.py:42
  61.7 0.0 collective-permute-done.12.b1_ref
  61.7 1.0 %add_returned.1 = (bf16[4,64,256]{2,1,0:T(8,128)(2,1)S(1)}, bf16[4,64,256]{2,1,0:T(8,128)(2,1)S(1)}, bf16[4,64,256]{2,1,0:T(8,128)(2,1)S(1)}, bf16[4,64,256]{2,1...) custom-call(s32[4,32]{1,0:T(4,128)} %bitcast.79, ...), custom_call_target="tpu_custom_call" | custom-call | tf_op jit(solution)/shard_map/add_returned/pallas_call | solution.py:305
  62.7 2.3 %collective-permute-start.15 = (bf16[256,256]{1,0:T(8,128)(2,1)S(1)}, bf16[256,256]{1,0:T(8,128)(2,1)S(1)}, u32[]{:S(2)}, u32[]{:S(2)}) collective-permute-start(bf16[256,256]{1,0:T(8,128)(2,1)S(1)} %bitcast.76), channel_id=1, source_target_pairs={{0,7},{1,0},{2,1},{3,2},{4,3},{5,4},{6,5},{7,6},{8,15},{9,8},{10,9... | collective-permute-start | bytes 393224 | tf_op jit(solution)/shard_map/ppermute | solution.py:61
  65.0 2.6 %collective-permute-start.16 = (bf16[256,256]{1,0:T(8,128)(2,1)S(1)}, bf16[256,256]{1,0:T(8,128)(2,1)S(1)}, u32[]{:S(2)}, u32[]{:S(2)}) collective-permute-start(bf16[256,256]{1,0:T(8,128)(2,1)S(1)} %bitcast.74), channel_id=1, source_target_pairs={{0,1},{1,2},{2,3},{3,4},{4,5},{5,6},{6,7},{7,0},{8,9},{9,10},{10,1... | collective-permute-start | bytes 393224 | tf_op jit(solution)/shard_map/ppermute | solution.py:61
  67.6 1.6 %collective-permute-start.17 = (bf16[256,256]{1,0:T(8,128)(2,1)S(1)}, bf16[256,256]{1,0:T(8,128)(2,1)S(1)}, u32[]{:S(2)}, u32[]{:S(2)}) collective-permute-start(bf16[256,256]{1,0:T(8,128)(2,1)S(1)} %bitcast.71), channel_id=1, source_target_pairs={{0,6},{1,7},{2,0},{3,1},{4,2},{5,3},{6,4},{7,5},{8,14},{9,15},{10,... | collective-permute-start | bytes 393224 | tf_op jit(solution)/shard_map/ppermute | solution.py:61
  69.1 1.4 %collective-permute-start.18 = (bf16[256,256]{1,0:T(8,128)(2,1)S(1)}, bf16[256,256]{1,0:T(8,128)(2,1)S(1)}, u32[]{:S(2)}, u32[]{:S(2)}) collective-permute-start(bf16[256,256]{1,0:T(8,128)(2,1)S(1)} %bitcast.69), channel_id=1, source_target_pairs={{0,2},{1,3},{2,4},{3,5},{4,6},{5,7},{6,0},{7,1},{8,10},{9,11},{10,... | collective-permute-start | bytes 393224 | tf_op jit(solution)/shard_map/ppermute | solution.py:61
  70.5 2.7 %collective-permute-start.19 = (bf16[256,256]{1,0:T(8,128)(2,1)S(1)}, bf16[256,256]{1,0:T(8,128)(2,1)S(1)}, u32[]{:S(2)}, u32[]{:S(2)}) collective-permute-start(bf16[256,256]{1,0:T(8,128)(2,1)S(1)} %bitcast.67), channel_id=1, source_target_pairs={{0,5},{1,6},{2,7},{3,0},{4,1},{5,2},{6,3},{7,4},{8,13},{9,14},{10,... | collective-permute-start | bytes 393224 | tf_op jit(solution)/shard_map/ppermute | solution.py:61
  73.2 0.0 collective-permute-done.15
  73.2 1.1 %collective-permute-start.20 = (bf16[256,256]{1,0:T(8,128)(2,1)S(1)}, bf16[256,256]{1,0:T(8,128)(2,1)S(1)}, u32[]{:S(2)}, u32[]{:S(2)}) collective-permute-start(bf16[256,256]{1,0:T(8,128)(2,1)S(1)} %bitcast.65), channel_id=1, source_target_pairs={{0,3},{1,4},{2,5},{3,6},{4,7},{5,0},{6,1},{7,2},{8,11},{9,12},{10,... | collective-permute-start | bytes 393224 | tf_op jit(solution)/shard_map/ppermute | solution.py:61
  74.3 0.0 collective-permute-done.16
  74.3 2.8 %collective-permute-start.21 = (bf16[256,256]{1,0:T(8,128)(2,1)S(1)}, bf16[256,256]{1,0:T(8,128)(2,1)S(1)}, u32[]{:S(2)}, u32[]{:S(2)}) collective-permute-start(bf16[256,256]{1,0:T(8,128)(2,1)S(1)} %bitcast.64), channel_id=1, source_target_pairs={{0,4},{1,5},{2,6},{3,7},{4,0},{5,1},{6,2},{7,3},{8,12},{9,13},{10,... | collective-permute-start | bytes 393224 | tf_op jit(solution)/shard_map/ppermute | solution.py:61
  77.2 2.7 %collective-permute-done.17 = bf16[256,256]{1,0:T(8,128)(2,1)S(1)} collective-permute-done((bf16[256,256]{1,0:T(8,128)(2,1)S(1)}, bf16[256,256]{1,0:T(8,128)(2,1)S(1)}, u32[]{:S(2)}, u32[]{:S(2)}) %collective-permute-start.17) | collective-permute-done | bytes 131104 | tf_op jit(solution)/shard_map/ppermute | solution.py:61
  79.9 1.1 %collective-permute-done.18 = bf16[256,256]{1,0:T(8,128)(2,1)S(1)} collective-permute-done((bf16[256,256]{1,0:T(8,128)(2,1)S(1)}, bf16[256,256]{1,0:T(8,128)(2,1)S(1)}, u32[]{:S(2)}, u32[]{:S(2)}) %collective-permute-start.18) | collective-permute-done | bytes 131104 | tf_op jit(solution)/shard_map/ppermute | solution.py:61
  80.9 5.5 %collective-permute-done.19 = bf16[256,256]{1,0:T(8,128)(2,1)S(1)} collective-permute-done((bf16[256,256]{1,0:T(8,128)(2,1)S(1)}, bf16[256,256]{1,0:T(8,128)(2,1)S(1)}, u32[]{:S(2)}, u32[]{:S(2)}) %collective-permute-start.19) | collective-permute-done | bytes 131104 | tf_op jit(solution)/shard_map/ppermute | solution.py:61
  86.4 3.4 %collective-permute-done.20 = bf16[256,256]{1,0:T(8,128)(2,1)S(1)} collective-permute-done((bf16[256,256]{1,0:T(8,128)(2,1)S(1)}, bf16[256,256]{1,0:T(8,128)(2,1)S(1)}, u32[]{:S(2)}, u32[]{:S(2)}) %collective-permute-start.20) | collective-permute-done | bytes 131104 | tf_op jit(solution)/shard_map/ppermute | solution.py:61
  89.8 0.0 collective-permute-done.21
  89.8 1.1 %unpack.1 = (bf16[64,2048]{1,0:T(8,128)(2,1)}, bf16[64,2048]{1,0:T(8,128)(2,1)}, bf16[64,2048]{1,0:T(8,128)(2,1)}, bf16[64,2048]{1,0:T(8,128)(2,1)}) custom-call(bf16[4,64,256]{2,1,0:T(8,128)(2,1)S(1)} %get-tuple-element.72.refs_0_, bf16[4,64,256]{2,1,0:T(8,128)(2,1)S(1)} %bitcast.57, bf16[4,64,256]{2,1,0:T(8,128)(2,1)S(1)} %bitcast.58, ...), custom_call_target="tpu_custom_call" | custom-call | tf_op jit(solution)/shard_map/unpack/pallas_call | solution.py:113
  (3 shorter events, 0.0 us)
Async XLA Ops:
  1.9 10.9 %collective-permute-start.1 = (bf16[256,256]{1,0:T(8,128)(2,1)S(1)}, bf16[256,256]{1,0:T(8,128)(2,1)S(1)}, u32[]{:S(2)}, u32[]{:S(2)}) collective-permute-start(bf16[256,256]{1,0:T(8,128)(2,1)S(1)} %bitcast.77), channel_id=1, source_target_pairs={{0,7},{1,0},{2,1},{3,2},{4,3},{5,4},{6,5},{7,6},{8,15},{9,8},{10,9... | collective-permute-start | bytes 393224 | tf_op jit(solution)/shard_map/ppermute | solution.py:61
  7.8 9.7 %collective-permute-start = (bf16[256,256]{1,0:T(8,128)(2,1)S(1)}, bf16[256,256]{1,0:T(8,128)(2,1)S(1)}, u32[]{:S(2)}, u32[]{:S(2)}) collective-permute-start(bf16[256,256]{1,0:T(8,128)(2,1)S(1)} %bitcast.75), channel_id=1, source_target_pairs={{0,1},{1,2},{2,3},{3,4},{4,5},{5,6},{6,7},{7,0},{8,9},{9,10},{10,1... | collective-permute-start | bytes 393224 | tf_op jit(solution)/shard_map/ppermute | solution.py:61
  7.8 13.7 %collective-permute-start.2 = (bf16[256,256]{1,0:T(8,128)(2,1)S(1)}, bf16[256,256]{1,0:T(8,128)(2,1)S(1)}, u32[]{:S(2)}, u32[]{:S(2)}) collective-permute-start(bf16[256,256]{1,0:T(8,128)(2,1)S(1)} %bitcast.73), channel_id=1, source_target_pairs={{0,2},{1,3},{2,4},{3,5},{4,6},{5,7},{6,0},{7,1},{8,10},{9,11},{10,... | collective-permute-start | bytes 393224 | tf_op jit(solution)/shard_map/ppermute | solution.py:61
  7.8 13.7 %collective-permute-start.3 = (bf16[256,256]{1,0:T(8,128)(2,1)S(1)}, bf16[256,256]{1,0:T(8,128)(2,1)S(1)}, u32[]{:S(2)}, u32[]{:S(2)}) collective-permute-start(bf16[256,256]{1,0:T(8,128)(2,1)S(1)} %bitcast.72), channel_id=1, source_target_pairs={{0,6},{1,7},{2,0},{3,1},{4,2},{5,3},{6,4},{7,5},{8,14},{9,15},{10,... | collective-permute-start | bytes 393224 | tf_op jit(solution)/shard_map/ppermute | solution.py:61
  12.0 17.3 %collective-permute-start.4 = (bf16[256,256]{1,0:T(8,128)(2,1)S(1)}, bf16[256,256]{1,0:T(8,128)(2,1)S(1)}, u32[]{:S(2)}, u32[]{:S(2)}) collective-permute-start(bf16[256,256]{1,0:T(8,128)(2,1)S(1)} %bitcast.70), channel_id=1, source_target_pairs={{0,3},{1,4},{2,5},{3,6},{4,7},{5,0},{6,1},{7,2},{8,11},{9,12},{10,... | collective-permute-start | bytes 393224 | tf_op jit(solution)/shard_map/ppermute | solution.py:61
  12.8 18.3 %collective-permute-start.5 = (bf16[256,256]{1,0:T(8,128)(2,1)S(1)}, bf16[256,256]{1,0:T(8,128)(2,1)S(1)}, u32[]{:S(2)}, u32[]{:S(2)}) collective-permute-start(bf16[256,256]{1,0:T(8,128)(2,1)S(1)} %bitcast.68), channel_id=1, source_target_pairs={{0,5},{1,6},{2,7},{3,0},{4,1},{5,2},{6,3},{7,4},{8,13},{9,14},{10,... | collective-permute-start | bytes 393224 | tf_op jit(solution)/shard_map/ppermute | solution.py:61
  17.5 13.5 %collective-permute-start.6 = (bf16[256,256]{1,0:T(8,128)(2,1)S(1)}, bf16[256,256]{1,0:T(8,128)(2,1)S(1)}, u32[]{:S(2)}, u32[]{:S(2)}) collective-permute-start(bf16[256,256]{1,0:T(8,128)(2,1)S(1)} %bitcast.66), channel_id=1, source_target_pairs={{0,4},{1,5},{2,6},{3,7},{4,0},{5,1},{6,2},{7,3},{8,12},{9,13},{10,... | collective-permute-start | bytes 393224 | tf_op jit(solution)/shard_map/ppermute | solution.py:61
  31.8 13.4 %collective-permute-start.8 = (bf16[4,2,64,256]{3,2,1,0:T(8,128)(2,1)S(1)}, bf16[4,2,64,256]{3,2,1,0:T(8,128)(2,1)S(1)}, u32[]{:S(2)}, u32[]{:S(2)}) collective-permute-start(bf16[4,2,64,256]{3,2,1,0:T(8,128)(2,1)S(1)} %get-tuple-element.52), channel_id=1, source_target_pairs={{8,16},{16,8},{24,32},{32,24},{40,48},{48,40},{56,64},{64,56},{72,... | collective-permute-start | bytes 786440 | tf_op jit(solution)/shard_map/ppermute | solution.py:42
  33.8 11.5 %collective-permute-start.7 = (bf16[4,2,64,256]{3,2,1,0:T(8,128)(2,1)S(1)}, bf16[4,2,64,256]{3,2,1,0:T(8,128)(2,1)S(1)}, u32[]{:S(2)}, u32[]{:S(2)}) collective-permute-start(bf16[4,2,64,256]{3,2,1,0:T(8,128)(2,1)S(1)} %get-tuple-element.52), channel_id=1, source_target_pairs={{0,8},{8,0},{16,24},{24,16},{32,40},{40,32},{48,56},{56,48},{64,72... | collective-permute-start | bytes 786440 | tf_op jit(solution)/shard_map/ppermute | solution.py:42
  35.5 9.4 %collective-permute-start.10 = (bf16[2,2,64,256]{3,2,1,0:T(8,128)(2,1)S(1)}, bf16[2,2,64,256]{3,2,1,0:T(8,128)(2,1)S(1)}, u32[]{:S(2)}, u32[]{:S(2)}) collective-permute-start(bf16[2,2,64,256]{3,2,1,0:T(8,128)(2,1)S(1)} %get-tuple-element.53), channel_id=1, source_target_pairs={{16,32},{32,16},{24,40},{40,24},{48,64},{64,48},{56,72},{72,56},{8... | collective-permute-start | bytes 393224 | tf_op jit(solution)/shard_map/ppermute | solution.py:42
  40.0 5.2 %collective-permute-start.9 = (bf16[2,2,64,256]{3,2,1,0:T(8,128)(2,1)S(1)}, bf16[2,2,64,256]{3,2,1,0:T(8,128)(2,1)S(1)}, u32[]{:S(2)}, u32[]{:S(2)}) collective-permute-start(bf16[2,2,64,256]{3,2,1,0:T(8,128)(2,1)S(1)} %get-tuple-element.53), channel_id=1, source_target_pairs={{0,16},{16,0},{8,24},{24,8},{32,48},{48,32},{40,56},{56,40},{64,80... | collective-permute-start | bytes 393224 | tf_op jit(solution)/shard_map/ppermute | solution.py:42
  48.3 13.5 %collective-permute-start.11 = (bf16[4,2,64,256]{3,2,1,0:T(8,128)(2,1)S(1)}, bf16[4,2,64,256]{3,2,1,0:T(8,128)(2,1)S(1)}, u32[]{:S(2)}, u32[]{:S(2)}) collective-permute-start(bf16[4,2,64,256]{3,2,1,0:T(8,128)(2,1)S(1)} %get-tuple-element.68), channel_id=1, source_target_pairs={{0,8},{8,0},{16,24},{24,16},{32,40},{40,32},{48,56},{56,48},{64,72... | collective-permute-start | bytes 786440 | tf_op jit(solution)/shard_map/ppermute | solution.py:42
  48.4 13.4 %collective-permute-start.12 = (bf16[4,2,64,256]{3,2,1,0:T(8,128)(2,1)S(1)}, bf16[4,2,64,256]{3,2,1,0:T(8,128)(2,1)S(1)}, u32[]{:S(2)}, u32[]{:S(2)}) collective-permute-start(bf16[4,2,64,256]{3,2,1,0:T(8,128)(2,1)S(1)} %get-tuple-element.69), channel_id=1, source_target_pairs={{8,16},{16,8},{24,32},{32,24},{40,48},{48,40},{56,64},{64,56},{72,... | collective-permute-start | bytes 786440 | tf_op jit(solution)/shard_map/ppermute | solution.py:42
  52.7 6.4 %collective-permute-start.13 = (bf16[2,2,64,256]{3,2,1,0:T(8,128)(2,1)S(1)}, bf16[2,2,64,256]{3,2,1,0:T(8,128)(2,1)S(1)}, u32[]{:S(2)}, u32[]{:S(2)}) collective-permute-start(bf16[2,2,64,256]{3,2,1,0:T(8,128)(2,1)S(1)} %get-tuple-element.70), channel_id=1, source_target_pairs={{0,16},{16,0},{8,24},{24,8},{32,48},{48,32},{40,56},{56,40},{64,80... | collective-permute-start | bytes 393224 | tf_op jit(solution)/shard_map/ppermute | solution.py:42
  52.8 9.0 %collective-permute-start.14 = (bf16[2,2,64,256]{3,2,1,0:T(8,128)(2,1)S(1)}, bf16[2,2,64,256]{3,2,1,0:T(8,128)(2,1)S(1)}, u32[]{:S(2)}, u32[]{:S(2)}) collective-permute-start(bf16[2,2,64,256]{3,2,1,0:T(8,128)(2,1)S(1)} %get-tuple-element.71), channel_id=1, source_target_pairs={{16,32},{32,16},{24,40},{40,24},{48,64},{64,48},{56,72},{72,56},{8... | collective-permute-start | bytes 393224 | tf_op jit(solution)/shard_map/ppermute | solution.py:42
  62.7 10.5 %collective-permute-start.15 = (bf16[256,256]{1,0:T(8,128)(2,1)S(1)}, bf16[256,256]{1,0:T(8,128)(2,1)S(1)}, u32[]{:S(2)}, u32[]{:S(2)}) collective-permute-start(bf16[256,256]{1,0:T(8,128)(2,1)S(1)} %bitcast.76), channel_id=1, source_target_pairs={{0,7},{1,0},{2,1},{3,2},{4,3},{5,4},{6,5},{7,6},{8,15},{9,8},{10,9... | collective-permute-start | bytes 393224 | tf_op jit(solution)/shard_map/ppermute | solution.py:61
  65.0 9.4 %collective-permute-start.16 = (bf16[256,256]{1,0:T(8,128)(2,1)S(1)}, bf16[256,256]{1,0:T(8,128)(2,1)S(1)}, u32[]{:S(2)}, u32[]{:S(2)}) collective-permute-start(bf16[256,256]{1,0:T(8,128)(2,1)S(1)} %bitcast.74), channel_id=1, source_target_pairs={{0,1},{1,2},{2,3},{3,4},{4,5},{5,6},{6,7},{7,0},{8,9},{9,10},{10,1... | collective-permute-start | bytes 393224 | tf_op jit(solution)/shard_map/ppermute | solution.py:61
  67.6 12.3 %collective-permute-start.17 = (bf16[256,256]{1,0:T(8,128)(2,1)S(1)}, bf16[256,256]{1,0:T(8,128)(2,1)S(1)}, u32[]{:S(2)}, u32[]{:S(2)}) collective-permute-start(bf16[256,256]{1,0:T(8,128)(2,1)S(1)} %bitcast.71), channel_id=1, source_target_pairs={{0,6},{1,7},{2,0},{3,1},{4,2},{5,3},{6,4},{7,5},{8,14},{9,15},{10,... | collective-permute-start | bytes 393224 | tf_op jit(solution)/shard_map/ppermute | solution.py:61
  69.1 11.8 %collective-permute-start.18 = (bf16[256,256]{1,0:T(8,128)(2,1)S(1)}, bf16[256,256]{1,0:T(8,128)(2,1)S(1)}, u32[]{:S(2)}, u32[]{:S(2)}) collective-permute-start(bf16[256,256]{1,0:T(8,128)(2,1)S(1)} %bitcast.69), channel_id=1, source_target_pairs={{0,2},{1,3},{2,4},{3,5},{4,6},{5,7},{6,0},{7,1},{8,10},{9,11},{10,... | collective-permute-start | bytes 393224 | tf_op jit(solution)/shard_map/ppermute | solution.py:61
  70.5 15.9 %collective-permute-start.19 = (bf16[256,256]{1,0:T(8,128)(2,1)S(1)}, bf16[256,256]{1,0:T(8,128)(2,1)S(1)}, u32[]{:S(2)}, u32[]{:S(2)}) collective-permute-start(bf16[256,256]{1,0:T(8,128)(2,1)S(1)} %bitcast.67), channel_id=1, source_target_pairs={{0,5},{1,6},{2,7},{3,0},{4,1},{5,2},{6,3},{7,4},{8,13},{9,14},{10,... | collective-permute-start | bytes 393224 | tf_op jit(solution)/shard_map/ppermute | solution.py:61
  73.2 16.6 %collective-permute-start.20 = (bf16[256,256]{1,0:T(8,128)(2,1)S(1)}, bf16[256,256]{1,0:T(8,128)(2,1)S(1)}, u32[]{:S(2)}, u32[]{:S(2)}) collective-permute-start(bf16[256,256]{1,0:T(8,128)(2,1)S(1)} %bitcast.65), channel_id=1, source_target_pairs={{0,3},{1,4},{2,5},{3,6},{4,7},{5,0},{6,1},{7,2},{8,11},{9,12},{10,... | collective-permute-start | bytes 393224 | tf_op jit(solution)/shard_map/ppermute | solution.py:61
  74.3 15.5 %collective-permute-start.21 = (bf16[256,256]{1,0:T(8,128)(2,1)S(1)}, bf16[256,256]{1,0:T(8,128)(2,1)S(1)}, u32[]{:S(2)}, u32[]{:S(2)}) collective-permute-start(bf16[256,256]{1,0:T(8,128)(2,1)S(1)} %bitcast.64), channel_id=1, source_target_pairs={{0,4},{1,5},{2,6},{3,7},{4,0},{5,1},{6,2},{7,3},{8,12},{9,13},{10,... | collective-permute-start | bytes 393224 | tf_op jit(solution)/shard_map/ppermute | solution.py:61

commit v6 on v4

--- a/solution.py
+++ b/solution.py
@@ -55,32 +55,25 @@
 
 
 def head_shifts(pieces, sign):
-    frames, length = lax.axis_size("frame"), lax.axis_size("head")
+    length = lax.axis_size("head")
     arrived = []
     for piece, by in zip(pieces, SHIFTS):
         if by:
-            pairs = []
-            for frame in range(frames):
-                step = -sign * by if frame % 2 else sign * by
-                pairs += [(frame * length + i, frame * length + (i + step) % length) for i in range(length)]
             flat = piece.reshape(-1, piece.shape[-1])
-            piece = lax.ppermute(flat, ("frame", "head"), pairs).reshape(piece.shape)
+            flat = lax.ppermute(flat, "head", [(i, (i + sign * by) % length) for i in range(length)])
+            piece = flat.reshape(piece.shape)
         arrived.append(piece)
     return arrived
 
 
-def moved(step):
+def place_above(slot):
     length = lax.axis_size("head")
-    odd = lax.rem(lax.axis_index("frame"), 2)
-    return lax.rem(lax.axis_index("head") + length + step * (1 - 2 * odd), length)
-
-
-def place_above(slot):
-    return moved(SHIFTS[slot])
+    return lax.rem(lax.axis_index("head") + SHIFTS[slot], length)
 
 
 def place_below(slot):
-    return moved(-SHIFTS[slot])
+    length = lax.axis_size("head")
+    return lax.rem(lax.axis_index("head") + (length - SHIFTS[slot]), length)
 
 
 def columns_of(slot, piece):
@@ -93,23 +86,20 @@
     piece = width // parts
 
     def body(*refs):
-        in_refs, out_refs, sem = refs[:count], refs[count:-1], refs[-1]
-        copies = []
-        for k, out_ref in enumerate(out_refs):
-            for i, ref in enumerate(in_refs):
-                copies.append(
-                    pltpu.make_async_copy(ref.at[:, columns_of(k, piece)], out_ref.at[i], sem.at[k, i])
-                )
+        in_refs, out_refs, (held, sem) = refs[:count], refs[count:-2], refs[-2:]
+        copies = [pltpu.make_async_copy(ref, held.at[i], sem.at[i]) for i, ref in enumerate(in_refs)]
         for copy in copies:
             copy.start()
-        for copy in copies:
+        for i, copy in enumerate(copies):
             copy.wait()
+            for k, out_ref in enumerate(out_refs):
+                out_ref[i] = held[i, :, columns_of(k, piece)]
 
     shape = jax.ShapeDtypeStruct((count, rows, piece), arrays[0].dtype)
     anywhere = pl.BlockSpec(memory_space=pltpu.HBM)
     arrays = [pltpu.with_memory_space_constraint(array, pltpu.HBM) for array in arrays]
-    sems = [pltpu.SemaphoreType.DMA((parts, count))]
-    return call(body, [shape] * parts, [anywhere] * count, [VM] * parts, "pack", 4, sems)(*arrays)
+    scratch = [pltpu.VMEM((count, rows, width), arrays[0].dtype), pltpu.SemaphoreType.DMA((count,))]
+    return call(body, [shape] * parts, [anywhere] * count, [VM] * parts, "pack", 4, scratch)(*arrays)
 
 
 def unpack(pieces):

time: 92.8 us -> 92.5 us (level)
  the two profiles are of different devices: /device:TPU:61 before, /device:TPU:4 now
where the time goes in v6:
time: 92.5 us; the launch traced here: 90.8 us
  starting transfers between devices  49.9 us (54%)
  waiting for transfers between devices  30.9 us (33%)
  Pallas kernels  9.26 us (10%)
    ppermute x14, starting transfers between devices, head_shifts(): lax.ppermute(flat, 'head', [(i, (i + sign * by) % length) for i in range(...  35.2 us
    ppermute x14, waiting for transfers between devices, head_shifts(): lax.ppermute(flat, 'head', [(i, (i + sign * by) % length) for i in range(...  21.3 us
    ppermute x8, starting transfers between devices, swapped(): return lax.ppermute(array, 'frame', pairs)  14.7 us
    ppermute x8, waiting for transfers between devices, swapped(): return lax.ppermute(array, 'frame', pairs)  9.68 us
    pallas_call x1, Pallas kernels, remote_part(): call(body, outs, [VM] * (parts + 6), [VM] * 7, 'remote_part', 24)  1.94 us
  transfers between devices with their start and end apart: 22, of which 10 were waited for; matrix products, arithmetic and copies ran while one was open for 0% of the time, Pallas kernels for 4%

profile of v6, /device:TPU:4, one launch (start us, length us, event | category | flops | bytes accessed | tf_op | source)
XLA Modules:
  0.0 90.8 jit_solution(18185327642436593051)
XLA Ops:
  0.6 1.3 %pack.1 = (bf16[4,64,256]{2,1,0:T(8,128)(2,1)S(1)}, bf16[4,64,256]{2,1,0:T(8,128)(2,1)S(1)}, bf16[4,64,256]{2,1,0:T(8,128)(2,1)S(1)}, bf16[4,64,256]{2,1,0:T(8,1...) custom-call(bf16[64,2048]{1,0:T(8,128)(2,1)} %refs_0_.1, ...), custom_call_target="tpu_custom_call" | custom-call | tf_op jit(solution)/shard_map/pack/pallas_call | solution.py:102
  1.9 2.0 %collective-permute-start = (bf16[256,256]{1,0:T(8,128)(2,1)S(1)}, bf16[256,256]{1,0:T(8,128)(2,1)S(1)}, u32[]{:S(2)}, u32[]{:S(2)}) collective-permute-start(bf16[256,256]{1,0:T(8,128)(2,1)S(1)} %bitcast.84), channel_id=1, source_target_pairs={{0,1},{1,2},{2,3},{3,4},{4,5},{5,6},{6,7},{7,0},{8,9},{9,10},{10,1... | collective-permute-start | bytes 393224 | tf_op jit(solution)/shard_map/ppermute | solution.py:63
  3.9 4.0 %collective-permute-start.1 = (bf16[256,256]{1,0:T(8,128)(2,1)S(1)}, bf16[256,256]{1,0:T(8,128)(2,1)S(1)}, u32[]{:S(2)}, u32[]{:S(2)}) collective-permute-start(bf16[256,256]{1,0:T(8,128)(2,1)S(1)} %bitcast.82), channel_id=1, source_target_pairs={{0,7},{1,0},{2,1},{3,2},{4,3},{5,4},{6,5},{7,6},{8,15},{9,8},{10,9... | collective-permute-start | bytes 393224 | tf_op jit(solution)/shard_map/ppermute | solution.py:63
  7.9 4.1 %collective-permute-start.3 = (bf16[256,256]{1,0:T(8,128)(2,1)S(1)}, bf16[256,256]{1,0:T(8,128)(2,1)S(1)}, u32[]{:S(2)}, u32[]{:S(2)}) collective-permute-start(bf16[256,256]{1,0:T(8,128)(2,1)S(1)} %bitcast.79), channel_id=1, source_target_pairs={{0,6},{1,7},{2,0},{3,1},{4,2},{5,3},{6,4},{7,5},{8,14},{9,15},{10,... | collective-permute-start | bytes 393224 | tf_op jit(solution)/shard_map/ppermute | solution.py:63
  12.1 0.6 collective-permute-start.4
  12.7 0.0 collective-permute-done
  12.7 4.4 %collective-permute-start.5 = (bf16[256,256]{1,0:T(8,128)(2,1)S(1)}, bf16[256,256]{1,0:T(8,128)(2,1)S(1)}, u32[]{:S(2)}, u32[]{:S(2)}) collective-permute-start(bf16[256,256]{1,0:T(8,128)(2,1)S(1)} %bitcast.75), channel_id=1, source_target_pairs={{0,5},{1,6},{2,7},{3,0},{4,1},{5,2},{6,3},{7,4},{8,13},{9,14},{10,... | collective-permute-start | bytes 393224 | tf_op jit(solution)/shard_map/ppermute | solution.py:63
  17.1 0.0 collective-permute-done.1
  17.1 4.5 %collective-permute-start.6 = (bf16[256,256]{1,0:T(8,128)(2,1)S(1)}, bf16[256,256]{1,0:T(8,128)(2,1)S(1)}, u32[]{:S(2)}, u32[]{:S(2)}) collective-permute-start(bf16[256,256]{1,0:T(8,128)(2,1)S(1)} %bitcast.73), channel_id=1, source_target_pairs={{0,4},{1,5},{2,6},{3,7},{4,0},{5,1},{6,2},{7,3},{8,12},{9,13},{10,... | collective-permute-start | bytes 393224 | tf_op jit(solution)/shard_map/ppermute | solution.py:63
  21.6 0.0 collective-permute-done.2
  21.6 0.0 collective-permute-done.3
  21.6 8.2 %collective-permute-done.4 = bf16[256,256]{1,0:T(8,128)(2,1)S(1)} collective-permute-done((bf16[256,256]{1,0:T(8,128)(2,1)S(1)}, bf16[256,256]{1,0:T(8,128)(2,1)S(1)}, u32[]{:S(2)}, u32[]{:S(2)}) %collective-permute-start.4) | collective-permute-done | bytes 131104 | tf_op jit(solution)/shard_map/ppermute | solution.py:63
  29.8 0.0 collective-permute-done.5
  29.8 0.8 pick_blocks.1
  30.6 0.1 collective-permute-start.7
  30.7 5.0 %collective-permute-start.8 = (bf16[4,2,64,256]{3,2,1,0:T(8,128)(2,1)S(1)}, bf16[4,2,64,256]{3,2,1,0:T(8,128)(2,1)S(1)}, u32[]{:S(2)}, u32[]{:S(2)}) collective-permute-start(bf16[4,2,64,256]{3,2,1,0:T(8,128)(2,1)S(1)} %get-tuple-element.49), channel_id=1, source_target_pairs={{8,16},{16,8},{24,32},{32,24},{40,48},{48,40},{56,64},{64,56},{72,... | collective-permute-start | bytes 786440 | tf_op jit(solution)/shard_map/ppermute | solution.py:44
  35.7 0.1 collective-permute-start.9
  35.8 3.1 %collective-permute-start.10 = (bf16[2,2,64,256]{3,2,1,0:T(8,128)(2,1)S(1)}, bf16[2,2,64,256]{3,2,1,0:T(8,128)(2,1)S(1)}, u32[]{:S(2)}, u32[]{:S(2)}) collective-permute-start(bf16[2,2,64,256]{3,2,1,0:T(8,128)(2,1)S(1)} %get-tuple-element.50), channel_id=1, source_target_pairs={{16,32},{32,16},{24,40},{40,24},{48,64},{64,48},{56,72},{72,56},{8... | collective-permute-start | bytes 393224 | tf_op jit(solution)/shard_map/ppermute | solution.py:44
  38.9 0.9 own_scores.1
  39.7 0.0 collective-permute-done.7.refs_8_
  39.7 0.7 collective-permute-done.8.refs_9_
  40.5 0.9 near_scores.1
  41.4 0.5 collective-permute-done.9.refs_8_.refs_10_
  41.8 3.2 %collective-permute-done.10.refs_9_.refs_11_ = bf16[2,2,64,256]{3,2,1,0:T(8,128)(2,1)S(1)} collective-permute-done((bf16[2,2,64,256]{3,2,1,0:T(8,128)(2,1)S(1)}, bf16[2,2,64,256]{3,2,1,0:T(8,128)(2,1)S(1)}, u32[]{:S(2)}, u32[]{:S(2)}) %collective-permute-start.10) | collective-permute-done | bytes 131104 | tf_op jit(solution)/shard_map/ppermute | solution.py:44
  45.1 1.9 %remote_part.1 = (f32[2,8,512]{2,1,0:T(8,128)S(1)}, bf16[4,2,64,256]{3,2,1,0:T(8,128)(2,1)S(1)}, bf16[4,2,64,256]{3,2,1,0:T(8,128)(2,1)S(1)}, bf16[2,2,64,256]{3...) custom-call(bf16[4,64,256]{2,1,0:T(8,128)(2,1)S(1)} %get-tuple-eleme, ...), custom_call_target="tpu_custom_call" | custom-call | tf_op jit(solution)/shard_map/remote_part/pallas_call | solution.py:276
  47.0 0.1 collective-permute-start.11
  47.1 3.9 %collective-permute-start.12 = (bf16[4,2,64,256]{3,2,1,0:T(8,128)(2,1)S(1)}, bf16[4,2,64,256]{3,2,1,0:T(8,128)(2,1)S(1)}, u32[]{:S(2)}, u32[]{:S(2)}) collective-permute-start(bf16[4,2,64,256]{3,2,1,0:T(8,128)(2,1)S(1)} %get-tuple-element.63), channel_id=1, source_target_pairs={{8,16},{16,8},{24,32},{32,24},{40,48},{48,40},{56,64},{64,56},{72,... | collective-permute-start | bytes 786440 | tf_op jit(solution)/shard_map/ppermute | solution.py:44
  51.0 0.2 collective-permute-start.13
  51.2 2.2 %collective-permute-start.14 = (bf16[2,2,64,256]{3,2,1,0:T(8,128)(2,1)S(1)}, bf16[2,2,64,256]{3,2,1,0:T(8,128)(2,1)S(1)}, u32[]{:S(2)}, u32[]{:S(2)}) collective-permute-start(bf16[2,2,64,256]{3,2,1,0:T(8,128)(2,1)S(1)} %get-tuple-element.65), channel_id=1, source_target_pairs={{16,32},{32,16},{24,40},{40,24},{48,64},{64,48},{56,72},{72,56},{8... | collective-permute-start | bytes 393224 | tf_op jit(solution)/shard_map/ppermute | solution.py:44
  53.5 1.5 %own_grads.1 = (bf16[8,2,64,256]{3,2,1,0:T(8,128)(2,1)S(1)}, f32[8,2,64,256]{3,2,1,0:T(8,128)S(1)}) custom-call(bf16[4,64,256]{2,1,0:T(8,128)(2,1)S(1)} %get-tuple-element.41.refs_0_, bf16[4,64,256]{2,1,0:T(8,128)(2,1)S(1)} %bitcast.33, bf16[4,64,256]{2,1,0:T(8,128)(2,1)S(1)} %bitcast.38, bf16[4,64,256]{2,1,0:T(8,128)(2,1)S(1)} %bitcast.43, ...), custom_call_target="tpu_custom_call" | custom-call | tf_op jit(solution)/shard_map/own_grads/pallas_call | solution.py:317
  55.0 2.8 %collective-permute-done.13.a2_ref = bf16[2,2,64,256]{3,2,1,0:T(8,128)(2,1)S(1)} collective-permute-done((bf16[2,2,64,256]{3,2,1,0:T(8,128)(2,1)S(1)}, bf16[2,2,64,256]{3,2,1,0:T(8,128)(2,1)S(1)}, u32[]{:S(2)}, u32[]{:S(2)}) %collective-permute-start.13) | collective-permute-done | bytes 131104 | tf_op jit(solution)/shard_map/ppermute | solution.py:44
  57.8 2.4 %collective-permute-done.14.b2_ref = bf16[2,2,64,256]{3,2,1,0:T(8,128)(2,1)S(1)} collective-permute-done((bf16[2,2,64,256]{3,2,1,0:T(8,128)(2,1)S(1)}, bf16[2,2,64,256]{3,2,1,0:T(8,128)(2,1)S(1)}, u32[]{:S(2)}, u32[]{:S(2)}) %collective-permute-start.14) | collective-permute-done | bytes 131104 | tf_op jit(solution)/shard_map/ppermute | solution.py:44
  60.2 0.0 collective-permute-done.11.a1_ref
  60.2 0.0 collective-permute-done.12.b1_ref
  60.2 1.0 %add_returned.1 = (bf16[4,64,256]{2,1,0:T(8,128)(2,1)S(1)}, bf16[4,64,256]{2,1,0:T(8,128)(2,1)S(1)}, bf16[4,64,256]{2,1,0:T(8,128)(2,1)S(1)}, bf16[4,64,256]{2,1...) custom-call(s32[4,32]{1,0:T(4,128)} %bitcast.86, ...), custom_call_target="tpu_custom_call" | custom-call | tf_op jit(solution)/shard_map/add_returned/pallas_call | solution.py:345
  61.2 2.7 %collective-permute-start.15 = (bf16[256,256]{1,0:T(8,128)(2,1)S(1)}, bf16[256,256]{1,0:T(8,128)(2,1)S(1)}, u32[]{:S(2)}, u32[]{:S(2)}) collective-permute-start(bf16[256,256]{1,0:T(8,128)(2,1)S(1)} %bitcast.83), channel_id=1, source_target_pairs={{0,7},{1,0},{2,1},{3,2},{4,3},{5,4},{6,5},{7,6},{8,15},{9,8},{10,9... | collective-permute-start | bytes 393224 | tf_op jit(solution)/shard_map/ppermute | solution.py:63
  63.9 3.4 %collective-permute-start.16 = (bf16[256,256]{1,0:T(8,128)(2,1)S(1)}, bf16[256,256]{1,0:T(8,128)(2,1)S(1)}, u32[]{:S(2)}, u32[]{:S(2)}) collective-permute-start(bf16[256,256]{1,0:T(8,128)(2,1)S(1)} %bitcast.81), channel_id=1, source_target_pairs={{0,1},{1,2},{2,3},{3,4},{4,5},{5,6},{6,7},{7,0},{8,9},{9,10},{10,1... | collective-permute-start | bytes 393224 | tf_op jit(solution)/shard_map/ppermute | solution.py:63
  67.2 2.0 %collective-permute-start.17 = (bf16[256,256]{1,0:T(8,128)(2,1)S(1)}, bf16[256,256]{1,0:T(8,128)(2,1)S(1)}, u32[]{:S(2)}, u32[]{:S(2)}) collective-permute-start(bf16[256,256]{1,0:T(8,128)(2,1)S(1)} %bitcast.78), channel_id=1, source_target_pairs={{0,6},{1,7},{2,0},{3,1},{4,2},{5,3},{6,4},{7,5},{8,14},{9,15},{10,... | collective-permute-start | bytes 393224 | tf_op jit(solution)/shard_map/ppermute | solution.py:63
  69.2 0.9 %collective-permute-start.18 = (bf16[256,256]{1,0:T(8,128)(2,1)S(1)}, bf16[256,256]{1,0:T(8,128)(2,1)S(1)}, u32[]{:S(2)}, u32[]{:S(2)}) collective-permute-start(bf16[256,256]{1,0:T(8,128)(2,1)S(1)} %bitcast.76), channel_id=1, source_target_pairs={{0,2},{1,3},{2,4},{3,5},{4,6},{5,7},{6,0},{7,1},{8,10},{9,11},{10,... | collective-permute-start | bytes 393224 | tf_op jit(solution)/shard_map/ppermute | solution.py:63
  70.2 3.0 %collective-permute-start.19 = (bf16[256,256]{1,0:T(8,128)(2,1)S(1)}, bf16[256,256]{1,0:T(8,128)(2,1)S(1)}, u32[]{:S(2)}, u32[]{:S(2)}) collective-permute-start(bf16[256,256]{1,0:T(8,128)(2,1)S(1)} %bitcast.74), channel_id=1, source_target_pairs={{0,5},{1,6},{2,7},{3,0},{4,1},{5,2},{6,3},{7,4},{8,13},{9,14},{10,... | collective-permute-start | bytes 393224 | tf_op jit(solution)/shard_map/ppermute | solution.py:63
  73.2 0.8 collective-permute-start.20
  74.0 0.0 collective-permute-done.16
  74.0 2.7 %collective-permute-start.21 = (bf16[256,256]{1,0:T(8,128)(2,1)S(1)}, bf16[256,256]{1,0:T(8,128)(2,1)S(1)}, u32[]{:S(2)}, u32[]{:S(2)}) collective-permute-start(bf16[256,256]{1,0:T(8,128)(2,1)S(1)} %bitcast.71), channel_id=1, source_target_pairs={{0,4},{1,5},{2,6},{3,7},{4,0},{5,1},{6,2},{7,3},{8,12},{9,13},{10,... | collective-permute-start | bytes 393224 | tf_op jit(solution)/shard_map/ppermute | solution.py:63
  76.7 3.2 %collective-permute-done.17 = bf16[256,256]{1,0:T(8,128)(2,1)S(1)} collective-permute-done((bf16[256,256]{1,0:T(8,128)(2,1)S(1)}, bf16[256,256]{1,0:T(8,128)(2,1)S(1)}, u32[]{:S(2)}, u32[]{:S(2)}) %collective-permute-start.17) | collective-permute-done | bytes 131104 | tf_op jit(solution)/shard_map/ppermute | solution.py:63
  79.9 1.7 %collective-permute-done.18 = bf16[256,256]{1,0:T(8,128)(2,1)S(1)} collective-permute-done((bf16[256,256]{1,0:T(8,128)(2,1)S(1)}, bf16[256,256]{1,0:T(8,128)(2,1)S(1)}, u32[]{:S(2)}, u32[]{:S(2)}) %collective-permute-start.18) | collective-permute-done | bytes 131104 | tf_op jit(solution)/shard_map/ppermute | solution.py:63
  81.6 4.2 %collective-permute-done.19 = bf16[256,256]{1,0:T(8,128)(2,1)S(1)} collective-permute-done((bf16[256,256]{1,0:T(8,128)(2,1)S(1)}, bf16[256,256]{1,0:T(8,128)(2,1)S(1)}, u32[]{:S(2)}, u32[]{:S(2)}) %collective-permute-start.19) | collective-permute-done | bytes 131104 | tf_op jit(solution)/shard_map/ppermute | solution.py:63
  85.8 3.9 %collective-permute-done.20 = bf16[256,256]{1,0:T(8,128)(2,1)S(1)} collective-permute-done((bf16[256,256]{1,0:T(8,128)(2,1)S(1)}, bf16[256,256]{1,0:T(8,128)(2,1)S(1)}, u32[]{:S(2)}, u32[]{:S(2)}) %collective-permute-start.20) | collective-permute-done | bytes 131104 | tf_op jit(solution)/shard_map/ppermute | solution.py:63
  89.7 1.1 %unpack.1 = (bf16[64,2048]{1,0:T(8,128)(2,1)}, bf16[64,2048]{1,0:T(8,128)(2,1)}, bf16[64,2048]{1,0:T(8,128)(2,1)}, bf16[64,2048]{1,0:T(8,128)(2,1)}) custom-call(bf16[4,64,256]{2,1,0:T(8,128)(2,1)S(1)} %get-tuple-element.66.refs_0_, bf16[4,64,256]{2,1,0:T(8,128)(2,1)S(1)} %bitcast.64, bf16[4,64,256]{2,1,0:T(8,128)(2,1)S(1)} %bitcast.65, ...), custom_call_target="tpu_custom_call" | custom-call | tf_op jit(solution)/shard_map/unpack/pallas_call | solution.py:115
  (4 shorter events, 0.0 us)
Async XLA Ops:
  1.9 10.8 %collective-permute-start = (bf16[256,256]{1,0:T(8,128)(2,1)S(1)}, bf16[256,256]{1,0:T(8,128)(2,1)S(1)}, u32[]{:S(2)}, u32[]{:S(2)}) collective-permute-start(bf16[256,256]{1,0:T(8,128)(2,1)S(1)} %bitcast.84), channel_id=1, source_target_pairs={{0,1},{1,2},{2,3},{3,4},{4,5},{5,6},{6,7},{7,0},{8,9},{9,10},{10,1... | collective-permute-start | bytes 393224 | tf_op jit(solution)/shard_map/ppermute | solution.py:63
  3.9 13.2 %collective-permute-start.1 = (bf16[256,256]{1,0:T(8,128)(2,1)S(1)}, bf16[256,256]{1,0:T(8,128)(2,1)S(1)}, u32[]{:S(2)}, u32[]{:S(2)}) collective-permute-start(bf16[256,256]{1,0:T(8,128)(2,1)S(1)} %bitcast.82), channel_id=1, source_target_pairs={{0,7},{1,0},{2,1},{3,2},{4,3},{5,4},{6,5},{7,6},{8,15},{9,8},{10,9... | collective-permute-start | bytes 393224 | tf_op jit(solution)/shard_map/ppermute | solution.py:63
  7.9 13.7 %collective-permute-start.2 = (bf16[256,256]{1,0:T(8,128)(2,1)S(1)}, bf16[256,256]{1,0:T(8,128)(2,1)S(1)}, u32[]{:S(2)}, u32[]{:S(2)}) collective-permute-start(bf16[256,256]{1,0:T(8,128)(2,1)S(1)} %bitcast.80), channel_id=1, source_target_pairs={{0,2},{1,3},{2,4},{3,5},{4,6},{5,7},{6,0},{7,1},{8,10},{9,11},{10,... | collective-permute-start | bytes 393224 | tf_op jit(solution)/shard_map/ppermute | solution.py:63
  7.9 13.7 %collective-permute-start.3 = (bf16[256,256]{1,0:T(8,128)(2,1)S(1)}, bf16[256,256]{1,0:T(8,128)(2,1)S(1)}, u32[]{:S(2)}, u32[]{:S(2)}) collective-permute-start(bf16[256,256]{1,0:T(8,128)(2,1)S(1)} %bitcast.79), channel_id=1, source_target_pairs={{0,6},{1,7},{2,0},{3,1},{4,2},{5,3},{6,4},{7,5},{8,14},{9,15},{10,... | collective-permute-start | bytes 393224 | tf_op jit(solution)/shard_map/ppermute | solution.py:63
  12.1 17.8 %collective-permute-start.4 = (bf16[256,256]{1,0:T(8,128)(2,1)S(1)}, bf16[256,256]{1,0:T(8,128)(2,1)S(1)}, u32[]{:S(2)}, u32[]{:S(2)}) collective-permute-start(bf16[256,256]{1,0:T(8,128)(2,1)S(1)} %bitcast.77), channel_id=1, source_target_pairs={{0,3},{1,4},{2,5},{3,6},{4,7},{5,0},{6,1},{7,2},{8,11},{9,12},{10,... | collective-permute-start | bytes 393224 | tf_op jit(solution)/shard_map/ppermute | solution.py:63
  12.7 17.1 %collective-permute-start.5 = (bf16[256,256]{1,0:T(8,128)(2,1)S(1)}, bf16[256,256]{1,0:T(8,128)(2,1)S(1)}, u32[]{:S(2)}, u32[]{:S(2)}) collective-permute-start(bf16[256,256]{1,0:T(8,128)(2,1)S(1)} %bitcast.75), channel_id=1, source_target_pairs={{0,5},{1,6},{2,7},{3,0},{4,1},{5,2},{6,3},{7,4},{8,13},{9,14},{10,... | collective-permute-start | bytes 393224 | tf_op jit(solution)/shard_map/ppermute | solution.py:63
  17.1 12.7 %collective-permute-start.6 = (bf16[256,256]{1,0:T(8,128)(2,1)S(1)}, bf16[256,256]{1,0:T(8,128)(2,1)S(1)}, u32[]{:S(2)}, u32[]{:S(2)}) collective-permute-start(bf16[256,256]{1,0:T(8,128)(2,1)S(1)} %bitcast.73), channel_id=1, source_target_pairs={{0,4},{1,5},{2,6},{3,7},{4,0},{5,1},{6,2},{7,3},{8,12},{9,13},{10,... | collective-permute-start | bytes 393224 | tf_op jit(solution)/shard_map/ppermute | solution.py:63
  30.6 9.1 %collective-permute-start.7 = (bf16[4,2,64,256]{3,2,1,0:T(8,128)(2,1)S(1)}, bf16[4,2,64,256]{3,2,1,0:T(8,128)(2,1)S(1)}, u32[]{:S(2)}, u32[]{:S(2)}) collective-permute-start(bf16[4,2,64,256]{3,2,1,0:T(8,128)(2,1)S(1)} %get-tuple-element.49), channel_id=1, source_target_pairs={{0,8},{8,0},{16,24},{24,16},{32,40},{40,32},{48,56},{56,48},{64,72... | collective-permute-start | bytes 786440 | tf_op jit(solution)/shard_map/ppermute | solution.py:44
  30.7 9.8 %collective-permute-start.8 = (bf16[4,2,64,256]{3,2,1,0:T(8,128)(2,1)S(1)}, bf16[4,2,64,256]{3,2,1,0:T(8,128)(2,1)S(1)}, u32[]{:S(2)}, u32[]{:S(2)}) collective-permute-start(bf16[4,2,64,256]{3,2,1,0:T(8,128)(2,1)S(1)} %get-tuple-element.49), channel_id=1, source_target_pairs={{8,16},{16,8},{24,32},{32,24},{40,48},{48,40},{56,64},{64,56},{72,... | collective-permute-start | bytes 786440 | tf_op jit(solution)/shard_map/ppermute | solution.py:44
  35.7 6.2 %collective-permute-start.9 = (bf16[2,2,64,256]{3,2,1,0:T(8,128)(2,1)S(1)}, bf16[2,2,64,256]{3,2,1,0:T(8,128)(2,1)S(1)}, u32[]{:S(2)}, u32[]{:S(2)}) collective-permute-start(bf16[2,2,64,256]{3,2,1,0:T(8,128)(2,1)S(1)} %get-tuple-element.50), channel_id=1, source_target_pairs={{0,16},{16,0},{8,24},{24,8},{32,48},{48,32},{40,56},{56,40},{64,80... | collective-permute-start | bytes 393224 | tf_op jit(solution)/shard_map/ppermute | solution.py:44
  35.8 9.3 %collective-permute-start.10 = (bf16[2,2,64,256]{3,2,1,0:T(8,128)(2,1)S(1)}, bf16[2,2,64,256]{3,2,1,0:T(8,128)(2,1)S(1)}, u32[]{:S(2)}, u32[]{:S(2)}) collective-permute-start(bf16[2,2,64,256]{3,2,1,0:T(8,128)(2,1)S(1)} %get-tuple-element.50), channel_id=1, source_target_pairs={{16,32},{32,16},{24,40},{40,24},{48,64},{64,48},{56,72},{72,56},{8... | collective-permute-start | bytes 393224 | tf_op jit(solution)/shard_map/ppermute | solution.py:44
  47.0 13.2 %collective-permute-start.11 = (bf16[4,2,64,256]{3,2,1,0:T(8,128)(2,1)S(1)}, bf16[4,2,64,256]{3,2,1,0:T(8,128)(2,1)S(1)}, u32[]{:S(2)}, u32[]{:S(2)}) collective-permute-start(bf16[4,2,64,256]{3,2,1,0:T(8,128)(2,1)S(1)} %get-tuple-element.62), channel_id=1, source_target_pairs={{0,8},{8,0},{16,24},{24,16},{32,40},{40,32},{48,56},{56,48},{64,72... | collective-permute-start | bytes 786440 | tf_op jit(solution)/shard_map/ppermute | solution.py:44
  47.1 13.1 %collective-permute-start.12 = (bf16[4,2,64,256]{3,2,1,0:T(8,128)(2,1)S(1)}, bf16[4,2,64,256]{3,2,1,0:T(8,128)(2,1)S(1)}, u32[]{:S(2)}, u32[]{:S(2)}) collective-permute-start(bf16[4,2,64,256]{3,2,1,0:T(8,128)(2,1)S(1)} %get-tuple-element.63), channel_id=1, source_target_pairs={{8,16},{16,8},{24,32},{32,24},{40,48},{48,40},{56,64},{64,56},{72,... | collective-permute-start | bytes 786440 | tf_op jit(solution)/shard_map/ppermute | solution.py:44
  51.0 6.8 %collective-permute-start.13 = (bf16[2,2,64,256]{3,2,1,0:T(8,128)(2,1)S(1)}, bf16[2,2,64,256]{3,2,1,0:T(8,128)(2,1)S(1)}, u32[]{:S(2)}, u32[]{:S(2)}) collective-permute-start(bf16[2,2,64,256]{3,2,1,0:T(8,128)(2,1)S(1)} %get-tuple-element.64), channel_id=1, source_target_pairs={{0,16},{16,0},{8,24},{24,8},{32,48},{48,32},{40,56},{56,40},{64,80... | collective-permute-start | bytes 393224 | tf_op jit(solution)/shard_map/ppermute | solution.py:44
  51.2 9.0 %collective-permute-start.14 = (bf16[2,2,64,256]{3,2,1,0:T(8,128)(2,1)S(1)}, bf16[2,2,64,256]{3,2,1,0:T(8,128)(2,1)S(1)}, u32[]{:S(2)}, u32[]{:S(2)}) collective-permute-start(bf16[2,2,64,256]{3,2,1,0:T(8,128)(2,1)S(1)} %get-tuple-element.65), channel_id=1, source_target_pairs={{16,32},{32,16},{24,40},{40,24},{48,64},{64,48},{56,72},{72,56},{8... | collective-permute-start | bytes 393224 | tf_op jit(solution)/shard_map/ppermute | solution.py:44
  61.2 12.0 %collective-permute-start.15 = (bf16[256,256]{1,0:T(8,128)(2,1)S(1)}, bf16[256,256]{1,0:T(8,128)(2,1)S(1)}, u32[]{:S(2)}, u32[]{:S(2)}) collective-permute-start(bf16[256,256]{1,0:T(8,128)(2,1)S(1)} %bitcast.83), channel_id=1, source_target_pairs={{0,7},{1,0},{2,1},{3,2},{4,3},{5,4},{6,5},{7,6},{8,15},{9,8},{10,9... | collective-permute-start | bytes 393224 | tf_op jit(solution)/shard_map/ppermute | solution.py:63
  63.9 10.1 %collective-permute-start.16 = (bf16[256,256]{1,0:T(8,128)(2,1)S(1)}, bf16[256,256]{1,0:T(8,128)(2,1)S(1)}, u32[]{:S(2)}, u32[]{:S(2)}) collective-permute-start(bf16[256,256]{1,0:T(8,128)(2,1)S(1)} %bitcast.81), channel_id=1, source_target_pairs={{0,1},{1,2},{2,3},{3,4},{4,5},{5,6},{6,7},{7,0},{8,9},{9,10},{10,1... | collective-permute-start | bytes 393224 | tf_op jit(solution)/shard_map/ppermute | solution.py:63
  67.2 12.7 %collective-permute-start.17 = (bf16[256,256]{1,0:T(8,128)(2,1)S(1)}, bf16[256,256]{1,0:T(8,128)(2,1)S(1)}, u32[]{:S(2)}, u32[]{:S(2)}) collective-permute-start(bf16[256,256]{1,0:T(8,128)(2,1)S(1)} %bitcast.78), channel_id=1, source_target_pairs={{0,6},{1,7},{2,0},{3,1},{4,2},{5,3},{6,4},{7,5},{8,14},{9,15},{10,... | collective-permute-start | bytes 393224 | tf_op jit(solution)/shard_map/ppermute | solution.py:63
  69.2 12.4 %collective-permute-start.18 = (bf16[256,256]{1,0:T(8,128)(2,1)S(1)}, bf16[256,256]{1,0:T(8,128)(2,1)S(1)}, u32[]{:S(2)}, u32[]{:S(2)}) collective-permute-start(bf16[256,256]{1,0:T(8,128)(2,1)S(1)} %bitcast.76), channel_id=1, source_target_pairs={{0,2},{1,3},{2,4},{3,5},{4,6},{5,7},{6,0},{7,1},{8,10},{9,11},{10,... | collective-permute-start | bytes 393224 | tf_op jit(solution)/shard_map/ppermute | solution.py:63
  70.2 15.6 %collective-permute-start.19 = (bf16[256,256]{1,0:T(8,128)(2,1)S(1)}, bf16[256,256]{1,0:T(8,128)(2,1)S(1)}, u32[]{:S(2)}, u32[]{:S(2)}) collective-permute-start(bf16[256,256]{1,0:T(8,128)(2,1)S(1)} %bitcast.74), channel_id=1, source_target_pairs={{0,5},{1,6},{2,7},{3,0},{4,1},{5,2},{6,3},{7,4},{8,13},{9,14},{10,... | collective-permute-start | bytes 393224 | tf_op jit(solution)/shard_map/ppermute | solution.py:63
  73.2 16.5 %collective-permute-start.20 = (bf16[256,256]{1,0:T(8,128)(2,1)S(1)}, bf16[256,256]{1,0:T(8,128)(2,1)S(1)}, u32[]{:S(2)}, u32[]{:S(2)}) collective-permute-start(bf16[256,256]{1,0:T(8,128)(2,1)S(1)} %bitcast.72), channel_id=1, source_target_pairs={{0,3},{1,4},{2,5},{3,6},{4,7},{5,0},{6,1},{7,2},{8,11},{9,12},{10,... | collective-permute-start | bytes 393224 | tf_op jit(solution)/shard_map/ppermute | solution.py:63
  74.0 15.7 %collective-permute-start.21 = (bf16[256,256]{1,0:T(8,128)(2,1)S(1)}, bf16[256,256]{1,0:T(8,128)(2,1)S(1)}, u32[]{:S(2)}, u32[]{:S(2)}) collective-permute-start(bf16[256,256]{1,0:T(8,128)(2,1)S(1)} %bitcast.71), channel_id=1, source_target_pairs={{0,4},{1,5},{2,6},{3,7},{4,0},{5,1},{6,2},{7,3},{8,12},{9,13},{10,... | collective-permute-start | bytes 393224 | tf_op jit(solution)/shard_map/ppermute | solution.py:63
